TPU v7x, 32 devices: a whole 2x2x4 slice. The times are simulated.
32 devices in a mesh: seq: 4 (over y, x), blk: 8 (over z, core).
Axes of the slice: x: 2, y: 2, z: 4, core: 2. Of those that a mesh axis runs over, the one named last changes fastest.
Arguments:
- hidden_in: bfloat16 [16384, 768], P(('seq', 'blk')), may hold values from -6 to 6
- query_weight: float32 [768, 768], P(('seq', 'blk')), may hold values from -0.3125 to 0.3125
- key_weight: float32 [768, 768], P(('seq', 'blk')), may hold values from -0.21875 to 0.21875
- value_weight: float32 [768, 768], P(('seq', 'blk')), may hold values from -0.21875 to 0.21875
- output_weight: float32 [768, 768], P(('seq', 'blk')), may hold values from -0.875 to 0.875
- inner_weight: float32 [768, 3072], P(('seq', 'blk')), may hold values from -0.21875 to 0.21875
- outer_weight: float32 [3072, 768], P(('seq', 'blk')), may hold values from -0.109375 to 0.109375
- query_bias: float32 [768], P(('seq', 'blk')), may hold values from -2 to 2
- value_bias: float32 [768], P(('seq', 'blk')), may hold values from -2 to 2
- output_bias: float32 [768], P(('seq', 'blk')), may hold values from -2 to 2
- attention_gain: float32 [768], P(('seq', 'blk')), may hold values from 0.5 to 1.5
- attention_shift: float32 [768], P(('seq', 'blk')), may hold values from -2 to 2
- inner_bias: float32 [3072], P(('seq', 'blk')), may hold values from -2 to 2
- outer_bias: float32 [768], P(('seq', 'blk')), may hold values from -2 to 2
- final_gain: float32 [768], P(('seq', 'blk')), may hold values from 0.5 to 1.5
- final_shift: float32 [768], P(('seq', 'blk')), may hold values from -2 to 2
- cotangent: bfloat16 [16384, 768], P(('seq', 'blk')), may hold values from -12 to 12
- grad_mask: int32 [16384, 768], P(('seq', 'blk')), may hold values 0 or 1
- cluster_order: int32 [4, 12, 4096], P('seq'), may hold values from 0 to 4095, each once within a row
Outputs:
- hidden_out: bfloat16 [16384, 768], P(('seq', 'blk'))
- input_grad: float32 [16384, 768], P(('seq', 'blk'))
- grad_query_weight: float32 [768, 768], P(('seq', 'blk'))
- grad_key_weight: float32 [768, 768], P(('seq', 'blk'))
- grad_value_weight: float32 [768, 768], P(('seq', 'blk'))
- grad_output_weight: float32 [768, 768], P(('seq', 'blk'))
- grad_inner_weight: float32 [768, 3072], P(('seq', 'blk'))
- grad_outer_weight: float32 [3072, 768], P(('seq', 'blk'))
- grad_query_bias: float32 [768], P(('seq', 'blk'))
- grad_value_bias: float32 [768], P(('seq', 'blk'))
- grad_output_bias: float32 [768], P(('seq', 'blk'))
- grad_attention_gain: float32 [768], P(('seq', 'blk'))
- grad_attention_shift: float32 [768], P(('seq', 'blk'))
- grad_inner_bias: float32 [3072], P(('seq', 'blk'))
- grad_outer_bias: float32 [768], P(('seq', 'blk'))
- grad_final_gain: float32 [768], P(('seq', 'blk'))
- grad_final_shift: float32 [768], P(('seq', 'blk'))
Inputs may be any that keep to these rules, and one draw needn't show every extreme that they name: cluster_order[s, h] lists each position of sequence s once; the clusters of head h are its consecutive runs of 128 entries.
All inputs are finite; a program needn't handle non-finite values. No bound on the sum of `grad_mask` on one device may be relied on, other than what follows from the above.
Results may differ from a plain program's by a relative error of at most 0.015.
The roundings to bfloat16 on the way count: a program that leaves them out, or rounds other values in their place, can miss the bound.
Values may be sent and summed in bfloat16 or wider, within the bound.
A program may use at most 320 MiB of HBM per device.

v0:
```python
import math

import jax
import jax.numpy as jnp
from jax import lax
from jax.sharding import PartitionSpec as P

CLUSTER = 128


epsilon = 1e-06


def layer_norm(value, gain, shift):
    center = value - jnp.mean(value, axis=-1, keepdims=True)
    spread = jnp.mean(center * center, axis=-1, keepdims=True)
    return center * lax.rsqrt(spread + epsilon) * gain + shift


def exact_gelu(value):
    return jax.nn.gelu(value, approximate=False)


def row_contract(left, right):
    return lax.dot_general(
        left, right, (((0,), (0,)), ((), ())), preferred_element_type=jnp.float32
    )


def back_product(grad, weight):
    return lax.dot_general(
        grad, weight, (((1,), (1,)), ((), ())), preferred_element_type=jnp.float32
    )


def column_sum(value):
    return jnp.sum(value.astype(jnp.float32), axis=0)


def head_major(value, heads):
    return value.reshape(value.shape[0], heads, -1).transpose(1, 0, 2)


def token_major(value):
    return value.transpose(1, 0, 2).reshape(value.shape[1], value.shape[0] * value.shape[2])


def masked_scores(left, right, left_ids, right_ids, scale):
    scores = back_product(left, right) * scale
    return jnp.where(left_ids[:, None] == right_ids[None, :], scores, -jnp.inf)


def body(
    hidden_in,
    query_weight,
    key_weight,
    value_weight,
    output_weight,
    inner_weight,
    outer_weight,
    query_bias,
    value_bias,
    output_bias,
    attention_gain,
    attention_shift,
    inner_bias,
    outer_bias,
    final_gain,
    final_shift,
    cotangent,
    grad_mask,
    cluster_order,
):
    rows = hidden_in.shape[0]
    width = hidden_in.shape[1]
    heads = cluster_order.shape[1]
    length = cluster_order.shape[2]
    scale = 1.0 / math.sqrt(width // heads)
    masters = (
        query_weight,
        key_weight,
        value_weight,
        output_weight,
        inner_weight,
        outer_weight,
        query_bias,
        value_bias,
        output_bias,
        attention_gain,
        attention_shift,
        inner_bias,
        outer_bias,
        final_gain,
        final_shift,
    )
    lowered = [master.astype(jnp.bfloat16) for master in masters]
    fetched = (
        lax.all_gather(lowered[0], ("seq", "blk"), axis=0, tiled=True),
        lax.all_gather(lowered[1], ("seq", "blk"), axis=0, tiled=True),
        lax.all_gather(lowered[2], ("seq", "blk"), axis=0, tiled=True),
        lax.all_gather(lowered[3], ("seq", "blk"), axis=0, tiled=True),
        lax.all_gather(lowered[4], ("seq", "blk"), axis=0, tiled=True),
        lax.all_gather(lowered[5], ("seq", "blk"), axis=0, tiled=True),
        lax.all_gather(lowered[6], ("seq", "blk"), axis=0, tiled=True),
        lax.all_gather(lowered[7], ("seq", "blk"), axis=0, tiled=True),
        lax.all_gather(lowered[8], ("seq", "blk"), axis=0, tiled=True),
        lax.all_gather(lowered[9], ("seq", "blk"), axis=0, tiled=True),
        lax.all_gather(lowered[10], ("seq", "blk"), axis=0, tiled=True),
        lax.all_gather(lowered[11], ("seq", "blk"), axis=0, tiled=True),
        lax.all_gather(lowered[12], ("seq", "blk"), axis=0, tiled=True),
        lax.all_gather(lowered[13], ("seq", "blk"), axis=0, tiled=True),
        lax.all_gather(lowered[14], ("seq", "blk"), axis=0, tiled=True),
    )
    query_full, key_full, value_full, output_full, inner_full, outer_full = fetched[0:6]
    vectors = [vector.astype(jnp.float32) for vector in fetched[6:15]]
    (
        bias_query,
        bias_value,
        bias_output,
        gain_first,
        shift_first,
        bias_inner,
        bias_outer,
        gain_final,
        shift_final,
    ) = vectors
    hidden = hidden_in.astype(jnp.float32)
    query_low = (
        jnp.dot(hidden_in, query_full, preferred_element_type=jnp.float32) + bias_query
    ).astype(jnp.bfloat16)
    keys_low = jnp.dot(hidden_in, key_full, preferred_element_type=jnp.float32).astype(jnp.bfloat16)
    values_low = (
        jnp.dot(hidden_in, value_full, preferred_element_type=jnp.float32) + bias_value
    ).astype(jnp.bfloat16)
    all_keys, all_values = (
        lax.all_gather(keys_low, "blk", axis=0, tiled=True),
        lax.all_gather(values_low, "blk", axis=0, tiled=True),
    )
    order = cluster_order[0]
    head_rows = jnp.broadcast_to(jnp.arange(heads, dtype=jnp.int32)[:, None], (heads, length))
    positions = jnp.broadcast_to(jnp.arange(length, dtype=jnp.int32)[None, :], (heads, length))
    inverse = jnp.zeros((heads, length), jnp.int32).at[head_rows, order].set(positions)
    key_cluster = inverse // CLUSTER
    member = lax.dynamic_slice_in_dim(key_cluster, lax.axis_index("blk") * rows, rows, 1)
    query_heads = head_major(query_low, heads)
    key_heads = head_major(all_keys, heads)
    value_heads = head_major(all_values, heads)
    head_ids = jnp.arange(heads, dtype=jnp.int32)

    def attend(index):
        scores = masked_scores(
            query_heads[index], key_heads[index], member[index], key_cluster[index], scale
        )
        peak = jnp.max(scores, axis=-1, keepdims=True)
        weights = jnp.exp(scores - peak)
        total = jnp.sum(weights, axis=-1, keepdims=True)
        probs_low = (weights / total).astype(jnp.bfloat16)
        mixed = jnp.dot(probs_low, value_heads[index], preferred_element_type=jnp.float32)
        return (mixed, (peak + jnp.log(total))[:, 0])

    mixed, logsum = lax.map(attend, head_ids)
    context_low = token_major(mixed).astype(jnp.bfloat16)
    attention_out = (
        jnp.dot(context_low, output_full, preferred_element_type=jnp.float32) + bias_output
    )
    first_norm, first_pull = jax.vjp(layer_norm, hidden + attention_out, gain_first, shift_first)
    first_low = first_norm.astype(jnp.bfloat16)
    inner_pre = jnp.dot(first_low, inner_full, preferred_element_type=jnp.float32) + bias_inner
    activated, gelu_pull = jax.vjp(exact_gelu, inner_pre)
    activated_low = activated.astype(jnp.bfloat16)
    outer_out = jnp.dot(activated_low, outer_full, preferred_element_type=jnp.float32) + bias_outer
    final_norm, final_pull = jax.vjp(layer_norm, first_norm + outer_out, gain_final, shift_final)
    hidden_out = final_norm.astype(jnp.bfloat16)
    out_grad = cotangent.astype(jnp.float32) * grad_mask.astype(jnp.float32)
    second_grad, grad_final_gain, grad_final_shift = final_pull(out_grad)
    outer_low = second_grad.astype(jnp.bfloat16)
    back_weights = (
        lax.all_gather(lowered[0], ("seq", "blk"), axis=0, tiled=True),
        lax.all_gather(lowered[1], ("seq", "blk"), axis=0, tiled=True),
        lax.all_gather(lowered[2], ("seq", "blk"), axis=0, tiled=True),
        lax.all_gather(lowered[3], ("seq", "blk"), axis=0, tiled=True),
        lax.all_gather(lowered[4], ("seq", "blk"), axis=0, tiled=True),
        lax.all_gather(lowered[5], ("seq", "blk"), axis=0, tiled=True),
    )
    grad_outer_weight = row_contract(activated_low, outer_low)
    grad_outer_bias = column_sum(outer_low)
    inner_low = gelu_pull(back_product(outer_low, back_weights[5]))[0].astype(jnp.bfloat16)
    grad_inner_weight = row_contract(first_low, inner_low)
    grad_inner_bias = column_sum(inner_low)
    first_grad = back_product(inner_low, back_weights[4]) + second_grad
    residual_grad, grad_attention_gain, grad_attention_shift = first_pull(first_grad)
    attn_low = residual_grad.astype(jnp.bfloat16)
    grad_output_weight = row_contract(context_low, attn_low)
    grad_output_bias = column_sum(attn_low)
    context_grad = back_product(attn_low, back_weights[3]).astype(jnp.bfloat16)
    grad_heads = head_major(context_grad, heads)

    def own_rows_back(index):
        scores = masked_scores(
            query_heads[index], key_heads[index], member[index], key_cluster[index], scale
        )
        probs = jnp.exp(scores - logsum[index][:, None])
        probs_low = probs.astype(jnp.bfloat16)
        grad_part = grad_heads[index]
        prob_grad = back_product(grad_part, value_heads[index])
        weighted = jnp.sum(probs * prob_grad, axis=-1, keepdims=True)
        score_low = (probs * (prob_grad - weighted)).astype(jnp.bfloat16)
        query_grad = (
            jnp.dot(score_low, key_heads[index], preferred_element_type=jnp.float32) * scale
        )
        return (probs_low, score_low, query_grad, weighted[:, 0])

    def attend_back(index):
        probs_low, score_low, query_grad, weighted = own_rows_back(index)
        key_sum = row_contract(score_low, query_heads[index]) * scale
        value_sum = row_contract(probs_low, grad_heads[index])
        return (query_grad, key_sum, value_sum)

    query_grads, key_grads, value_grads = lax.map(attend_back, head_ids)
    key_own, value_own = (
        lax.psum_scatter(token_major(key_grads), "blk", scatter_dimension=0, tiled=True),
        lax.psum_scatter(token_major(value_grads), "blk", scatter_dimension=0, tiled=True),
    )
    query_grad_low = token_major(query_grads).astype(jnp.bfloat16)
    key_grad_low = key_own.astype(jnp.bfloat16)
    value_grad_low = value_own.astype(jnp.bfloat16)
    grad_query_weight = row_contract(hidden_in, query_grad_low)
    grad_key_weight = row_contract(hidden_in, key_grad_low)
    grad_value_weight = row_contract(hidden_in, value_grad_low)
    grad_query_bias = column_sum(query_grad_low)
    grad_value_bias = column_sum(value_grad_low)
    input_grad = (
        back_product(query_grad_low, back_weights[0])
        + back_product(key_grad_low, back_weights[1])
        + back_product(value_grad_low, back_weights[2])
        + residual_grad
    )
    shares = (
        lax.psum_scatter(grad_query_weight, ("seq", "blk"), scatter_dimension=0, tiled=True),
        lax.psum_scatter(grad_key_weight, ("seq", "blk"), scatter_dimension=0, tiled=True),
        lax.psum_scatter(grad_value_weight, ("seq", "blk"), scatter_dimension=0, tiled=True),
        lax.psum_scatter(grad_output_weight, ("seq", "blk"), scatter_dimension=0, tiled=True),
        lax.psum_scatter(grad_inner_weight, ("seq", "blk"), scatter_dimension=0, tiled=True),
        lax.psum_scatter(grad_outer_weight, ("seq", "blk"), scatter_dimension=0, tiled=True),
        lax.psum_scatter(grad_query_bias, ("seq", "blk"), scatter_dimension=0, tiled=True),
        lax.psum_scatter(grad_value_bias, ("seq", "blk"), scatter_dimension=0, tiled=True),
        lax.psum_scatter(grad_output_bias, ("seq", "blk"), scatter_dimension=0, tiled=True),
        lax.psum_scatter(grad_attention_gain, ("seq", "blk"), scatter_dimension=0, tiled=True),
        lax.psum_scatter(grad_attention_shift, ("seq", "blk"), scatter_dimension=0, tiled=True),
        lax.psum_scatter(grad_inner_bias, ("seq", "blk"), scatter_dimension=0, tiled=True),
        lax.psum_scatter(grad_outer_bias, ("seq", "blk"), scatter_dimension=0, tiled=True),
        lax.psum_scatter(grad_final_gain, ("seq", "blk"), scatter_dimension=0, tiled=True),
        lax.psum_scatter(grad_final_shift, ("seq", "blk"), scatter_dimension=0, tiled=True),
    )
    return (hidden_out, input_grad) + tuple(shares)


def solution(mesh):
    placed = (
        P(("seq", "blk"), None),
        P(("seq", "blk"), None),
        P(("seq", "blk"), None),
        P(("seq", "blk"), None),
        P(("seq", "blk"), None),
        P(("seq", "blk"), None),
        P(("seq", "blk"), None),
        P(("seq", "blk")),
        P(("seq", "blk")),
        P(("seq", "blk")),
        P(("seq", "blk")),
        P(("seq", "blk")),
        P(("seq", "blk")),
        P(("seq", "blk")),
        P(("seq", "blk")),
        P(("seq", "blk")),
        P(("seq", "blk"), None),
        P(("seq", "blk"), None),
        P("seq", None, None),
    )
    return jax.shard_map(
        body,
        mesh=mesh,
        in_specs=placed,
        out_specs=(
            P(("seq", "blk"), None),
            P(("seq", "blk"), None),
            P(("seq", "blk"), None),
            P(("seq", "blk"), None),
            P(("seq", "blk"), None),
            P(("seq", "blk"), None),
            P(("seq", "blk"), None),
            P(("seq", "blk"), None),
            P(("seq", "blk")),
            P(("seq", "blk")),
            P(("seq", "blk")),
            P(("seq", "blk")),
            P(("seq", "blk")),
            P(("seq", "blk")),
            P(("seq", "blk")),
            P(("seq", "blk")),
            P(("seq", "blk")),
        ),
        check_vma=False,
    )
```

profile of v0, /device:TPU:9, one launch (start us, length us, event | category | flops | bytes accessed | tf_op | source)
XLA Modules:
  0.0 1856.9 jit_solution(1359960909218621656)
XLA Ops:
  12.1 54.3 %all-gather.11.cloned.1.call-done = bf16[768,768]{1,0:T(8,128)(2,1)} async-done(((bf16[24,768]{1,0:T(8,128)(2,1)}), bf16[768,768]{1,0:T(8,128)(2,1)}) %all-gather.11.cloned.1.call-update) | async-done | bytes 1179664 | tf_op jit(solution)/shard_map/all_gather | solution.py:99
  71.8 38.4 %all-reduce.19 = (bf16[768]{0:T(1024)(128)(2,1)S(1)}, bf16[768]{0:T(1024)(128)(2,1)S(1)}, bf16[768]{0:T(1024)(128)(2,1)S(1)}, bf16[768]{0:T(1024)(128)(2,1)S(1)}...) all-reduce(bf16[768]{0:T(1024)(128)(2,1)S(1)} %dynamic-update-slice, ...), channel_id=1, replica_groups=mesh['seq'=4,'blk'=8] {'seq','blk'}, use_global_device_ids=true, to_apply=%add | all-reduce | flops 9216 | bytes 36864
  110.3 12.9 all-gather.15.cloned.1.call-done
  130.6 179.9 %scatter_custom_fusion = s32[49152]{0:T(1024)S(1)} fusion(s32[49152]{0:T(1024)S(1)} %reshape.203, s32[49152]{0:T(1024)S(1)} %reshape.205, s32[]{:T(128)} %constant.70.clone.1), kind=kCustom, calls=%fused_computation.117 | custom fusion | bytes 196612
  314.5 8.7 copy.58
  323.2 12.0 copy.61
  335.2 8.7 copy.59
  343.9 12.1 copy.62
  356.0 117.8 %while.26 = (s32[]{:T(128)}, bf16[12,512,64]{1,2,0:T(8,128)(2,1)S(1)}, f32[12,512]{1,0:T(8,128)S(1)}, s32[12]{0:T(128)S(1)}, s32[12,512]{1,0:T(8,128)S(1)}, /*in...) while((s32[]{:T(128)}, ...), condition=%wide.region_4.5_spmd, body=%wide.region_1.4_spmd.sunk | while | flops 555744768 | bytes 27602112 | solution.py:161
  477.6 20.0 %multiply_convert_fusion.1 = (bf16[512,3072]{1,0:T(8,128)(2,1)}, f32[512,3072]{1,0:T(8,128)}, f32[512,3072]{1,0:T(8,128)}) fusion(f32[3072]{0:T(1024)S(1)} %convert_element_type.187, bf16[768,3072]{1,0:T(8,128)(2,1)} %all-gather.21.cloned.1.call-done, f32[512,768]{1,0:T(8,128)S(1)} %get-tuple-element.311, f32[768]{0:T(1024)S(1)} %convert_element_type.183, ...), kind=kOutput, calls=%fused_computation.58 | convolution fusion | flops 2521694208 | bytes 22042624 | tf_op jit(solution)/shard_map/dot_general | solution.py:168
  509.7 8.4 convert_reduce_fusion
  525.8 368.6 %while.27 = (s32[]{:T(128)}, bf16[12,512,64]{1,2,0:T(8,128)(2,1)S(1)}, f32[12,4096,64]{1,2,0:T(8,128)}, f32[12,4096,64]{1,2,0:T(8,128)}, s32[12]{0:T(128)S(1)}, ...) while((s32[]{:T(128)}, ...), condition=%wide.region_15.16_spmd, body=%wide.region_13.15_spmd.sunk | while | flops 1363443200 | bytes 142150000 | solution.py:219
  532.3 8.1 multiply_reduce_fusion.9
  593.6 8.1 multiply_reduce_fusion.9
  624.3 8.1 multiply_reduce_fusion.9
  655.1 8.1 multiply_reduce_fusion.9
  747.2 8.1 multiply_reduce_fusion.9
  777.8 8.1 multiply_reduce_fusion.9
  808.5 8.1 multiply_reduce_fusion.9
  839.2 8.1 multiply_reduce_fusion.9
  869.9 8.1 multiply_reduce_fusion.9
  905.2 9.0 fusion.57
  914.2 8.5 fusion.69
  922.8 97.6 %reduce-scatter.15.cloned.1.call-done = f32[512,768]{0,1:T(8,128)} async-done(((f32[4096,768]{0,1:T(8,128)}), f32[512,768]{0,1:T(8,128)}) %reduce-scatter.15.cloned.1.call-update) | async-done | bytes 1572880 | tf_op jit(solution)/shard_map/reduce_scatter | solution.py:221
  1027.2 123.0 %reduce-scatter.17.cloned.1.call-done = f32[512,768]{0,1:T(8,128)} async-done(((f32[4096,768]{0,1:T(8,128)}), f32[512,768]{0,1:T(8,128)}) %reduce-scatter.17.cloned.1.call-update) | async-done | bytes 1572880 | tf_op jit(solution)/shard_map/reduce_scatter | solution.py:222
  1162.2 40.5 %all-reduce.18 = (f32[768]{0:T(1024)S(1)}, f32[768]{0:T(1024)S(1)}, f32[768]{0:T(1024)S(1)}, f32[768]{0:T(1024)S(1)}, f32[768]{0:T(1024)S(1)}, /*index=5*/f32[30...) all-reduce(f32[768]{0:T(1024)S(1)} %reduce_sum.186, ...), channel_id=10, replica_groups=mesh['seq'=4,'blk'=8] {'seq','blk'}, use_global_device_ids=true, to_apply=%region_25.26.clone | all-reduce | flops 9216 | bytes 73728
  1214.5 39.1 %reduce-scatter.25.cloned.1.call-done = f32[24,768]{1,0:T(8,128)} async-done(((f32[768,768]{1,0:T(8,128)}), f32[24,768]{1,0:T(8,128)}) %reduce-scatter.25.cloned.1.call-update) | async-done | bytes 73744
  1253.6 104.4 %reduce-scatter.19.cloned.1.call-done = f32[24,768]{1,0:T(8,128)} async-done(((f32[768,768]{1,0:T(8,128)}), f32[24,768]{1,0:T(8,128)}) %reduce-scatter.19.cloned.1.call-update) | async-done | bytes 73744 | tf_op jit(solution)/shard_map/reduce_scatter | solution.py:242
  1358.0 141.5 %reduce-scatter.21.cloned.1.call-done = f32[24,3072]{1,0:T(8,128)} async-done(((f32[768,3072]{1,0:T(8,128)}), f32[24,3072]{1,0:T(8,128)}) %reduce-scatter.21.cloned.1.call-update) | async-done | bytes 294928 | tf_op jit(solution)/shard_map/reduce_scatter | solution.py:243
  1499.5 141.5 %reduce-scatter.23.cloned.1.call-done = f32[96,768]{1,0:T(8,128)} async-done(((f32[3072,768]{1,0:T(8,128)}), f32[96,768]{1,0:T(8,128)}) %reduce-scatter.23.cloned.1.call-update) | async-done | bytes 294928 | tf_op jit(solution)/shard_map/reduce_scatter | solution.py:244
  1641.0 104.5 %reduce-scatter.27.cloned.1.call-done = f32[24,768]{1,0:T(8,128)} async-done(((f32[768,768]{1,0:T(8,128)}), f32[24,768]{1,0:T(8,128)}) %reduce-scatter.27.cloned.1.call-update) | async-done | bytes 73744
  1745.5 104.4 %reduce-scatter.29.cloned.1.call-done = f32[24,768]{1,0:T(8,128)} async-done(((f32[768,768]{1,0:T(8,128)}), f32[24,768]{1,0:T(8,128)}) %reduce-scatter.29.cloned.1.call-update) | async-done | bytes 73744
  (520 shorter events, 450.9 us)
Async XLA Ops:
  7.2 115.9 %copy-start.2 = (bf16[512,768]{1,0:T(8,128)(2,1)S(1)}, bf16[512,768]{1,0:T(8,128)(2,1)}, u32[]{:S(2)}) copy-start(bf16[512,768]{1,0:T(8,128)(2,1)} %param.23) | copy-start | bytes 2359300
  7.2 62.5 %copy-start.25 = (f32[24]{0:T(128)S(1)}, f32[24]{0:T(128)}, u32[]{:S(2)}) copy-start(f32[24]{0:T(128)} %param.30) | copy-start | bytes 292
  7.2 62.5 %copy-start.26 = (f32[24]{0:T(128)S(1)}, f32[24]{0:T(128)}, u32[]{:S(2)}) copy-start(f32[24]{0:T(128)} %param.31) | copy-start | bytes 292
  7.2 62.5 %copy-start.27 = (f32[24]{0:T(128)S(1)}, f32[24]{0:T(128)}, u32[]{:S(2)}) copy-start(f32[24]{0:T(128)} %param.32) | copy-start | bytes 292
  7.2 62.5 %copy-start.28 = (f32[24]{0:T(128)S(1)}, f32[24]{0:T(128)}, u32[]{:S(2)}) copy-start(f32[24]{0:T(128)} %param.34) | copy-start | bytes 292
  7.2 62.6 %copy-start.29 = (f32[24]{0:T(128)S(1)}, f32[24]{0:T(128)}, u32[]{:S(2)}) copy-start(f32[24]{0:T(128)} %param.33) | copy-start | bytes 292
  7.3 62.6 %copy-start.30 = (f32[96]{0:T(128)S(1)}, f32[96]{0:T(128)}, u32[]{:S(2)}) copy-start(f32[96]{0:T(128)} %param.35) | copy-start | bytes 1156
  7.3 62.6 %copy-start.31 = (f32[24]{0:T(128)S(1)}, f32[24]{0:T(128)}, u32[]{:S(2)}) copy-start(f32[24]{0:T(128)} %param.36) | copy-start | bytes 292
  7.3 62.6 %copy-start.32 = (f32[24]{0:T(128)S(1)}, f32[24]{0:T(128)}, u32[]{:S(2)}) copy-start(f32[24]{0:T(128)} %param.38) | copy-start | bytes 292
  7.3 62.6 %copy-start.33 = (f32[24]{0:T(128)S(1)}, f32[24]{0:T(128)}, u32[]{:S(2)}) copy-start(f32[24]{0:T(128)} %param.37) | copy-start | bytes 292
  7.3 59.1 %all-gather.11.cloned.1.call-start = ((), (), s32[]{:S(2)}) async-start(), calls=%async_computation.9 | async-start | bytes 1216512 | tf_op jit(solution)/shard_map/all_gather | solution.py:99
  8.9 114.2 %all-gather.15.cloned.1.call-start = ((), (), s32[]{:S(2)}) async-start(), calls=%async_computation.11 | async-start | bytes 1216512 | tf_op jit(solution)/shard_map/all_gather | solution.py:100
  10.5 300.3 %all-gather.9.cloned.1.call-start = ((), (), s32[]{:S(2)}) async-start(), calls=%async_computation.8 | async-start | bytes 1216512 | tf_op jit(solution)/shard_map/all_gather | solution.py:98
  12.1 302.4 %all-gather.13.cloned.1.call-start = ((), (), s32[]{:S(2)}) async-start(), calls=%async_computation.10 | async-start | bytes 7077888 | tf_op jit(solution)/shard_map/all_gather | solution.py:136
  69.6 56.5 %copy-start.18 = (f32[24,768]{1,0:T(8,128)S(1)}, f32[24,768]{1,0:T(8,128)}, u32[]{:S(2)}) copy-start(f32[24,768]{1,0:T(8,128)} %param.27) | copy-start | bytes 221188
  69.6 57.2 %copy-start.15 = (f32[24,3072]{1,0:T(8,128)S(1)}, f32[24,3072]{1,0:T(8,128)}, u32[]{:S(2)}) copy-start(f32[24,3072]{1,0:T(8,128)} %param.28) | copy-start | bytes 884740
  69.6 58.0 %copy-start.16 = (f32[96,768]{1,0:T(8,128)S(1)}, f32[96,768]{1,0:T(8,128)}, u32[]{:S(2)}) copy-start(f32[96,768]{1,0:T(8,128)} %param.29) | copy-start | bytes 884740
  69.7 265.6 %all-gather.17.cloned.1.call-start = ((), (), s32[]{:S(2)}) async-start(), calls=%async_computation.12 | async-start | bytes 7077888 | tf_op jit(solution)/shard_map/all_gather | solution.py:137
  110.2 18.5 copy-start.23
  110.3 19.4 %copy-start.22 = (s32[2]{0:T(128)S(1)}, s32[2]{0:T(128)}, u32[]{:S(2)}) copy-start(s32[2]{0:T(128)} %constant.161) | copy-start | bytes 28
  126.1 347.8 %all-gather.19.cloned.1.call-start = ((), (), s32[]{:S(2)}) async-start(), calls=%async_computation.13 | async-start | bytes 1216512 | tf_op jit(solution)/shard_map/all_gather | solution.py:101
  126.8 350.8 %all-gather.21.cloned.1.call-start = ((), (), s32[]{:S(2)}) async-start(), calls=%async_computation.14 | async-start | bytes 4866048 | tf_op jit(solution)/shard_map/all_gather | solution.py:102
  127.6 371.7 %all-gather.23.cloned.1.call-start = ((), (), s32[]{:S(2)}) async-start(), calls=%async_computation.15 | async-start | bytes 4866048 | tf_op jit(solution)/shard_map/all_gather | solution.py:103
  128.3 892.1 %reduce-scatter.15.cloned.1.call-start = ((), (), s32[]{:S(2)}) async-start(), calls=%async_computation.16 | async-start | bytes 14155776 | tf_op jit(solution)/shard_map/reduce_scatter | solution.py:221
  477.2 40.9 %copy-start.5 = (f32[512,768]{1,0:T(8,128)}, f32[512,768]{1,0:T(8,128)S(1)}, u32[]{:S(2)}) copy-start(f32[512,768]{1,0:T(8,128)S(1)} %get-tuple-element.311) | copy-start | bytes 4718596
  894.4 255.8 %reduce-scatter.17.cloned.1.call-start = ((), (), s32[]{:S(2)}) async-start(), calls=%async_computation.17 | async-start | bytes 14155776 | tf_op jit(solution)/shard_map/reduce_scatter | solution.py:222
  895.0 358.7 %reduce-scatter.25.cloned.1.call-start = ((), (), s32[]{:S(2)}) async-start(), calls=%async_computation.21 | async-start | bytes 2433024
  901.2 456.8 %reduce-scatter.19.cloned.1.call-start = ((), (), s32[]{:S(2)}) async-start(), calls=%async_computation.18 | async-start | bytes 2433024 | tf_op jit(solution)/shard_map/reduce_scatter | solution.py:242
  904.9 594.7 %reduce-scatter.21.cloned.1.call-start = ((), (), s32[]{:S(2)}) async-start(), calls=%async_computation.19 | async-start | bytes 9732096 | tf_op jit(solution)/shard_map/reduce_scatter | solution.py:243
  914.2 726.8 %reduce-scatter.23.cloned.1.call-start = ((), (), s32[]{:S(2)}) async-start(), calls=%async_computation.20 | async-start | bytes 9732096 | tf_op jit(solution)/shard_map/reduce_scatter | solution.py:244
  922.8 822.7 %reduce-scatter.27.cloned.1.call-start = ((), (), s32[]{:S(2)}) async-start(), calls=%async_computation.22 | async-start | bytes 2433024
  1027.1 822.8 %reduce-scatter.29.cloned.1.call-start = ((), (), s32[]{:S(2)}) async-start(), calls=%async_computation.23 | async-start | bytes 2433024
  (67 other events, 376.9 us)
Sparse Core Ops, SparseCore 0:
  11.7 54.7 all-gather.10
  70.0 53.0 all-gather.14
  126.7 52.9 all-gather.8
  181.8 62.4 all-gather.12
  246.4 63.3 all-gather.16
  313.3 53.8 all-gather.18
  370.7 63.4 all-gather.20
  437.2 61.9 all-gather.22
  894.5 125.8 reduce-scatter.14
  1022.6 127.6 reduce-scatter.16
  1156.1 97.5 reduce-scatter.24
  1259.4 98.6 reduce-scatter.18
  1364.5 135.0 reduce-scatter.20
  1505.9 135.1 reduce-scatter.22
  1646.7 98.7 reduce-scatter.26
  1751.2 98.6 reduce-scatter.28
where the time goes:
time: 1870 us; the launch traced here: 1860 us
  waiting for transfers between devices  926 us (50%)
  matrix products  387 us (21%)
  local copies, waits for them, and re-layouts  273 us (15%)
  other arithmetic  128 us (7%)
  blocking collectives  78.9 us (4%)
  loops' own time  48.2 us (3%)
    unnamed x19, waiting for transfers between devices  249 us
    unnamed x102, local copies, waits for them, and re-layouts  199 us
    dot_general x42, matrix products, back_product(): lax.dot_general(grad, weight, (((1,), (1,)), ((), ())), preferred_element...  182 us
    reduce_scatter x1, waiting for transfers between devices, body(): lax.psum_scatter(grad_inner_weight, ('seq', 'blk'), scatter_dimension=0,...  142 us
    reduce_scatter x1, waiting for transfers between devices, body(): lax.psum_scatter(grad_outer_weight, ('seq', 'blk'), scatter_dimension=0,...  141 us
    reduce_scatter x1, waiting for transfers between devices, body(): lax.psum_scatter(token_major(value_grads), 'blk', scatter_dimension=0, ti...  123 us
    reduce_scatter x1, waiting for transfers between devices, body(): lax.psum_scatter(grad_output_weight, ('seq', 'blk'), scatter_dimension=0,...  104 us
    reduce_scatter x1, waiting for transfers between devices, body(): lax.psum_scatter(token_major(key_grads), 'blk', scatter_dimension=0, tile...  97.6 us
  transfers between devices with their start and end apart: 16, of which 11 were waited for; matrix products, arithmetic and copies ran while one was open for 22% of the time, Pallas kernels for 0%

commit v1 on v0

--- a/solution.py
+++ b/solution.py
@@ -1,11 +1,54 @@
+import functools
 import math
 
 import jax
 import jax.numpy as jnp
 from jax import lax
+from jax.experimental import pallas as pl
+from jax.experimental.pallas import tpu as pltpu
 from jax.sharding import PartitionSpec as P
 
+MESH = pl.DeviceIdType.MESH
+ANY = pl.ANY
+LOW = jnp.bfloat16
+F32 = jnp.float32
+BIG = 60 * 2**20
+GROUP = 4
 CLUSTER = 128
+
+
+def spec(space):
+    return pl.BlockSpec(memory_space=space)
+
+
+def nt_dot(left, right):
+    return lax.dot_general(left, right, (((1,), (1,)), ((), ())), preferred_element_type=F32)
+
+
+def tn_dot(left, right):
+    return lax.dot_general(left, right, (((0,), (0,)), ((), ())), preferred_element_type=F32)
+
+
+def nn_dot(left, right):
+    return jnp.dot(left, right, preferred_element_type=F32)
+
+
+def greet(targets):
+    sem = pltpu.get_barrier_semaphore()
+    for target in targets:
+        pl.semaphore_signal(sem, inc=1, device_id=target, device_id_type=MESH)
+    pl.semaphore_wait(sem, len(targets))
+
+
+def send(src, dst, send_sem, recv_sem, target):
+    return pltpu.make_async_remote_copy(
+        src_ref=src,
+        dst_ref=dst,
+        send_sem=send_sem,
+        recv_sem=recv_sem,
+        device_id=target,
+        device_id_type=MESH,
+    )
 
 
 epsilon = 1e-06
@@ -43,6 +86,769 @@
 
 def token_major(value):
     return value.transpose(1, 0, 2).reshape(value.shape[1], value.shape[0] * value.shape[2])
+
+
+def entry_kernel(
+    seqs, blks, parts, x_ref, w_ref, o_ref, wall_ref,
+    own_sem, ssem, rsem, wl, ws, wr, us, ur,
+):
+    half = blks // 2
+    s = lax.axis_index("seq")
+    b = lax.axis_index("blk")
+    k = b // 2
+    c = lax.rem(b, 2)
+    mate = b + 1 - 2 * c
+    left = lax.rem(b + blks - 2, blks)
+    right = lax.rem(b + 2, blks)
+    has_left = k > 0
+    has_right = k < half - 1
+    blk_peers = [{"blk": lax.rem(b + d, blks)} for d in range(1, blks)]
+    seq_peers = [{"seq": lax.rem(s + d, seqs)} for d in range(1, seqs)]
+    greet(blk_peers + seq_peers)
+
+    def slab(d):
+        peer = lax.rem(b + d, blks)
+        return send(w_ref.at[peer], wall_ref.at[s, b], ws.at[d], wr.at[d], {"blk": peer})
+
+    def group(d):
+        return send(
+            wall_ref.at[s], wall_ref.at[s], us.at[d], ur.at[d], {"seq": lax.rem(s + d, seqs)}
+        )
+
+    def piece(src, blk, p, to, way):
+        return send(src, o_ref.at[blk, p], ssem.at[way, blk, p], rsem.at[blk, p], {"blk": to})
+
+    for d in range(1, blks):
+        slab(d).start()
+    own_slab = pltpu.make_async_copy(w_ref.at[b], wall_ref.at[s, b], wl)
+    own_slab.start()
+    for p in range(parts):
+        @pl.when(has_left)
+        def _():
+            piece(x_ref.at[p], b, p, left, 0).start()
+
+        @pl.when(has_right)
+        def _():
+            piece(x_ref.at[p], b, p, right, 1).start()
+    for p in range(parts):
+        piece(x_ref.at[p], b, p, mate, 2).start()
+    own = pltpu.make_async_copy(x_ref, o_ref.at[b], own_sem)
+    own.start()
+    own_slab.wait()
+    for d in range(1, blks):
+        slab(d).wait_recv()
+    for d in range(1, seqs):
+        group(d).start()
+    for t in range(1, half):
+        for p in range(parts):
+            @pl.when(k - t >= 0)
+            def _():
+                blk = b - 2 * t
+                piece(o_ref.at[blk, p], blk, p, right, 1).wait_recv()
+
+                @pl.when(has_right)
+                def _():
+                    piece(o_ref.at[blk, p], blk, p, right, 1).start()
+
+                piece(o_ref.at[blk, p], blk, p, mate, 2).start()
+
+            @pl.when(k + t < half)
+            def _():
+                blk = b + 2 * t
+                piece(o_ref.at[blk, p], blk, p, left, 0).wait_recv()
+
+                @pl.when(has_left)
+                def _():
+                    piece(o_ref.at[blk, p], blk, p, left, 0).start()
+
+                piece(o_ref.at[blk, p], blk, p, mate, 2).start()
+    for j in range(half):
+        blk = 2 * j + 1 - c
+        for p in range(parts):
+            piece(o_ref.at[blk, p], blk, p, mate, 2).wait_recv()
+    for j in range(half):
+        blk = 2 * j + c
+        for p in range(parts):
+            piece(o_ref.at[blk, p], blk, p, mate, 2).wait_send()
+
+            @pl.when(jnp.logical_and(has_right, j <= k))
+            def _():
+                piece(o_ref.at[blk, p], blk, p, right, 1).wait_send()
+
+            @pl.when(jnp.logical_and(has_left, j >= k))
+            def _():
+                piece(o_ref.at[blk, p], blk, p, left, 0).wait_send()
+    own.wait()
+    for d in range(1, blks):
+        slab(d).wait_send()
+    for d in range(1, seqs):
+        group(d).wait()
+
+
+def entry(hidden, slabs, seqs, blks, parts):
+    rows, width = hidden.shape
+    dma = pltpu.SemaphoreType.DMA
+    return pl.pallas_call(
+        functools.partial(entry_kernel, seqs, blks, parts),
+        name="entry",
+        out_shape=(
+            jax.ShapeDtypeStruct((blks, parts, rows // parts, width), LOW),
+            jax.ShapeDtypeStruct((seqs,) + slabs.shape, LOW),
+        ),
+        in_specs=[spec(pltpu.VMEM)] * 2,
+        out_specs=(spec(ANY), spec(ANY)),
+        scratch_shapes=[
+            dma, dma((3, blks, parts)), dma((blks, parts)), dma,
+            dma((blks,)), dma((blks,)), dma((seqs,)), dma((seqs,)),
+        ],
+        compiler_params=pltpu.CompilerParams(collective_id=0, has_side_effects=True),
+        cost_estimate=pl.CostEstimate(flops=0, transcendentals=0, bytes_accessed=200 * 10**6),
+    )(hidden.reshape(parts, rows // parts, width), slabs)
+
+
+def return_kernel(blks, nat_ref, pack_ref, even_ref, odd_ref, buf, lsem, ssem, rsem):
+    b = lax.axis_index("blk")
+    k = b // 2
+    c = lax.rem(b, 2)
+    greet([{"blk": lax.rem(b + d, blks)} for d in range(1, blks)])
+    start_return(blks, b, k, c, nat_ref, pack_ref, even_ref, odd_ref, buf, lsem, ssem, rsem)
+    finish_return(blks, b, k, c, nat_ref, pack_ref, even_ref, odd_ref, ssem, rsem)
+
+
+def full_way(blks, b, d, nat_ref, even_ref, ssem, rsem, slot):
+    peer = lax.rem(b + d, blks)
+    return send(nat_ref.at[peer], even_ref.at[slot], ssem.at[d], rsem.at[d], {"blk": peer})
+
+
+def start_return(blks, b, k, c, nat_ref, pack_ref, even_ref, odd_ref, buf, lsem, ssem, rsem):
+    @pl.when(c == 0)
+    def _():
+        for d in range(1, blks):
+            full_way(blks, b, d, nat_ref, even_ref, ssem, rsem, k).start()
+        inward = pltpu.make_async_copy(nat_ref.at[b], buf, lsem)
+        inward.start()
+        inward.wait()
+        outward = pltpu.make_async_copy(buf, even_ref.at[k], lsem)
+        outward.start()
+        outward.wait()
+
+    @pl.when(c == 1)
+    def _():
+        for d in range(1, blks):
+            full_way(blks, b, d, pack_ref, odd_ref, ssem, rsem, k).start()
+        part = buf.at[pl.ds(0, pack_ref.shape[1])]
+        inward = pltpu.make_async_copy(pack_ref.at[b], part, lsem)
+        inward.start()
+        inward.wait()
+        outward = pltpu.make_async_copy(part, odd_ref.at[k], lsem)
+        outward.start()
+        outward.wait()
+
+
+def finish_return(blks, b, k, c, nat_ref, pack_ref, even_ref, odd_ref, ssem, rsem):
+    for d in range(1, blks):
+        source = lax.rem(b + blks - d, blks)
+
+        @pl.when(lax.rem(source, 2) == 0)
+        def _():
+            full_way(blks, b, d, nat_ref, even_ref, ssem, rsem, source // 2).wait_recv()
+
+        @pl.when(lax.rem(source, 2) == 1)
+        def _():
+            full_way(blks, b, d, pack_ref, odd_ref, ssem, rsem, source // 2).wait_recv()
+
+    @pl.when(c == 0)
+    def _():
+        for d in range(1, blks):
+            full_way(blks, b, d, nat_ref, even_ref, ssem, rsem, k).wait_send()
+
+    @pl.when(c == 1)
+    def _():
+        for d in range(1, blks):
+            full_way(blks, b, d, pack_ref, odd_ref, ssem, rsem, k).wait_send()
+
+
+def return_rows(nat, pack, collective_id):
+    blks = nat.shape[0]
+    dma = pltpu.SemaphoreType.DMA
+    return pl.pallas_call(
+        functools.partial(return_kernel, blks),
+        name="return_rows",
+        out_shape=(
+            jax.ShapeDtypeStruct((blks // 2,) + nat.shape[1:], LOW),
+            jax.ShapeDtypeStruct((blks // 2,) + pack.shape[1:], LOW),
+        ),
+        in_specs=[spec(ANY)] * 2,
+        out_specs=(spec(ANY), spec(ANY)),
+        scratch_shapes=[pltpu.VMEM(nat.shape[1:], LOW), dma, dma((blks,)), dma((blks,))],
+        compiler_params=pltpu.CompilerParams(collective_id=collective_id, has_side_effects=True),
+        cost_estimate=pl.CostEstimate(flops=0, transcendentals=0, bytes_accessed=80 * 10**6),
+    )(nat, pack)
+
+
+def spread_kernel(blks, even_ref, odd_ref, nat_ref, pack_ref, buf, lsem, ssem, rsem):
+    b = lax.axis_index("blk")
+    c = lax.rem(b, 2)
+    greet([{"blk": lax.rem(b + d, blks)} for d in range(1, blks)])
+
+    def full(d, slot):
+        peer = lax.rem(b + d, blks)
+        return send(
+            even_ref.at[peer // 2], nat_ref.at[slot], ssem.at[d], rsem.at[d], {"blk": peer}
+        )
+
+    def packed(d, slot):
+        peer = lax.rem(b + d, blks)
+        return send(
+            odd_ref.at[peer // 2], pack_ref.at[slot], ssem.at[d], rsem.at[d], {"blk": peer}
+        )
+
+    for d in range(1, blks):
+        to_even = lax.rem(b + d, 2) == 0
+
+        @pl.when(to_even)
+        def _():
+            full(d, b).start()
+
+        @pl.when(jnp.logical_not(to_even))
+        def _():
+            packed(d, b).start()
+
+    @pl.when(c == 0)
+    def _():
+        inward = pltpu.make_async_copy(even_ref.at[b // 2], buf, lsem)
+        inward.start()
+        inward.wait()
+        outward = pltpu.make_async_copy(buf, nat_ref.at[b], lsem)
+        outward.start()
+        outward.wait()
+        for d in range(1, blks):
+            full(d, lax.rem(b + blks - d, blks)).wait_recv()
+
+    @pl.when(c == 1)
+    def _():
+        part = buf.at[pl.ds(0, odd_ref.shape[1])]
+        inward = pltpu.make_async_copy(odd_ref.at[b // 2], part, lsem)
+        inward.start()
+        inward.wait()
+        outward = pltpu.make_async_copy(part, pack_ref.at[b], lsem)
+        outward.start()
+        outward.wait()
+        for d in range(1, blks):
+            packed(d, lax.rem(b + blks - d, blks)).wait_recv()
+
+    for d in range(1, blks):
+        to_even = lax.rem(b + d, 2) == 0
+
+        @pl.when(to_even)
+        def _():
+            full(d, b).wait_send()
+
+        @pl.when(jnp.logical_not(to_even))
+        def _():
+            packed(d, b).wait_send()
+
+
+def spread_rows(even, odd, collective_id):
+    blks = 2 * even.shape[0]
+    dma = pltpu.SemaphoreType.DMA
+    return pl.pallas_call(
+        functools.partial(spread_kernel, blks),
+        name="spread_rows",
+        out_shape=(
+            jax.ShapeDtypeStruct((blks,) + even.shape[1:], LOW),
+            jax.ShapeDtypeStruct((blks,) + odd.shape[1:], LOW),
+        ),
+        in_specs=[spec(ANY)] * 2,
+        out_specs=(spec(ANY), spec(ANY)),
+        scratch_shapes=[pltpu.VMEM(even.shape[1:], LOW), dma, dma((blks,)), dma((blks,))],
+        compiler_params=pltpu.CompilerParams(collective_id=collective_id, has_side_effects=True),
+        cost_estimate=pl.CostEstimate(flops=0, transcendentals=0, bytes_accessed=80 * 10**6),
+    )(even, odd)
+
+
+def exit_kernel(
+    seqs, blks, nat_ref, pack_ref, grad_ref, even_ref, odd_ref, out_ref,
+    buf, stage, total, lsem, ssem, rsem, us, ur, gl, gs, gr,
+):
+    s = lax.axis_index("seq")
+    b = lax.axis_index("blk")
+    k = b // 2
+    c = lax.rem(b, 2)
+    blk_peers = [{"blk": lax.rem(b + d, blks)} for d in range(1, blks)]
+    seq_peers = [{"seq": lax.rem(s + d, seqs)} for d in range(1, seqs)]
+    greet(blk_peers + seq_peers)
+
+    def group(d):
+        peer = lax.rem(s + d, seqs)
+        return send(grad_ref.at[peer], stage.at[d], us.at[d], ur.at[d], {"seq": peer})
+
+    def slab(d):
+        peer = lax.rem(b + d, blks)
+        return send(total.at[peer], out_ref.at[b], gs.at[d], gr.at[d], {"blk": peer})
+
+    for d in range(1, seqs):
+        group(d).start()
+    start_return(blks, b, k, c, nat_ref, pack_ref, even_ref, odd_ref, buf, lsem, ssem, rsem)
+    for d in range(1, seqs):
+        group(d).wait_recv()
+    for o in range(blks):
+        acc = grad_ref[s, o].astype(F32)
+        for d in range(1, seqs):
+            acc = acc + stage[d, o].astype(F32)
+        total[o] = acc.astype(LOW)
+    for d in range(1, blks):
+        slab(d).start()
+    own = pltpu.make_async_copy(total.at[b], out_ref.at[b], gl)
+    own.start()
+    own.wait()
+    finish_return(blks, b, k, c, nat_ref, pack_ref, even_ref, odd_ref, ssem, rsem)
+    for d in range(1, blks):
+        slab(d).wait()
+    for d in range(1, seqs):
+        group(d).wait_send()
+
+
+def leave(nat, pack, grads):
+    blks = nat.shape[0]
+    seqs = grads.shape[0]
+    dma = pltpu.SemaphoreType.DMA
+    return pl.pallas_call(
+        functools.partial(exit_kernel, seqs, blks),
+        name="leave",
+        out_shape=(
+            jax.ShapeDtypeStruct((blks // 2,) + nat.shape[1:], LOW),
+            jax.ShapeDtypeStruct((blks // 2,) + pack.shape[1:], LOW),
+            jax.ShapeDtypeStruct(grads.shape[1:], LOW),
+        ),
+        in_specs=[spec(ANY), spec(ANY), spec(pltpu.VMEM)],
+        out_specs=(spec(ANY), spec(ANY), spec(ANY)),
+        scratch_shapes=[
+            pltpu.VMEM(nat.shape[1:], LOW),
+            pltpu.VMEM(grads.shape, LOW),
+            pltpu.VMEM(grads.shape[1:], LOW),
+            dma, dma((blks,)), dma((blks,)), dma((seqs,)), dma((seqs,)),
+            dma, dma((blks,)), dma((blks,)),
+        ],
+        compiler_params=pltpu.CompilerParams(collective_id=3, has_side_effects=True),
+        cost_estimate=pl.CostEstimate(flops=0, transcendentals=0, bytes_accessed=200 * 10**6),
+    )(nat, pack, grads)
+
+
+def lane_of(rows):
+    return lax.broadcasted_iota(jnp.int32, (rows, 128), 1)
+
+
+def low_lanes(value, slot, hd):
+    lane = lane_of(value.shape[0])
+    keep = jnp.logical_and(lane >= slot * hd, lane < (slot + 1) * hd)
+    return jnp.where(keep, value, 0.0).astype(LOW)
+
+
+def attend_kernel(
+    hd, scale, order, count, hid, weight, bias, proj, nat, pack, rows4, take, mix, back
+):
+    length = hid.shape[0]
+    step = nat.shape[1]
+
+    @pl.loop(0, length // step)
+    def _(i):
+        at = pl.multiple_of(i * step, step)
+        low = (nn_dot(hid[pl.ds(at, step), :], weight[...]) + bias[...]).astype(LOW)
+        proj[pl.ds(at, step), :] = low
+        wide = low.astype(F32)
+        for t in range(3):
+            rows4[pl.ds(at, step), t, :] = wide[:, t * 128 : (t + 1) * 128]
+
+    span = GROUP * 128
+
+    @pl.loop(0, count[0])
+    def _(slot):
+        @pl.loop(0, length // span)
+        def _(i):
+            base = slot * length + i * span
+            for j in range(span):
+                take[j] = rows4[order[base + j]]
+            for u in range(GROUP):
+                own = pl.ds(u * 128, 128)
+                query = low_lanes(take[own, 0, :], slot, hd)
+                scores = nt_dot(query, take[own, 1, :].astype(LOW)) * scale
+                weights = jnp.exp(scores - jnp.max(scores, axis=-1, keepdims=True))
+                probs = weights / jnp.sum(weights, axis=-1, keepdims=True)
+                mix[own, :] = nn_dot(probs.astype(LOW), take[own, 2, :].astype(LOW))
+            for j in range(span):
+                back[pl.ds(slot * length + order[base + j], 1), :] = mix[pl.ds(j, 1), :]
+
+    lane = lane_of(step)
+
+    @pl.when(count[0] == 2)
+    def _():
+        @pl.loop(0, length // step)
+        def _(i):
+            at = pl.multiple_of(i * step, step)
+            nat[i] = jnp.where(
+                lane < hd, back[pl.ds(at, step), :], back[pl.ds(length + at, step), :]
+            ).astype(LOW)
+
+    half = step // 2
+
+    @pl.when(count[0] == 1)
+    def _():
+        @pl.loop(0, length // step)
+        def _(i):
+            at = pl.multiple_of(i * step, step)
+            upper = pltpu.roll(back[pl.ds(at + half, half), :], hd, 1)
+            pack[i] = jnp.where(lane[:half] < hd, back[pl.ds(at, half), :], upper).astype(LOW)
+
+
+def attend(order, count, hid, weight, bias, blks, hd, scale):
+    length = hid.shape[0]
+    step = length // blks
+    return pl.pallas_call(
+        functools.partial(attend_kernel, hd, scale),
+        name="attend",
+        out_shape=(
+            jax.ShapeDtypeStruct((length, 384), LOW),
+            jax.ShapeDtypeStruct((blks, step, 128), LOW),
+            jax.ShapeDtypeStruct((blks, step // 2, 128), LOW),
+        ),
+        in_specs=[spec(pltpu.SMEM), spec(pltpu.SMEM)] + [spec(pltpu.VMEM)] * 3,
+        out_specs=(spec(pltpu.VMEM),) * 3,
+        scratch_shapes=[
+            pltpu.VMEM((length, 4, 128), F32),
+            pltpu.VMEM((GROUP * 128, 4, 128), F32),
+            pltpu.VMEM((GROUP * 128, 128), F32),
+            pltpu.VMEM((2 * length, 128), F32),
+        ],
+        compiler_params=pltpu.CompilerParams(vmem_limit_bytes=BIG),
+        cost_estimate=pl.CostEstimate(
+            flops=5 * 10**9, transcendentals=0, bytes_accessed=100 * 10**6
+        ),
+    )(order, count, hid, weight, bias)
+
+
+def attend_back_kernel(
+    hd, scale, order, count, proj, gnat, gpack, znat, zpack, sums, rows4, take, out4, back4
+):
+    length = proj.shape[0]
+    step = gnat.shape[1]
+    half = step // 2
+
+    @pl.loop(0, length // step)
+    def _(i):
+        at = pl.multiple_of(i * step, step)
+        wide = proj[pl.ds(at, step), :].astype(F32)
+        for t in range(3):
+            rows4[pl.ds(at, step), t, :] = wide[:, t * 128 : (t + 1) * 128]
+
+        @pl.when(count[0] == 2)
+        def _():
+            rows4[pl.ds(at, step), 3, :] = gnat[i].astype(F32)
+
+        @pl.when(count[0] == 1)
+        def _():
+            pair = gpack[i].astype(F32)
+            rows4[pl.ds(at, half), 3, :] = pair
+            rows4[pl.ds(at + half, half), 3, :] = pltpu.roll(pair, hd, 1)
+
+    span = GROUP * 128
+
+    @pl.loop(0, count[0])
+    def _(slot):
+        @pl.loop(0, length // span)
+        def _(i):
+            base = slot * length + i * span
+            for j in range(span):
+                take[j] = rows4[order[base + j]]
+            for u in range(GROUP):
+                own = pl.ds(u * 128, 128)
+                query = low_lanes(take[own, 0, :], slot, hd)
+                grad = low_lanes(take[own, 3, :], slot, hd)
+                keys = take[own, 1, :].astype(LOW)
+                scores = nt_dot(query, keys) * scale
+                weights = jnp.exp(scores - jnp.max(scores, axis=-1, keepdims=True))
+                probs = weights / jnp.sum(weights, axis=-1, keepdims=True)
+                prob_grad = nt_dot(grad, take[own, 2, :].astype(LOW))
+                shift = jnp.sum(probs * prob_grad, axis=-1, keepdims=True)
+                score_low = (probs * (prob_grad - shift)).astype(LOW)
+                out4[own, 0, :] = nn_dot(score_low, keys) * scale
+                out4[own, 1, :] = tn_dot(score_low, query) * scale
+                out4[own, 2, :] = tn_dot(probs.astype(LOW), grad)
+            for j in range(span):
+                back4[slot * length + order[base + j]] = out4[j]
+
+    lane = lane_of(step)
+    sums[...] = jnp.zeros_like(sums)
+
+    @pl.loop(0, length // step)
+    def _(i):
+        at = pl.multiple_of(i * step, step)
+        for t in range(3):
+            cols = pl.ds(t * 128, 128)
+            first = back4[pl.ds(at, step), t, :]
+
+            @pl.when(count[0] == 2)
+            def _():
+                both = jnp.where(lane < hd, first, back4[pl.ds(length + at, step), t, :])
+                low = both.astype(LOW)
+                znat[i, :, cols] = low
+                sums[0:1, cols] += jnp.sum(low.astype(F32), axis=0, keepdims=True)
+
+            @pl.when(count[0] == 1)
+            def _():
+                low = jnp.where(lane < hd, first, 0.0).astype(LOW)
+                znat[i, :, cols] = low
+                wide = low.astype(F32)
+                zpack[i, :, cols] = (wide[:half] + pltpu.roll(wide[half:], hd, 1)).astype(LOW)
+                sums[0:1, cols] += jnp.sum(wide, axis=0, keepdims=True)
+
+
+def attend_back(order, count, proj, gnat, gpack, hd, scale):
+    length = proj.shape[0]
+    blks, step, _ = gnat.shape
+    return pl.pallas_call(
+        functools.partial(attend_back_kernel, hd, scale),
+        name="attend_back",
+        out_shape=(
+            jax.ShapeDtypeStruct((blks, step, 384), LOW),
+            jax.ShapeDtypeStruct((blks, step // 2, 384), LOW),
+            jax.ShapeDtypeStruct((8, 384), F32),
+        ),
+        in_specs=[spec(pltpu.SMEM), spec(pltpu.SMEM)] + [spec(pltpu.VMEM)] * 3,
+        out_specs=(spec(pltpu.VMEM),) * 3,
+        scratch_shapes=[
+            pltpu.VMEM((length, 4, 128), F32),
+            pltpu.VMEM((GROUP * 128, 4, 128), F32),
+            pltpu.VMEM((GROUP * 128, 4, 128), F32),
+            pltpu.VMEM((2 * length, 4, 128), F32),
+        ],
+        compiler_params=pltpu.CompilerParams(vmem_limit_bytes=BIG),
+        cost_estimate=pl.CostEstimate(
+            flops=8 * 10**9, transcendentals=0, bytes_accessed=120 * 10**6
+        ),
+    )(order, count, proj, gnat, gpack)
+
+
+def join_columns(even, odd, hd):
+    rows = even.shape[1]
+    first = even.transpose(1, 0, 2).reshape(rows, -1)
+    spread = jnp.concatenate([odd[:, :, :hd], odd[:, :, hd:]], axis=1)
+    return jnp.concatenate([first, spread.transpose(1, 0, 2).reshape(rows, -1)], axis=1)
+
+
+def split_columns(value, chips, hd):
+    rows = value.shape[0]
+    wide = chips * 2 * hd
+    even = value[:, :wide].reshape(rows, chips, 2 * hd).transpose(1, 0, 2)
+    odd = value[:, wide:].reshape(rows, chips, hd).transpose(1, 0, 2)
+    return even, jnp.concatenate([odd[:, : rows // 2], odd[:, rows // 2 :]], axis=2)
+
+
+def by_device(value, chips, hd):
+    rows = value.shape[0]
+    wide = chips * 2 * hd
+    even = value[:, :wide].reshape(rows, chips, 2 * hd).transpose(1, 0, 2)
+    odd = value[:, wide:].reshape(rows, chips, hd).transpose(1, 0, 2)
+    odd = jnp.pad(odd, ((0, 0), (0, 0), (0, hd)))
+    return jnp.stack([even, odd], axis=1).reshape(2 * chips, rows, 2 * hd)
+
+
+def from_device(value, chips, hd):
+    rows = value.shape[1]
+    pairs = value.reshape(chips, 2, rows, 2 * hd)
+    even = pairs[:, 0].transpose(1, 0, 2).reshape(rows, -1)
+    odd = pairs[:, 1, :, :hd].transpose(1, 0, 2).reshape(rows, -1)
+    return jnp.concatenate([even, odd], axis=1)
+
+
+def fast_body(seqs, blks, heads):
+    def run(
+        hidden_in, query_weight, key_weight, value_weight, output_weight, inner_weight,
+        outer_weight, query_bias, value_bias, output_bias, attention_gain, attention_shift,
+        inner_bias, outer_bias, final_gain, final_shift, cotangent, grad_mask, cluster_order,
+    ):
+        rows, width = hidden_in.shape
+        own = query_weight.shape[0]
+        hidden_units = inner_weight.shape[1]
+        length = cluster_order.shape[2]
+        hd = width // heads
+        chips = blks // 2
+        scale = 1.0 / math.sqrt(hd)
+        devices = seqs * blks
+        b = lax.axis_index("blk")
+        k = b // 2
+        even_core = lax.rem(b, 2) == 0
+        query_low, key_low, value_low, output_low, inner_low_w, outer_low_w = [
+            w.astype(LOW)
+            for w in (
+                query_weight, key_weight, value_weight, output_weight, inner_weight, outer_weight,
+            )
+        ]
+        small = jnp.concatenate(
+            [
+                query_bias, value_bias, output_bias, attention_gain, attention_shift,
+                outer_bias, final_gain, final_shift, inner_bias,
+            ]
+        ).astype(LOW)
+        slabs = jnp.concatenate(
+            [by_device(w, chips, hd) for w in (query_low, key_low, value_low)], axis=2
+        )
+        extra = jnp.pad(small[None, :], ((0, 7), (0, 384 - small.shape[0])))
+        slabs = jnp.concatenate(
+            [slabs, jnp.broadcast_to(extra[None], (blks,) + extra.shape)], axis=1
+        )
+        axes = ("seq", "blk")
+        first_half = lax.all_gather(
+            jnp.concatenate([output_low, inner_low_w], axis=1), axes, axis=0, tiled=True
+        )
+        outer_full = lax.all_gather(outer_low_w, axes, axis=0, tiled=True)
+        projections = lax.all_gather(
+            jnp.concatenate([query_low, key_low, value_low], axis=1), axes, axis=0, tiled=True
+        )
+        hidden_all, gathered = entry(hidden_in, slabs, seqs, blks, 2)
+        hidden_all = hidden_all.reshape(length, width)
+        gathered = gathered.reshape(devices, own + 8, 384)
+        weight_own = gathered[:, :own].reshape(width, 384)
+        vec = gathered[:, own, : small.shape[0]]
+        vecs = (
+            vec[:, : 8 * own].reshape(devices, 8, own).transpose(1, 0, 2).reshape(8, width)
+        ).astype(F32)
+        bias_inner = vec[:, 8 * own :].reshape(1, hidden_units).astype(F32)
+        bias_query, bias_value = [
+            by_device(vecs[i : i + 1], chips, hd) for i in (0, 1)
+        ]
+        bias_output, gain_first, shift_first, bias_outer, gain_final, shift_final = [
+            vecs[i] for i in range(2, 8)
+        ]
+        bias_own = lax.dynamic_index_in_dim(
+            jnp.concatenate([bias_query, jnp.zeros_like(bias_query), bias_value], axis=2),
+            b, 0, keepdims=False,
+        )
+        order = cluster_order[0]
+        head_first = jnp.where(even_core, 2 * k, 2 * chips + k)
+        order_own = jnp.concatenate(
+            [
+                lax.dynamic_index_in_dim(order, head_first, 0, keepdims=False),
+                lax.dynamic_index_in_dim(order, 2 * k + 1, 0, keepdims=False),
+            ]
+        )
+        count = jnp.where(even_core, 2, 1).astype(jnp.int32).reshape(1)
+        proj, cnat, cpack = attend(
+            order_own, count, hidden_all, weight_own, bias_own, blks, hd, scale
+        )
+        ceven, codd = return_rows(cnat, cpack, 1)
+        context_low = join_columns(ceven, codd, hd)
+
+        output_full = first_half[:, :width]
+        inner_full = first_half[:, width:]
+        hidden = hidden_in.astype(F32)
+        attention_out = nn_dot(context_low, output_full) + bias_output
+        first_norm, first_pull = jax.vjp(layer_norm, hidden + attention_out, gain_first, shift_first)
+        first_low = first_norm.astype(LOW)
+        inner_pre = nn_dot(first_low, inner_full) + bias_inner
+        activated, gelu_pull = jax.vjp(exact_gelu, inner_pre)
+        activated_low = activated.astype(LOW)
+        outer_out = nn_dot(activated_low, outer_full) + bias_outer
+        final_norm, final_pull = jax.vjp(layer_norm, first_norm + outer_out, gain_final, shift_final)
+        hidden_out = final_norm.astype(LOW)
+        out_grad = cotangent.astype(F32) * grad_mask.astype(F32)
+        second_grad, grad_final_gain, grad_final_shift = final_pull(out_grad)
+        outer_low = second_grad.astype(LOW)
+        grad_outer_weight = tn_dot(activated_low, outer_low)
+        grad_outer_bias = column_sum(outer_low)
+        inner_low = gelu_pull(nt_dot(outer_low, outer_full))[0].astype(LOW)
+        grad_inner_weight = tn_dot(first_low, inner_low)
+        grad_inner_bias = column_sum(inner_low)
+        first_grad = nt_dot(inner_low, inner_full) + second_grad
+        residual_grad, grad_attention_gain, grad_attention_shift = first_pull(first_grad)
+        attn_low = residual_grad.astype(LOW)
+        grad_output_weight = tn_dot(context_low, attn_low)
+        grad_output_bias = column_sum(attn_low)
+        context_grad = nt_dot(attn_low, output_full).astype(LOW)
+
+        vec_grads = jnp.stack(
+            [
+                grad_output_bias, grad_attention_gain, grad_attention_shift,
+                grad_outer_bias, grad_final_gain, grad_final_shift,
+            ]
+        )
+        vec_grads = vec_grads.reshape(6, devices, own).transpose(1, 0, 2).reshape(devices, 6 * own)
+        vec_grads = jnp.concatenate(
+            [vec_grads, grad_inner_bias.reshape(devices, hidden_units // devices)], axis=1
+        )
+        vec_grads = jnp.pad(vec_grads, ((0, 0), (0, width - vec_grads.shape[1])))
+        merged = jnp.concatenate(
+            [
+                grad_outer_weight.reshape(devices, hidden_units // devices, width).astype(LOW),
+                grad_inner_weight.reshape(devices, own, hidden_units // width, width)
+                .transpose(0, 2, 1, 3)
+                .reshape(devices, -1, width)
+                .astype(LOW),
+                grad_output_weight.reshape(devices, own, width).astype(LOW),
+                jnp.pad(vec_grads[:, None, :].astype(LOW), ((0, 0), (0, 7), (0, 0))),
+            ],
+            axis=1,
+        )
+        share = lax.psum_scatter(
+            merged.reshape(-1, width), axes, scatter_dimension=0, tiled=True
+        ).astype(F32)
+
+        geven, godd = split_columns(context_grad, chips, hd)
+        gnat, gpack = spread_rows(geven, godd, 2)
+        znat, zpack, sums = attend_back(order_own, count, proj, gnat, gpack, hd, scale)
+        own_grads = tn_dot(hidden_all, znat.reshape(length, 384)).reshape(seqs, blks, own, 384)
+        grads = jnp.concatenate(
+            [own_grads, jnp.broadcast_to(sums, (seqs, blks, 8, 384))], axis=2
+        ).astype(LOW)
+        zeven, zodd, proj_grads = leave(znat, zpack, grads)
+        triple = jnp.concatenate(
+            [
+                join_columns(zeven[:, :, i * 128 : (i + 1) * 128], zodd[:, :, i * 128 : (i + 1) * 128], hd)
+                for i in range(3)
+            ],
+            axis=1,
+        )
+        input_grad = nt_dot(triple, projections) + residual_grad
+        grad_query_weight, grad_key_weight, grad_value_weight = [
+            from_device(proj_grads[:, :, i * 128 : (i + 1) * 128].astype(F32), chips, hd)
+            for i in range(3)
+        ]
+        me = lax.axis_index("seq") * blks + b
+        grad_query_bias = lax.dynamic_slice_in_dim(grad_query_weight[own], me * own, own)
+        grad_value_bias = lax.dynamic_slice_in_dim(grad_value_weight[own], me * own, own)
+        share_outer = share[: hidden_units // devices]
+        at = hidden_units // devices
+        tail = at + own * (hidden_units // width)
+        share_inner = (
+            share[at:tail]
+            .reshape(hidden_units // width, own, width)
+            .transpose(1, 0, 2)
+            .reshape(own, hidden_units)
+        )
+        share_output = share[tail : tail + own]
+        vec_own = share[tail + own]
+        vec_parts = [vec_own[i * own : (i + 1) * own] for i in range(6)]
+        return (
+            hidden_out,
+            input_grad,
+            grad_query_weight[:own],
+            grad_key_weight[:own],
+            grad_value_weight[:own],
+            share_output,
+            share_inner,
+            share_outer,
+            grad_query_bias,
+            grad_value_bias,
+            vec_parts[0],
+            vec_parts[1],
+            vec_parts[2],
+            vec_own[6 * own : 6 * own + hidden_units // devices],
+            vec_parts[3],
+            vec_parts[4],
+            vec_parts[5],
+        )
+
+    return run
 
 
 def masked_scores(left, right, left_ids, right_ids, scale):
@@ -277,8 +1083,11 @@
         P(("seq", "blk"), None),
         P("seq", None, None),
     )
+    seqs, blks = mesh.shape["seq"], mesh.shape["blk"]
+    heads = 12
+    fast = blks % 2 == 0 and 3 * blks == 2 * heads
     return jax.shard_map(
-        body,
+        fast_body(seqs, blks, heads) if fast else body,
         mesh=mesh,
         in_specs=placed,
         out_specs=(

time: 1870 us -> 505 us (0.27)
  waiting for transfers between devices: 926 us -> 0.09 us
  matrix products: 387 us -> 67 us
  Pallas kernels: 0 us -> 320 us
  local copies, waits for them, and re-layouts: 273 us -> 61.6 us
  other arithmetic: 128 us -> 32.5 us
  blocking collectives: 78.9 us -> 0 us
  loops' own time: 48.2 us -> 0 us
    reduce_scatter x5 -> x1, waiting for transfers between devices: 608 us -> 0.01 us  [run(): lax.psum_scatter(merged.reshape(-1, width), axes, scatter_dimension=0, ti...]
    dot_general x102 -> x11, matrix products: 387 us -> 67 us  [the longest x3 26.9 us: nn_dot(): return jnp.dot(left, right, preferred_element_type=F32)]
    pallas_call x0 -> x6, Pallas kernels: none -> 320 us  [the longest x1 101 us: leave(): pl.pallas_call(functools.partial(exit_kernel, seqs, blks), name='leave',...]
    unnamed x19 -> x4, waiting for transfers between devices: 249 us -> 0.07 us
    unnamed x102 -> x46, local copies, waits for them, and re-layouts: 199 us -> 8.26 us
    convert_element_type x36 -> x10, other arithmetic: 102 us -> 7.38 us  [the longest x6 6.18 us: run(): w.astype(LOW)]
    unnamed x2 -> x0, blocking collectives: 78.9 us -> none
    all_gather x8 -> x3, waiting for transfers between devices: 68.9 us -> 0.02 us  [the longest x1 0.02 us: run(): lax.all_gather(jnp.concatenate([output_low, inner_low_w], axis=1), axes,...]
  transfers between devices with their start and end apart: 16 -> 4, of which waited for: 11 -> 0; matrix products, arithmetic and copies ran while one was open for 22% -> 30% of each run, Pallas kernels for 0% -> 64%
where the time goes in v1:
time: 505 us; the launch traced here: 496 us
  Pallas kernels  320 us (63%)
  matrix products  67 us (13%)
  local copies, waits for them, and re-layouts  61.6 us (12%)
  other arithmetic  32.5 us (6%)
  between operations  15 us (3%)
    pallas_call x1, Pallas kernels, leave(): pl.pallas_call(functools.partial(exit_kernel, seqs, blks), name='leave',...  101 us
    pallas_call x1, Pallas kernels, entry(): pl.pallas_call(functools.partial(entry_kernel, seqs, blks, parts), name='...  85.6 us
    pallas_call x1, Pallas kernels, return_rows(): pl.pallas_call(functools.partial(return_kernel, blks), name='return_rows'...  43.4 us
    pallas_call x1, Pallas kernels, attend_back(): pl.pallas_call(functools.partial(attend_back_kernel, hd, scale), name='at...  39.3 us
    pallas_call x1, Pallas kernels, attend(): pl.pallas_call(functools.partial(attend_kernel, hd, scale), name='attend'...  30.7 us
    dot_general x3, matrix products, nn_dot(): return jnp.dot(left, right, preferred_element_type=F32)  26.9 us
    dot_general x4, matrix products, nt_dot(): lax.dot_general(left, right, (((1,), (1,)), ((), ())), preferred_element_...  22.6 us
    pallas_call x1, Pallas kernels, spread_rows(): pl.pallas_call(functools.partial(spread_kernel, blks), name='spread_rows'...  19.8 us
  transfers between devices with their start and end apart: 4, of which 0 were waited for; matrix products, arithmetic and copies ran while one was open for 30% of the time, Pallas kernels for 64%

profile of v1, /device:TPU:9, one launch (start us, length us, event | category | flops | bytes accessed | tf_op | source)
XLA Modules:
  0.0 496.4 jit_solution(282919704408337046)
XLA Ops:
  9.9 1.6 convert_element_type.150
  19.6 85.6 %entry.1 = (bf16[8,2,256,768]{3,2,1,0:T(8,128)(2,1)}, bf16[4,8,32,384]{3,2,1,0:T(8,128)(2,1)}) custom-call(bf16[2,256,768]{2,1,0:T(8,128)(2,1)} %bitcast.233, bf16[8,32,384]{2,1,0:T(8,128)(2,1)} %pad_maximum_fusion.5.w_ref), custom_call_target="tpu_custom_call" | custom-call | bytes 200000000 | tf_op jit(solution)/shard_map/entry/pallas_call | solution.py:191
  106.3 1.9 slice.307
  111.3 30.7 %attend.1 = (bf16[4096,384]{1,0:T(8,128)(2,1)}, bf16[8,512,128]{2,1,0:T(8,128)(2,1)}, bf16[8,256,128]{2,1,0:T(8,128)(2,1)}) custom-call(s32[8192]{0:T(1024)} %pad_add_fusion.order, s32[1]{0:T(128)} %bitcast.2.count, bf16[4096,768]{1,0:T(8,128)(2,1)} %bitcast.214, bf16[768,384]{1,0:T(8,128)(2,1)} %bitcast.234, f32[1,384]{1,0:T(1,128)} %fusion.26.bias), custom_call_target="tpu_custom_call" | custom-call | flops 5000000000 | bytes 100000000 | tf_op jit(solution)/shard_map/attend/pallas_call | solution.py:507
  141.9 43.4 %return_rows.1 = (bf16[4,512,128]{2,1,0:T(8,128)(2,1)}, bf16[4,256,128]{2,1,0:T(8,128)(2,1)}) custom-call(bf16[8,512,128]{2,1,0:T(8,128)(2,1)} %get-tuple-element.34.nat_ref, bf16[8,256,128]{2,1,0:T(8,128)(2,1)} %get-tuple-element.35.pack_ref), custom_call_target="tpu_custom_call" | custom-call | bytes 80000000 | tf_op jit(solution)/shard_map/return_rows/pallas_call | solution.py:274
  187.5 2.4 fusion.44
  190.6 18.3 %multiply_convert_fusion = (bf16[512,3072]{1,0:T(8,128)(2,1)}, f32[512,3072]{1,0:T(8,128)}, f32[512,3072]{1,0:T(8,128)}) fusion(f32[3072]{0:T(1024)S(1)} %reshape.472, bf16[768,3840]{1,0:T(8,128)(2,1)S(1)} %copy-done.11, f32[512,768]{1,0:T(8,128)S(1)} %get-tuple-element.103, f32[768]{0:T(1024)S(1)} %add.135, f32[768]{0:T(1024)S(1)} %mul.158, ...), kind=kOutput, calls=%fused_computation.6 | convolution fusion | flops 2521694208 | bytes 22044672 | tf_op jit(solution)/shard_map/dot_general | solution.py:33
  208.9 6.2 %fusion.45 = (f32[512]{0:T(512)S(1)}, f32[512,768]{1,0:T(8,128)S(1)}) fusion(f32[768]{0:T(1024)S(1)} %add.140, bf16[512,3072]{1,0:T(8,128)(2,1)} %get-tuple-element.71, bf16[3072,768]{1,0:T(8,128)(2,1)} %all-gather.6.cloned.1.call-done, f32[768]{0:T(1024)S(1)} %add.135, f32[768]{0:T(1024)S(1)} %mul.158, f32[512]{0:T(512)S(1)} %fusion.22, ...), kind=kOutput, calls=%fused_computation.173 | convolution fusion | flops 2418671104 | bytes 11025408 | tf_op jit(solution)/shard_map/dot_general | solution.py:33
  216.3 1.7 fusion.37
  218.3 2.4 copy-done.13
  220.6 8.2 %fusion.35 = (bf16[3072]{0:T(1024)(128)(2,1)S(1)}, bf16[512,3072]{1,0:T(8,128)(2,1)}) fusion(f32[512,3072]{1,0:T(8,128)S(1)} %copy-done.13, f32[512,3072]{1,0:T(8,128)} %get-tuple-element.104, f32[3072]{0:T(1024)S(1)} %reshape.472, bf16[512,768]{1,0:T(8,128)(2,1)S(1)} %get-tuple-element.62, bf16[3072,768]{1,0:T(8,128)(2,1)S(1)} %bitcast.263), kind=kOutput, calls=%fused_computation.164 | convolution fusion | flops 2441081856 | bytes 21252096 | tf_op jit(solution)/shard_map/dot_general | solution.py:25
  228.9 6.4 %multiply_reduce_fusion.1 = (bf16[768]{0:T(1024)(128)(2,1)S(1)}, f32[512]{0:T(512)S(1)}, bf16[768]{0:T(1024)(128)(2,1)S(1)}, f32[512,768]{1,0:T(8,128)S(1)}) fusion(f32[512,768]{1,0:T(8,128)S(1)} %get-tuple-element.103, f32[512]{0:T(512)S(1)} %fusion.22, f32[512]{0:T(512)S(1)} %broadcast_multiply_fusion.1, f32[768]{0:T(1024)S(1)} %mul.158, ...), kind=kOutput, calls=%fused_computation.29 | convolution fusion | flops 2419849216 | bytes 12597248 | tf_op jit(solution)/shard_map/dot_general | solution.py:25
  238.1 6.5 %convolution_convert_fusion = bf16[768,3072]{1,0:T(8,128)(2,1)} fusion(bf16[512,3072]{1,0:T(8,128)(2,1)} %get-tuple-element.66, f32[512,768]{1,0:T(8,128)S(1)} %get-tuple-element.103, f32[768]{0:T(1024)S(1)} %add.135, f32[768]{0:T(1024)S(1)} %mul.158, f32[512]{0:T(512)S(1)} %fusion.22, f32[512]{0:T(512)S(1)} %broadcast_multiply_fusion.1), kind=kOutput, calls=%fused_computation.20 | convolution fusion | flops 2420244480 | bytes 9447424 | tf_op jit(solution)/shard_map/dot_general | solution.py:29
  244.6 9.7 %convert_element_type.161 = bf16[32,24,4,768]{3,2,1,0:T(4,128)(2,1)} reshape(bf16[768,3072]{1,0:T(8,128)(2,1)} %convolution_convert_fusion) | data formatting | bytes 9437184 | tf_op jit(solution)/shard_map/convert_element_type | solution.py:786
  254.3 3.4 copy.149
  258.9 2.9 convolution_convert_fusion.1
  261.8 5.3 %fusion.1 = bf16[32,224,768]{2,1,0:T(8,128)(2,1)} fusion(bf16[32,1,768]{2,1,0:T(2,128)(2,1)S(1)} %copy.156, bf16[32,24,768]{2,1,0:T(8,128)(2,1)S(1)} %bitcast.226, bf16[32,96,768]{2,1,0:T(8,128)(2,1)S(1)} %bitcast.213, bf16[32,96,768]{2,1,0:T(8,128)(2,1)S(1)} %bitcast.217), kind=kLoop, calls=%fused_computation.2 | loop fusion | flops 55050240 | bytes 21676032 | tf_op jit(solution)/shard_map/concatenate | solution.py:780
  267.1 8.7 %copy.136 = bf16[768,4096]{1,0:T(8,128)(2,1)} copy(bf16[768,4096]{0,1:T(8,128)(2,1)} %bitcast.215) | data formatting | bytes 12582912 | tf_op jit(solution)/shard_map/dot_general | solution.py:29
  275.9 2.1 convolution_convert_fusion.3
  280.6 19.8 %spread_rows.1 = (bf16[8,512,128]{2,1,0:T(8,128)(2,1)}, bf16[8,256,128]{2,1,0:T(8,128)(2,1)}) custom-call(bf16[4,512,128]{2,1,0:T(8,128)(2,1)} %bitcast.222, bf16[4,256,128]{2,1,0:T(8,128)(2,1)} %pad_maximum_fusion.4.odd_ref), custom_call_target="tpu_custom_call" | custom-call | bytes 80000000 | tf_op jit(solution)/shard_map/spread_rows/pallas_call | solution.py:355
  300.4 39.3 %attend_back.1 = (bf16[8,512,384]{2,1,0:T(8,128)(2,1)}, bf16[8,256,384]{2,1,0:T(8,128)(2,1)}, f32[8,384]{1,0:T(8,128)}) custom-call(s32[8192]{0:T(1024)} %pad_add_fusion.order, s32[1]{0:T(128)} %bitcast.2.count, bf16[4096,384]{1,0:T(8,128)(2,1)} %get-tuple-element.38.proj, bf16[8,512,128]{2,1,0:T(8,128)(2,1)} %get-tuple-element.39.gnat, ...), custom_call_target="tpu_custom_call" | custom-call | flops 8000000000 | bytes 120000000 | tf_op jit(solution)/shard_map/attend_back/pallas_call | solution.py:609
  340.5 7.2 %convolution_convert_fusion.4 = bf16[4,8,24,384]{3,2,1,0:T(8,128)(2,1)S(1)} fusion(bf16[4,8,24,4096]{3,2,1,0:T(8,128)(2,1)} %bitcast.216, bf16[4096,384,1,1]{1,0,3,2:T(8,128)(2,1)} %bitcast.218), kind=kOutput, calls=%fused_computation.45 | convolution fusion | flops 2416214016 | bytes 10027008 | tf_op jit(solution)/shard_map/dot_general | solution.py:29
  348.7 101.4 %leave.1 = (bf16[4,512,384]{2,1,0:T(8,128)(2,1)}, bf16[4,256,384]{2,1,0:T(8,128)(2,1)}, bf16[8,32,384]{2,1,0:T(8,128)(2,1)}) custom-call(bf16[8,512,384]{2,1,0:T(8,128)(2,1)} %get-tuple-element.41.nat_ref, bf16[8,256,384]{2,1,0:T(8,128)(2,1)} %get-tuple-element.42.pack_ref, bf16[4,8,32,384]{3,2,1,0:T(8,128)(2,1)} %pad_maximum_fusion.1.grad_ref), custom_call_target="tpu_custom_call" | custom-call | bytes 200000000 | tf_op jit(solution)/shard_map/leave/pallas_call | solution.py:416
  450.1 1.6 fusion.43
  453.4 2.4 slice_bitcast_fusion
  462.3 1.9 maximum_bitcast_fusion.3
  464.2 1.9 copy.142
  467.7 1.6 reshape.462
  474.2 1.7 constant_dynamic-update-slice_fusion.2
  477.4 5.9 %add_add_fusion.4 = f32[512,768]{1,0:T(8,128)} fusion(f32[512,768]{1,0:T(8,128)S(1)} %get-tuple-element.68, bf16[512,2304]{0,1:T(8,128)(2,1)} %constant_dynamic-update-slice_fusion, bf16[768,2304]{1,0:T(8,128)(2,1)} %all-gather.8.cloned.1.call-done, f32[512]{0:T(512)S(1)} %negate_multiply_fusion.1), kind=kOutput, calls=%fused_computation.40 | convolution fusion | flops 1812725760 | bytes 9046016 | tf_op jit(solution)/shard_map/dot_general | solution.py:25
  485.6 1.7 fusion.41
  488.1 1.4 slice.335
  (193 shorter events, 46.0 us)
Async XLA Ops:
  7.2 180.3 %all-gather.4.cloned.1.call-start = ((), (), s32[]{:S(2)}) async-start(), calls=%async_computation.1 | async-start | bytes 6082560 | tf_op jit(solution)/shard_map/all_gather | solution.py:701
  9.8 199.1 %all-gather.6.cloned.1.call-start = ((), (), s32[]{:S(2)}) async-start(), calls=%async_computation.2 | async-start | bytes 4866048 | tf_op jit(solution)/shard_map/all_gather | solution.py:704
  11.5 465.9 %all-gather.8.cloned.1.call-start = ((), (), s32[]{:S(2)}) async-start(), calls=%async_computation.3 | async-start | bytes 3649536 | tf_op jit(solution)/shard_map/all_gather | solution.py:705
  14.9 468.4 %reduce-scatter.2.cloned.1.call-start = ((), (), s32[]{:S(2)}) async-start(), calls=%async_computation.4 | async-start | bytes 11354112 | tf_op jit(solution)/shard_map/reduce_scatter | solution.py:792
  141.9 45.5 %copy-start.4 = (bf16[512,768]{1,0:T(8,128)(2,1)S(1)}, bf16[512,768]{1,0:T(8,128)(2,1)}, u32[]{:S(2)}) copy-start(bf16[512,768]{1,0:T(8,128)(2,1)} %param.19) | copy-start | bytes 2359300
  185.3 1.6 copy-start.10
  187.1 3.1 copy-start.8
  187.5 3.1 copy-start.11
  208.9 6.6 %copy-start = (s32[512,768]{1,0:T(8,128)S(1)}, s32[512,768]{1,0:T(8,128)}, u32[]{:S(2)}) copy-start(s32[512,768]{1,0:T(8,128)} %param.36) | copy-start | bytes 4718596
  208.9 6.6 %copy-start.1 = (bf16[512,768]{1,0:T(8,128)(2,1)S(1)}, bf16[512,768]{1,0:T(8,128)(2,1)}, u32[]{:S(2)}) copy-start(bf16[512,768]{1,0:T(8,128)(2,1)} %param.35) | copy-start | bytes 2359300
  215.5 2.8 slice-start
  216.3 2.0 slice-start.1
  216.3 4.3 copy-start.13
  218.2 10.6 %copy-start.6 = (bf16[512,768]{1,0:T(8,128)(2,1)}, bf16[512,768]{1,0:T(8,128)(2,1)S(1)}, u32[]{:S(2)}) copy-start(bf16[512,768]{1,0:T(8,128)(2,1)S(1)} %get-tuple-element.62) | copy-start | bytes 2359300
  254.3 3.4 copy-start.5
  254.3 3.4 copy-start.9
  254.3 4.2 copy-start.12
  257.7 1.2 copy-start.7
  450.1 7.0 %copy-start.2 = (bf16[4,256,384]{2,1,0:T(8,128)(2,1)S(1)}, bf16[4,256,384]{2,1,0:T(8,128)(2,1)}, u32[]{:S(2)}) copy-start(bf16[4,256,384]{2,1,0:T(8,128)(2,1)} %get-tuple-element.45) | copy-start | bytes 2359300
  469.2 7.5 %copy-start.3 = (bf16[512,4,64]{0,2,1:T(8,128)(2,1)S(1)}, bf16[512,4,64]{0,2,1:T(8,128)(2,1)}, u32[]{:S(2)}) copy-start(bf16[512,4,64]{0,2,1:T(8,128)(2,1)} %copy.142) | copy-start | bytes 786436
Sparse Core Ops, SparseCore 0:
  11.6 77.8 all-gather.3
  92.5 65.8 all-gather.5
  161.4 61.1 all-gather.7
  267.3 173.9 reduce-scatter.1

commit v2 on v1

--- a/solution.py
+++ b/solution.py
@@ -528,11 +528,14 @@
 
 
 def attend_back_kernel(
-    hd, scale, order, count, proj, gnat, gpack, znat, zpack, sums, rows4, take, out4, back4
+    hd, scale, order, count, hidden_hbm, proj, gnat, gpack, extra, znat, zpack, slabs,
+    rows4, take, out4, back4, hid, wide_grad, sem,
 ):
     length = proj.shape[0]
     step = gnat.shape[1]
     half = step // 2
+    fetch = pltpu.make_async_copy(hidden_hbm, hid, sem)
+    fetch.start()
 
     @pl.loop(0, length // step)
     def _(i):
@@ -578,70 +581,398 @@
                 back4[slot * length + order[base + j]] = out4[j]
 
     lane = lane_of(step)
-    sums[...] = jnp.zeros_like(sums)
-
-    @pl.loop(0, length // step)
-    def _(i):
+    fetch.wait()
+    wide_grad[...] = jnp.zeros_like(wide_grad)
+    zero = jnp.zeros((1, 384), F32)
+
+    def settle(i, sums):
         at = pl.multiple_of(i * step, step)
+        parts = []
         for t in range(3):
             cols = pl.ds(t * 128, 128)
             first = back4[pl.ds(at, step), t, :]
-
-            @pl.when(count[0] == 2)
-            def _():
-                both = jnp.where(lane < hd, first, back4[pl.ds(length + at, step), t, :])
-                low = both.astype(LOW)
-                znat[i, :, cols] = low
-                sums[0:1, cols] += jnp.sum(low.astype(F32), axis=0, keepdims=True)
-
-            @pl.when(count[0] == 1)
-            def _():
-                low = jnp.where(lane < hd, first, 0.0).astype(LOW)
-                znat[i, :, cols] = low
-                wide = low.astype(F32)
-                zpack[i, :, cols] = (wide[:half] + pltpu.roll(wide[half:], hd, 1)).astype(LOW)
-                sums[0:1, cols] += jnp.sum(wide, axis=0, keepdims=True)
-
-
-def attend_back(order, count, proj, gnat, gpack, hd, scale):
+            second = back4[pl.ds(length + at, step), t, :]
+            second = jnp.where(count[0] == 2, second, jnp.zeros_like(second))
+            low = jnp.where(lane < hd, first, second).astype(LOW)
+            znat[i, :, cols] = low
+            wide = low.astype(F32)
+            parts.append(jnp.sum(wide, axis=0, keepdims=True))
+            zpack[i, :, cols] = (wide[:half] + pltpu.roll(wide[half:], hd, 1)).astype(LOW)
+        wide_grad[...] += tn_dot(hid[pl.ds(at, step), :], znat[i])
+        return sums + jnp.concatenate(parts, axis=1)
+
+    sums = lax.fori_loop(0, length // step, settle, zero)
+    devices = slabs.shape[0]
+    own = hid.shape[1] // devices
+    lane8 = lane_of(8)
+    row8 = lax.broadcasted_iota(jnp.int32, (8, 128), 0)
+    first_col = count[1]
+    limit = count[2]
+    q_row = jnp.broadcast_to(sums[:, :128], (8, 128))
+    v_row = jnp.broadcast_to(sums[:, 256:], (8, 128))
+    for i in range(devices):
+        begin = i * own - first_col
+        q_lane = lane8 + begin
+        v_lane = q_lane - 64
+        q_part = pltpu.roll(q_row, lax.rem(4096 - begin, 128), 1)
+        v_part = pltpu.roll(v_row, lax.rem(4096 - begin + 64, 128), 1)
+        q_ok = (lane8 < own) & (q_lane >= 0) & (q_lane < limit)
+        v_ok = (lane8 >= 64) & (lane8 < 64 + own) & (v_lane >= 0) & (v_lane < limit)
+        line = jnp.where(q_ok, q_part, jnp.where(v_ok, v_part, 0.0))
+        tile = jnp.where(row8 == 0, line, extra[i])
+        tail = jnp.concatenate([tile, jnp.zeros((8, 256), F32)], axis=1)
+        at = i * own
+        slabs[i, : own - 8, :] = wide_grad[at : at + own - 8, :].astype(LOW)
+        slabs[i, own - 8 :, :] = jnp.concatenate(
+            [wide_grad[at + own - 8 : at + own, :], tail], axis=0
+        ).astype(LOW)
+
+
+def attend_back(order, count, hidden_all, proj, gnat, gpack, extra, hd, scale):
     length = proj.shape[0]
     blks, step, _ = gnat.shape
+    devices = extra.shape[0]
+    width = hidden_all.shape[1]
     return pl.pallas_call(
         functools.partial(attend_back_kernel, hd, scale),
         name="attend_back",
         out_shape=(
             jax.ShapeDtypeStruct((blks, step, 384), LOW),
             jax.ShapeDtypeStruct((blks, step // 2, 384), LOW),
-            jax.ShapeDtypeStruct((8, 384), F32),
+            jax.ShapeDtypeStruct((devices, width // devices + 8, 384), LOW),
         ),
-        in_specs=[spec(pltpu.SMEM), spec(pltpu.SMEM)] + [spec(pltpu.VMEM)] * 3,
+        in_specs=[spec(pltpu.SMEM), spec(pltpu.SMEM), spec(ANY)] + [spec(pltpu.VMEM)] * 4,
         out_specs=(spec(pltpu.VMEM),) * 3,
         scratch_shapes=[
             pltpu.VMEM((length, 4, 128), F32),
             pltpu.VMEM((GROUP * 128, 4, 128), F32),
             pltpu.VMEM((GROUP * 128, 4, 128), F32),
             pltpu.VMEM((2 * length, 4, 128), F32),
+            pltpu.VMEM(hidden_all.shape, LOW),
+            pltpu.VMEM((width, 384), F32),
+            pltpu.SemaphoreType.DMA,
         ],
         compiler_params=pltpu.CompilerParams(vmem_limit_bytes=BIG),
         cost_estimate=pl.CostEstimate(
             flops=8 * 10**9, transcendentals=0, bytes_accessed=120 * 10**6
         ),
-    )(order, count, proj, gnat, gpack)
-
-
-def join_columns(even, odd, hd):
-    rows = even.shape[1]
-    first = even.transpose(1, 0, 2).reshape(rows, -1)
-    spread = jnp.concatenate([odd[:, :, :hd], odd[:, :, hd:]], axis=1)
-    return jnp.concatenate([first, spread.transpose(1, 0, 2).reshape(rows, -1)], axis=1)
-
-
-def split_columns(value, chips, hd):
-    rows = value.shape[0]
-    wide = chips * 2 * hd
-    even = value[:, :wide].reshape(rows, chips, 2 * hd).transpose(1, 0, 2)
-    odd = value[:, wide:].reshape(rows, chips, hd).transpose(1, 0, 2)
-    return even, jnp.concatenate([odd[:, : rows // 2], odd[:, rows // 2 :]], axis=2)
+    )(order, count, hidden_all, proj, gnat, gpack, extra)
+
+
+def middle_kernel(
+    hd, ceven, codd, hidden, first_hbm, outer_hbm, vecs, bias_inner, cot, mask,
+    hout, resid, geven, godd, merged, extra,
+    wa, wb, ctx, act, slope, ilow, first, flow, olow, unit, acc, hid_low, sums, inner_sums, sems,
+):
+    rows, width = hidden.shape
+    ff = outer_hbm.shape[0]
+    chips = ceven.shape[0]
+    get_out = pltpu.make_async_copy(
+        first_hbm.at[:, pl.ds(0, width)], wa.at[:, pl.ds(0, width)], sems.at[0]
+    )
+    get_in = pltpu.make_async_copy(
+        first_hbm.at[:, pl.ds(width, ff)], wa.at[:, pl.ds(width, ff)], sems.at[1]
+    )
+    get_outer = pltpu.make_async_copy(outer_hbm, wb, sems.at[2])
+    get_out.start()
+    get_in.start()
+    get_outer.start()
+    half = rows // 2
+    lane = lane_of(half)
+    low_half = lane < hd
+    for z in range(chips):
+        ctx[:, z * 128 : (z + 1) * 128] = ceven[z]
+    for z in range(0, chips, 2):
+        here = codd[z].astype(F32)
+        there = codd[z + 1].astype(F32)
+        at = chips * 128 + z * 64
+        ctx[:half, at : at + 128] = jnp.where(low_half, here, pltpu.roll(there, hd, 1)).astype(LOW)
+        ctx[half:, at : at + 128] = jnp.where(low_half, pltpu.roll(here, hd, 1), there).astype(LOW)
+    sums[...] = jnp.zeros_like(sums)
+    wide = 256
+    tile = 64
+
+    def add_rows(row, value):
+        sums[row : row + 1, :] += jnp.sum(value, axis=0, keepdims=True)
+
+    get_out.wait()
+
+    @pl.loop(0, width // wide)
+    def _(n):
+        at = pl.multiple_of(n * wide, wide)
+        acc[:, pl.ds(at, wide)] = nn_dot(ctx[...], wa[:, pl.ds(at, wide)])
+
+    @pl.loop(0, rows // tile)
+    def _(i):
+        own = pl.ds(pl.multiple_of(i * tile, tile), tile)
+        value = hidden[own, :].astype(F32) + acc[own, :] + vecs[2:3, :]
+        center = value - jnp.mean(value, axis=-1, keepdims=True)
+        spread = jnp.mean(center * center, axis=-1, keepdims=True)
+        inv = lax.rsqrt(spread + epsilon)
+        norm = center * inv * vecs[3:4, :] + vecs[4:5, :]
+        first[own, :] = norm
+        flow[own, :] = norm.astype(LOW)
+        unit[own, :] = center * inv
+        resid[own, 0:128] = jnp.broadcast_to(inv, (tile, 128))
+
+    get_in.wait()
+
+    @pl.loop(0, ff // wide)
+    def _(j):
+        at = pl.multiple_of(j * wide, wide)
+        cols = pl.ds(at, wide)
+        pre = nn_dot(flow[...], wa[:, pl.ds(width + at, wide)]) + bias_inner[0:1, cols]
+        gate = 0.5 + 0.5 * lax.erf(pre * (0.5**0.5))
+        act[:, cols] = (pre * gate).astype(LOW)
+        slope[:, cols] = gate + pre * jnp.exp(-0.5 * pre * pre) * (0.5 / math.pi) ** 0.5
+
+    get_outer.wait()
+
+    @pl.loop(0, width // wide)
+    def _(n):
+        at = pl.multiple_of(n * wide, wide)
+        acc[:, pl.ds(at, wide)] = nn_dot(act[...], wb[:, pl.ds(at, wide)])
+
+    @pl.loop(0, rows // tile)
+    def _(i):
+        own = pl.ds(pl.multiple_of(i * tile, tile), tile)
+        value = first[own, :] + acc[own, :] + vecs[5:6, :]
+        center = value - jnp.mean(value, axis=-1, keepdims=True)
+        spread = jnp.mean(center * center, axis=-1, keepdims=True)
+        inv = lax.rsqrt(spread + epsilon)
+        norm = center * inv
+        hout[own, :] = (norm * vecs[6:7, :] + vecs[7:8, :]).astype(LOW)
+        out_grad = cot[own, :].astype(F32) * mask[own, :].astype(F32)
+        pull = out_grad * vecs[6:7, :]
+        pull = pull - jnp.mean(pull, axis=-1, keepdims=True) - norm * jnp.mean(
+            pull * norm, axis=-1, keepdims=True
+        )
+        grad = pull * inv
+        low = grad.astype(LOW)
+        first[own, :] = grad
+        olow[own, :] = low
+        add_rows(4, low.astype(F32))
+        add_rows(5, out_grad * norm)
+        add_rows(6, out_grad)
+
+    @pl.loop(0, ff // wide)
+    def _(j):
+        cols = pl.ds(pl.multiple_of(j * wide, wide), wide)
+        low = (nt_dot(olow[...], wb[cols, :]) * slope[:, cols]).astype(LOW)
+        ilow[:, cols] = low
+        inner_sums[0:1, cols] = jnp.sum(low.astype(F32), axis=0, keepdims=True)
+
+    @pl.loop(0, width // wide)
+    def _(n):
+        at = pl.multiple_of(n * wide, wide)
+        acc[:, pl.ds(at, wide)] = nt_dot(ilow[...], wa[pl.ds(at, wide), width:])
+
+    @pl.loop(0, rows // tile)
+    def _(i):
+        own = pl.ds(pl.multiple_of(i * tile, tile), tile)
+        grad = acc[own, :] + first[own, :]
+        norm = unit[own, :]
+        inv = resid[own, 0:1]
+        pull = grad * vecs[3:4, :]
+        pull = pull - jnp.mean(pull, axis=-1, keepdims=True) - norm * jnp.mean(
+            pull * norm, axis=-1, keepdims=True
+        )
+        back = pull * inv
+        low = back.astype(LOW)
+        resid[own, :] = back
+        hid_low[own, :] = low
+        add_rows(1, low.astype(F32))
+        add_rows(2, grad * norm)
+        add_rows(3, grad)
+
+    @pl.loop(0, width // wide)
+    def _(n):
+        at = pl.multiple_of(n * wide, wide)
+        acc[:, pl.ds(at, wide)] = nt_dot(hid_low[...], wa[pl.ds(at, wide), :width])
+
+    for z in range(chips):
+        geven[z] = acc[:, z * 128 : (z + 1) * 128].astype(LOW)
+    for z in range(0, chips, 2):
+        at = chips * 128 + z * 64
+        top = acc[:half, at : at + 128]
+        bottom = acc[half:, at : at + 128]
+        godd[z] = jnp.where(low_half, top, pltpu.roll(bottom, hd, 1)).astype(LOW)
+        godd[z + 1] = jnp.where(low_half, pltpu.roll(top, hd, 1), bottom).astype(LOW)
+
+    devices = merged.shape[0]
+    own_rows = width // devices
+    outer_rows = ff // devices
+    block = 384
+    per = block // outer_rows
+
+    @pl.loop(0, ff // block)
+    def _(j):
+        part = tn_dot(act[:, pl.ds(pl.multiple_of(j * block, block), block)], olow[...])
+        for i in range(per):
+            merged[j * per + i, :outer_rows, :] = part[
+                i * outer_rows : (i + 1) * outer_rows, :
+            ].astype(LOW)
+
+    folds = ff // width
+    many = block // own_rows
+
+    @pl.loop(0, width // block)
+    def _(m):
+        cols = pl.ds(pl.multiple_of(m * block, block), block)
+        for h in range(0, folds, 2):
+            left = tn_dot(flow[:, cols], ilow[:, h * width : (h + 1) * width])
+            right = tn_dot(flow[:, cols], ilow[:, (h + 1) * width : (h + 2) * width])
+            at = outer_rows + h * own_rows
+            for i in range(many):
+                for r in range(0, own_rows, 8):
+                    base = i * own_rows + r
+                    merged[m * many + i, at + 2 * r : at + 2 * r + 16, :] = jnp.concatenate(
+                        [left[base : base + 8, :], right[base : base + 8, :]], axis=0
+                    ).astype(LOW)
+        part = tn_dot(ctx[:, cols], hid_low[...])
+        at = outer_rows + folds * own_rows
+        for i in range(many):
+            base = i * own_rows
+            merged[m * many + i, at : at + 16, :] = part[base : base + 16, :].astype(LOW)
+            merged[m * many + i, at + 16 : at + 32, :] = jnp.concatenate(
+                [part[base + 16 : base + 24, :], jnp.zeros((8, width), F32)], axis=0
+            ).astype(LOW)
+
+    row8 = lax.broadcasted_iota(jnp.int32, (8, 128), 0)
+    for i in range(devices):
+        piece = sums[:, i * own_rows : (i + 1) * own_rows]
+        piece = jnp.concatenate([piece, jnp.zeros((8, 128 - own_rows), F32)], axis=1)
+        inner = inner_sums[0:1, i * outer_rows : (i + 1) * outer_rows]
+        inner = jnp.concatenate([inner, jnp.zeros((1, 128 - outer_rows), F32)], axis=1)
+        extra[i] = jnp.where(row8 == 7, jnp.broadcast_to(inner, (8, 128)), piece)
+
+
+def middle(ceven, codd, hidden, first_half, outer_full, vecs, bias_inner, cot, mask, devices, hd):
+    rows, width = hidden.shape
+    ff = outer_full.shape[0]
+    slab = ff // devices + (ff // width + 1) * (width // devices) + 8
+    wide_low = pltpu.VMEM((rows, width), LOW)
+    wide_f32 = pltpu.VMEM((rows, width), F32)
+    return pl.pallas_call(
+        functools.partial(middle_kernel, hd),
+        name="middle",
+        out_shape=(
+            jax.ShapeDtypeStruct((rows, width), LOW),
+            jax.ShapeDtypeStruct((rows, width), F32),
+            jax.ShapeDtypeStruct(ceven.shape, LOW),
+            jax.ShapeDtypeStruct(codd.shape, LOW),
+            jax.ShapeDtypeStruct((devices, slab, width), LOW),
+            jax.ShapeDtypeStruct((devices, 8, 128), F32),
+        ),
+        in_specs=[spec(pltpu.VMEM)] * 3 + [spec(ANY)] * 2 + [spec(pltpu.VMEM)] * 4,
+        out_specs=(spec(pltpu.VMEM),) * 6,
+        scratch_shapes=[
+            pltpu.VMEM(first_half.shape, LOW),
+            pltpu.VMEM(outer_full.shape, LOW),
+            wide_low,
+            pltpu.VMEM((rows, ff), LOW),
+            pltpu.VMEM((rows, ff), F32),
+            pltpu.VMEM((rows, ff), LOW),
+            wide_f32, wide_low, wide_low, wide_f32, wide_f32, wide_low,
+            pltpu.VMEM((8, width), F32),
+            pltpu.VMEM((8, ff), F32),
+            pltpu.SemaphoreType.DMA((3,)),
+        ],
+        compiler_params=pltpu.CompilerParams(vmem_limit_bytes=BIG),
+        cost_estimate=pl.CostEstimate(
+            flops=17 * 10**9, transcendentals=0, bytes_accessed=40 * 10**6
+        ),
+    )(ceven, codd, hidden, first_half, outer_full, vecs, bias_inner, cot, mask)
+
+
+def final_kernel(
+    hd, zeven, zodd, proj_hbm, resid, proj_grads, share,
+    out, gq, gk, gv, go, gi, gu, g0, g1, g2, g3, g4, g5, g6, g7, g8, wp, triple, sem,
+):
+    rows, width = resid.shape
+    chips = zeven.shape[0]
+    fetch = pltpu.make_async_copy(proj_hbm, wp, sem)
+    fetch.start()
+    half = rows // 2
+    low_half = lane_of(half) < hd
+    for t in range(3):
+        cols = slice(t * 128, (t + 1) * 128)
+        for z in range(chips):
+            at = t * width + z * 128
+            triple[:, at : at + 128] = zeven[z, :, cols]
+        for z in range(0, chips, 2):
+            at = t * width + chips * 128 + z * 64
+            here = zodd[z, :, cols].astype(F32)
+            there = zodd[z + 1, :, cols].astype(F32)
+            triple[:half, at : at + 128] = jnp.where(
+                low_half, here, pltpu.roll(there, hd, 1)
+            ).astype(LOW)
+            triple[half:, at : at + 128] = jnp.where(
+                low_half, pltpu.roll(here, hd, 1), there
+            ).astype(LOW)
+    own = gq.shape[0]
+    keep = lane_of(own) < hd
+    for t, ref in enumerate((gq, gk, gv)):
+        cols = slice(t * 128, (t + 1) * 128)
+        for z in range(chips):
+            ref[:, z * 128 : (z + 1) * 128] = proj_grads[2 * z, :, cols].astype(F32)[:own]
+        for z in range(0, chips, 2):
+            here = proj_grads[2 * z + 1, :, cols].astype(F32)[:own]
+            there = proj_grads[2 * z + 3, :, cols].astype(F32)[:own]
+            at = chips * 128 + z * 64
+            ref[:, at : at + 128] = jnp.where(keep, here, pltpu.roll(there, hd, 1))
+    ff = gi.shape[1]
+    outer_rows = gu.shape[0]
+    folds = ff // width
+    gu[...] = share[:outer_rows, :].astype(F32)
+    for h in range(0, folds, 2):
+        at = outer_rows + h * own
+        for r in range(0, own, 8):
+            pair = share[at + 2 * r : at + 2 * r + 16, :].astype(F32)
+            gi[r : r + 8, h * width : (h + 1) * width] = pair[:8]
+            gi[r : r + 8, (h + 1) * width : (h + 2) * width] = pair[8:]
+    at = outer_rows + folds * own
+    go[...] = share[at : at + own + 8, :].astype(F32)[:own]
+    total = proj_grads[0, :, :128].astype(F32)[own:]
+    for d in range(1, 2 * chips):
+        total = total + proj_grads[d, :, :128].astype(F32)[own:]
+    g0[...] = total[0, :own]
+    g1[...] = total[0, 64 : 64 + own]
+    for v, ref in enumerate((g2, g3, g4)):
+        ref[...] = total[1 + v, :own]
+    g5[...] = total[7, : g5.shape[0]]
+    for v, ref in enumerate((g6, g7, g8)):
+        ref[...] = total[4 + v, :own]
+    fetch.wait()
+    wide = 256
+
+    @pl.loop(0, width // wide)
+    def _(n):
+        at = pl.multiple_of(n * wide, wide)
+        cols = pl.ds(at, wide)
+        out[:, cols] = nt_dot(triple[...], wp[pl.ds(at, wide), :]) + resid[:, cols]
+
+
+def final(zeven, zodd, projections, resid, proj_grads, share, own, ff, hd):
+    rows, width = resid.shape
+    mats = [(rows, width)] + [(own, width)] * 4 + [(own, ff), (ff * own // width, width)]
+    vectors = [(own,)] * 5 + [(ff * own // width,)] + [(own,)] * 3
+    return pl.pallas_call(
+        functools.partial(final_kernel, hd),
+        name="final",
+        out_shape=tuple(jax.ShapeDtypeStruct(shape, F32) for shape in mats + vectors),
+        in_specs=[spec(pltpu.VMEM)] * 2 + [spec(ANY)] + [spec(pltpu.VMEM)] * 3,
+        out_specs=(spec(pltpu.VMEM),) * 16,
+        scratch_shapes=[
+            pltpu.VMEM(projections.shape, LOW),
+            pltpu.VMEM((rows, 3 * width), LOW),
+            pltpu.SemaphoreType.DMA,
+        ],
+        compiler_params=pltpu.CompilerParams(vmem_limit_bytes=BIG),
+        cost_estimate=pl.CostEstimate(
+            flops=2 * 10**9, transcendentals=0, bytes_accessed=12 * 10**6
+        ),
+    )(zeven, zodd, projections, resid, proj_grads, share)
 
 
 def by_device(value, chips, hd):
@@ -651,14 +982,6 @@
     odd = value[:, wide:].reshape(rows, chips, hd).transpose(1, 0, 2)
     odd = jnp.pad(odd, ((0, 0), (0, 0), (0, hd)))
     return jnp.stack([even, odd], axis=1).reshape(2 * chips, rows, 2 * hd)
-
-
-def from_device(value, chips, hd):
-    rows = value.shape[1]
-    pairs = value.reshape(chips, 2, rows, 2 * hd)
-    even = pairs[:, 0].transpose(1, 0, 2).reshape(rows, -1)
-    odd = pairs[:, 1, :, :hd].transpose(1, 0, 2).reshape(rows, -1)
-    return jnp.concatenate([even, odd], axis=1)
 
 
 def fast_body(seqs, blks, heads):
@@ -717,9 +1040,6 @@
         bias_query, bias_value = [
             by_device(vecs[i : i + 1], chips, hd) for i in (0, 1)
         ]
-        bias_output, gain_first, shift_first, bias_outer, gain_final, shift_final = [
-            vecs[i] for i in range(2, 8)
-        ]
         bias_own = lax.dynamic_index_in_dim(
             jnp.concatenate([bias_query, jnp.zeros_like(bias_query), bias_value], axis=2),
             b, 0, keepdims=False,
@@ -732,120 +1052,35 @@
                 lax.dynamic_index_in_dim(order, 2 * k + 1, 0, keepdims=False),
             ]
         )
-        count = jnp.where(even_core, 2, 1).astype(jnp.int32).reshape(1)
+        count = jnp.stack(
+            [
+                jnp.where(even_core, 2, 1),
+                jnp.where(even_core, 2 * hd * k, (2 * chips + k) * hd),
+                jnp.where(even_core, 2 * hd, hd),
+            ]
+        ).astype(jnp.int32)
         proj, cnat, cpack = attend(
             order_own, count, hidden_all, weight_own, bias_own, blks, hd, scale
         )
         ceven, codd = return_rows(cnat, cpack, 1)
-        context_low = join_columns(ceven, codd, hd)
-
-        output_full = first_half[:, :width]
-        inner_full = first_half[:, width:]
-        hidden = hidden_in.astype(F32)
-        attention_out = nn_dot(context_low, output_full) + bias_output
-        first_norm, first_pull = jax.vjp(layer_norm, hidden + attention_out, gain_first, shift_first)
-        first_low = first_norm.astype(LOW)
-        inner_pre = nn_dot(first_low, inner_full) + bias_inner
-        activated, gelu_pull = jax.vjp(exact_gelu, inner_pre)
-        activated_low = activated.astype(LOW)
-        outer_out = nn_dot(activated_low, outer_full) + bias_outer
-        final_norm, final_pull = jax.vjp(layer_norm, first_norm + outer_out, gain_final, shift_final)
-        hidden_out = final_norm.astype(LOW)
-        out_grad = cotangent.astype(F32) * grad_mask.astype(F32)
-        second_grad, grad_final_gain, grad_final_shift = final_pull(out_grad)
-        outer_low = second_grad.astype(LOW)
-        grad_outer_weight = tn_dot(activated_low, outer_low)
-        grad_outer_bias = column_sum(outer_low)
-        inner_low = gelu_pull(nt_dot(outer_low, outer_full))[0].astype(LOW)
-        grad_inner_weight = tn_dot(first_low, inner_low)
-        grad_inner_bias = column_sum(inner_low)
-        first_grad = nt_dot(inner_low, inner_full) + second_grad
-        residual_grad, grad_attention_gain, grad_attention_shift = first_pull(first_grad)
-        attn_low = residual_grad.astype(LOW)
-        grad_output_weight = tn_dot(context_low, attn_low)
-        grad_output_bias = column_sum(attn_low)
-        context_grad = nt_dot(attn_low, output_full).astype(LOW)
-
-        vec_grads = jnp.stack(
-            [
-                grad_output_bias, grad_attention_gain, grad_attention_shift,
-                grad_outer_bias, grad_final_gain, grad_final_shift,
-            ]
-        )
-        vec_grads = vec_grads.reshape(6, devices, own).transpose(1, 0, 2).reshape(devices, 6 * own)
-        vec_grads = jnp.concatenate(
-            [vec_grads, grad_inner_bias.reshape(devices, hidden_units // devices)], axis=1
-        )
-        vec_grads = jnp.pad(vec_grads, ((0, 0), (0, width - vec_grads.shape[1])))
-        merged = jnp.concatenate(
-            [
-                grad_outer_weight.reshape(devices, hidden_units // devices, width).astype(LOW),
-                grad_inner_weight.reshape(devices, own, hidden_units // width, width)
-                .transpose(0, 2, 1, 3)
-                .reshape(devices, -1, width)
-                .astype(LOW),
-                grad_output_weight.reshape(devices, own, width).astype(LOW),
-                jnp.pad(vec_grads[:, None, :].astype(LOW), ((0, 0), (0, 7), (0, 0))),
-            ],
-            axis=1,
+        hidden_out, residual_grad, geven, godd, merged, extra = middle(
+            ceven, codd, hidden_in, first_half, outer_full, vecs, bias_inner, cotangent,
+            grad_mask, devices, hd,
         )
         share = lax.psum_scatter(
             merged.reshape(-1, width), axes, scatter_dimension=0, tiled=True
-        ).astype(F32)
-
-        geven, godd = split_columns(context_grad, chips, hd)
+        )
         gnat, gpack = spread_rows(geven, godd, 2)
-        znat, zpack, sums = attend_back(order_own, count, proj, gnat, gpack, hd, scale)
-        own_grads = tn_dot(hidden_all, znat.reshape(length, 384)).reshape(seqs, blks, own, 384)
-        grads = jnp.concatenate(
-            [own_grads, jnp.broadcast_to(sums, (seqs, blks, 8, 384))], axis=2
-        ).astype(LOW)
-        zeven, zodd, proj_grads = leave(znat, zpack, grads)
-        triple = jnp.concatenate(
-            [
-                join_columns(zeven[:, :, i * 128 : (i + 1) * 128], zodd[:, :, i * 128 : (i + 1) * 128], hd)
-                for i in range(3)
-            ],
-            axis=1,
-        )
-        input_grad = nt_dot(triple, projections) + residual_grad
-        grad_query_weight, grad_key_weight, grad_value_weight = [
-            from_device(proj_grads[:, :, i * 128 : (i + 1) * 128].astype(F32), chips, hd)
-            for i in range(3)
-        ]
-        me = lax.axis_index("seq") * blks + b
-        grad_query_bias = lax.dynamic_slice_in_dim(grad_query_weight[own], me * own, own)
-        grad_value_bias = lax.dynamic_slice_in_dim(grad_value_weight[own], me * own, own)
-        share_outer = share[: hidden_units // devices]
-        at = hidden_units // devices
-        tail = at + own * (hidden_units // width)
-        share_inner = (
-            share[at:tail]
-            .reshape(hidden_units // width, own, width)
-            .transpose(1, 0, 2)
-            .reshape(own, hidden_units)
-        )
-        share_output = share[tail : tail + own]
-        vec_own = share[tail + own]
-        vec_parts = [vec_own[i * own : (i + 1) * own] for i in range(6)]
-        return (
-            hidden_out,
-            input_grad,
-            grad_query_weight[:own],
-            grad_key_weight[:own],
-            grad_value_weight[:own],
-            share_output,
-            share_inner,
-            share_outer,
-            grad_query_bias,
-            grad_value_bias,
-            vec_parts[0],
-            vec_parts[1],
-            vec_parts[2],
-            vec_own[6 * own : 6 * own + hidden_units // devices],
-            vec_parts[3],
-            vec_parts[4],
-            vec_parts[5],
+        znat, zpack, grads = attend_back(
+            order_own, count, hidden_all, proj, gnat, gpack, extra, hd, scale
+        )
+        zeven, zodd, proj_grads = leave(
+            znat, zpack, grads.reshape((seqs, blks) + grads.shape[1:])
+        )
+        return (hidden_out,) + tuple(
+            final(
+                zeven, zodd, projections, residual_grad, proj_grads, share, own, hidden_units, hd
+            )
         )
 
     return run

time: 505 us -> 416 us (0.82)
  matrix products: 67 us -> 0 us
  local copies, waits for them, and re-layouts: 61.6 us -> 5.35 us
  Pallas kernels: 320 us -> 376 us
  other arithmetic: 32.5 us -> 10.2 us
  waiting for transfers between devices: 0.09 us -> 5.58 us
    dot_general x11 -> x0, matrix products: 67 us -> none  [the longest x3 26.9 us: nn_dot(): return jnp.dot(left, right, preferred_element_type=F32)]
    pallas_call x0 -> x2, Pallas kernels: none -> 50.3 us  [the longest x1 42 us: middle(): pl.pallas_call(functools.partial(middle_kernel, hd), name='middle', out_s...]
    convert_element_type x2 -> x0, local copies, waits for them, and re-layouts: 13.1 us -> none  [run(): merged = jnp.concatenate([grad_outer_weight.reshape(devices, hidden_units...]
    slice x17 -> x3, local copies, waits for them, and re-layouts: 10.5 us -> 0.01 us  [by_device(): even = value[:, :wide].reshape(rows, chips, 2 * hd).transpose(1, 0, 2)]
    transpose x16 -> x0, local copies, waits for them, and re-layouts: 9.46 us -> none  [the longest x5 5.35 us: join_columns(): first = even.transpose(1, 0, 2).reshape(rows, -1)]
    dot_general x1 -> x0, local copies, waits for them, and re-layouts: 8.73 us -> none  [tn_dot(): lax.dot_general(left, right, (((0,), (0,)), ((), ())), preferred_element_...]
    concatenate x4 -> x0, other arithmetic: 8.49 us -> none  [the longest x1 5.26 us: run(): jnp.concatenate([grad_outer_weight.reshape(devices, hidden_units // devic...]
    unnamed x46 -> x21, local copies, waits for them, and re-layouts: 8.26 us -> 0.05 us
  transfers between devices with their start and end apart: 4 -> 4, of which waited for: 0 -> 1; matrix products, arithmetic and copies ran while one was open for 30% -> 3% of each run, Pallas kernels for 64% -> 89%
where the time goes in v2:
time: 416 us; the launch traced here: 411 us
  Pallas kernels  376 us (90%)
  between operations  14.3 us (3%)
  other arithmetic  10.2 us (2%)
  waiting for transfers between devices  5.58 us (1%)
  local copies, waits for them, and re-layouts  5.35 us (1%)
    pallas_call x1, Pallas kernels, leave(): pl.pallas_call(functools.partial(exit_kernel, seqs, blks), name='leave',...  102 us
    pallas_call x1, Pallas kernels, entry(): pl.pallas_call(functools.partial(entry_kernel, seqs, blks, parts), name='...  82.2 us
    pallas_call x1, Pallas kernels, attend_back(): pl.pallas_call(functools.partial(attend_back_kernel, hd, scale), name='at...  47.6 us
    pallas_call x1, Pallas kernels, return_rows(): pl.pallas_call(functools.partial(return_kernel, blks), name='return_rows'...  43.4 us
    pallas_call x1, Pallas kernels, middle(): pl.pallas_call(functools.partial(middle_kernel, hd), name='middle', out_s...  42 us
    pallas_call x1, Pallas kernels, attend(): pl.pallas_call(functools.partial(attend_kernel, hd, scale), name='attend'...  30.7 us
    pallas_call x1, Pallas kernels, spread_rows(): pl.pallas_call(functools.partial(spread_kernel, blks), name='spread_rows'...  20 us
  transfers between devices with their start and end apart: 4, of which 1 were waited for; matrix products, arithmetic and copies ran while one was open for 3% of the time, Pallas kernels for 89%

profile of v2, /device:TPU:9, one launch (start us, length us, event | category | flops | bytes accessed | tf_op | source)
XLA Modules:
  0.0 411.4 jit_solution(13012547796582160649)
XLA Ops:
  7.3 1.6 convert_element_type.58
  9.0 1.0 convert_element_type.57
  10.0 0.9 convert_element_type.56
  10.9 0.7 pad_maximum_fusion.1
  11.7 0.9 convert_element_type.49
  12.6 0.9 convert_element_type.50
  13.5 0.9 convert_element_type.51
  14.3 0.7 pad_maximum_fusion.2
  15.2 0.1 reshape.242
  15.4 0.1 reshape.245
  15.6 0.1 reshape.248
  15.9 0.1 concatenate.58
  16.0 0.7 pad_maximum_fusion.w_ref
  16.7 82.2 %entry.1 = (bf16[8,2,256,768]{3,2,1,0:T(8,128)(2,1)}, bf16[4,8,32,384]{3,2,1,0:T(8,128)(2,1)}) custom-call(bf16[2,256,768]{2,1,0:T(8,128)(2,1)} %bitcast.69, bf16[8,32,384]{2,1,0:T(8,128)(2,1)} %pad_maximum_fusion.w_ref), custom_call_target="tpu_custom_call" | custom-call | bytes 200000000 | tf_op jit(solution)/shard_map/entry/pallas_call | solution.py:191
  99.0 1.0 slice.69
  99.9 1.9 slice.68
  101.9 0.1 reshape.259
  102.0 0.1 reshape.257.vecs
  102.2 0.1 transpose_reshape.6
  102.4 0.7 reshape.258.bias_inner
  103.1 0.6 pad_add_fusion.1.count
  103.8 0.7 constant_dynamic-slice_fusion.1
  104.5 0.6 pad_add_fusion.order
  105.1 0.6 fusion.2.bias
  105.7 30.7 %attend.1 = (bf16[4096,384]{1,0:T(8,128)(2,1)}, bf16[8,512,128]{2,1,0:T(8,128)(2,1)}, bf16[8,256,128]{2,1,0:T(8,128)(2,1)}) custom-call(s32[8192]{0:T(1024)} %pad_add_fusion.order, s32[3]{0:T(128)} %pad_add_fusion.1.count, bf16[4096,768]{1,0:T(8,128)(2,1)} %bitcast.92, bf16[768,384]{1,0:T(8,128)(2,1)} %bitcast.71, f32[1,384]{1,0:T(1,128)} %fusion.2.bias), custom_call_target="tpu_custom_call" | custom-call | flops 5000000000 | bytes 100000000 | tf_op jit(solution)/shard_map/attend/pallas_call | solution.py:507
  136.4 43.4 %return_rows.1 = (bf16[4,512,128]{2,1,0:T(8,128)(2,1)}, bf16[4,256,128]{2,1,0:T(8,128)(2,1)}) custom-call(bf16[8,512,128]{2,1,0:T(8,128)(2,1)} %get-tuple-element.56.nat_ref, bf16[8,256,128]{2,1,0:T(8,128)(2,1)} %get-tuple-element.57.pack_ref), custom_call_target="tpu_custom_call" | custom-call | bytes 80000000 | tf_op jit(solution)/shard_map/return_rows/pallas_call | solution.py:274
  179.9 42.0 %middle.1 = (bf16[512,768]{1,0:T(8,128)(2,1)}, f32[512,768]{1,0:T(8,128)}, bf16[4,512,128]{2,1,0:T(8,128)(2,1)}, bf16[4,256,128]{2,1,0:T(8,128)(2,1)}, bf16[32,2...) custom-call(bf16[4,512,128]{2,1,0:T(8,128)(2,1)} %get-tuple-element.58.ceven, bf16[4,256,128]{2,1,0:T(8,128)(2,1)} %get-tuple-element.59.codd, ...), custom_call_target="tpu_custom_call" | custom-call | flops 16999999488 | bytes 40000000 | tf_op jit(solution)/shard_map/middle/pallas_call | solution.py:856
  221.9 20.0 %spread_rows.1 = (bf16[8,512,128]{2,1,0:T(8,128)(2,1)}, bf16[8,256,128]{2,1,0:T(8,128)(2,1)}) custom-call(bf16[4,512,128]{2,1,0:T(8,128)(2,1)} %get-tuple-element.62.even_ref, bf16[4,256,128]{2,1,0:T(8,128)(2,1)} %get-tuple-element.63.odd_ref), custom_call_target="tpu_custom_call" | custom-call | bytes 80000000 | tf_op jit(solution)/shard_map/spread_rows/pallas_call | solution.py:355
  241.9 47.6 %attend_back.1 = (bf16[8,512,384]{2,1,0:T(8,128)(2,1)}, bf16[8,256,384]{2,1,0:T(8,128)(2,1)}, bf16[32,32,384]{2,1,0:T(8,128)(2,1)}) custom-call(s32[8192]{0:T(1024)} %pad_add_fusion.order, s32[3]{0:T(128)} %pad_add_fusion.1.count, bf16[4096,768]{1,0:T(8,128)(2,1)} %bitcast.93, bf16[4096,384]{1,0:T(8,128)(2,1)} %get-tuple-element.61.proj, ...), custom_call_target="tpu_custom_call" | custom-call | flops 8000000000 | bytes 120000000 | tf_op jit(solution)/shard_map/attend_back/pallas_call | solution.py:636
  289.5 101.7 %leave.1 = (bf16[4,512,384]{2,1,0:T(8,128)(2,1)}, bf16[4,256,384]{2,1,0:T(8,128)(2,1)}, bf16[8,32,384]{2,1,0:T(8,128)(2,1)}) custom-call(bf16[8,512,384]{2,1,0:T(8,128)(2,1)} %get-tuple-element.67.nat_ref, bf16[8,256,384]{2,1,0:T(8,128)(2,1)} %get-tuple-element.68.pack_ref, bf16[4,8,32,384]{3,2,1,0:T(8,128)(2,1)} %bitcast.70), custom_call_target="tpu_custom_call" | custom-call | bytes 200000000 | tf_op jit(solution)/shard_map/leave/pallas_call | solution.py:416
  391.2 5.5 %reduce-scatter.2.cloned.1.call-done.share = bf16[224,768]{1,0:T(8,128)(2,1)} async-done(((bf16[7168,768]{1,0:T(8,128)(2,1)}), bf16[224,768]{1,0:T(8,128)(2,1)}) %reduce-scatter.2.cloned.1.call-update) | async-done | bytes 344080 | tf_op jit(solution)/shard_map/reduce_scatter | solution.py:1070
  396.6 8.3 %final.1 = (f32[512,768]{1,0:T(8,128)}, f32[24,768]{1,0:T(8,128)}, f32[24,768]{1,0:T(8,128)}, f32[24,768]{1,0:T(8,128)}, f32[24,768]{1,0:T(8,128)}, /*index=5*/f...) custom-call(bf16[4,512,384]{2,1,0:T(8,128)(2,1)} %get-tuple-element., ...), custom_call_target="tpu_custom_call" | custom-call | flops 2000000000 | bytes 12000000 | tf_op jit(solution)/shard_map/final/pallas_call | solution.py:960
  (69 shorter events, 0.9 us)
Async XLA Ops:
  7.2 8.6 %copy-start.9 = (f32[96]{0:T(128)S(1)}, f32[96]{0:T(128)}, u32[]{:S(2)}) copy-start(f32[96]{0:T(128)} %param.31) | copy-start | bytes 1156
  7.2 8.6 %copy-start.2 = (f32[24]{0:T(128)S(1)}, f32[24]{0:T(128)}, u32[]{:S(2)}) copy-start(f32[24]{0:T(128)} %param.30) | copy-start | bytes 292
  7.2 8.6 %copy-start.1 = (f32[24]{0:T(128)S(1)}, f32[24]{0:T(128)}, u32[]{:S(2)}) copy-start(f32[24]{0:T(128)} %param.32) | copy-start | bytes 292
  7.2 8.6 %copy-start.4 = (f32[24]{0:T(128)S(1)}, f32[24]{0:T(128)}, u32[]{:S(2)}) copy-start(f32[24]{0:T(128)} %param.28) | copy-start | bytes 292
  7.2 8.6 %copy-start.3 = (f32[24]{0:T(128)S(1)}, f32[24]{0:T(128)}, u32[]{:S(2)}) copy-start(f32[24]{0:T(128)} %param.29) | copy-start | bytes 292
  7.2 8.6 %copy-start.6 = (f32[24]{0:T(128)S(1)}, f32[24]{0:T(128)}, u32[]{:S(2)}) copy-start(f32[24]{0:T(128)} %param.26) | copy-start | bytes 292
  7.3 8.6 %copy-start.5 = (f32[24]{0:T(128)S(1)}, f32[24]{0:T(128)}, u32[]{:S(2)}) copy-start(f32[24]{0:T(128)} %param.27) | copy-start | bytes 292
  7.3 8.6 %copy-start.8 = (f32[24]{0:T(128)S(1)}, f32[24]{0:T(128)}, u32[]{:S(2)}) copy-start(f32[24]{0:T(128)} %param.33) | copy-start | bytes 292
  7.3 8.6 %copy-start.7 = (f32[24]{0:T(128)S(1)}, f32[24]{0:T(128)}, u32[]{:S(2)}) copy-start(f32[24]{0:T(128)} %param.34) | copy-start | bytes 292
  7.3 172.5 %all-gather.6.cloned.1.call-start = ((), (), s32[]{:S(2)}) async-start(), calls=%async_computation.2 | async-start | bytes 4866048 | tf_op jit(solution)/shard_map/all_gather | solution.py:1027
  9.0 170.9 %all-gather.4.cloned.1.call-start = ((), (), s32[]{:S(2)}) async-start(), calls=%async_computation.1 | async-start | bytes 6082560 | tf_op jit(solution)/shard_map/all_gather | solution.py:1024
  11.6 379.6 %all-gather.8.cloned.1.call-start = ((), (), s32[]{:S(2)}) async-start(), calls=%async_computation.3 | async-start | bytes 3649536 | tf_op jit(solution)/shard_map/all_gather | solution.py:1028
  15.0 381.6 %reduce-scatter.2.cloned.1.call-start = ((), (), s32[]{:S(2)}) async-start(), calls=%async_computation.4 | async-start | bytes 11354112 | tf_op jit(solution)/shard_map/reduce_scatter | solution.py:1070
  102.1 34.3 %copy-start = (f32[8,768]{1,0:T(8,128)}, f32[8,768]{1,0:T(8,128)S(1)}, u32[]{:S(2)}) copy-start(f32[8,768]{1,0:T(8,128)S(1)} %reshape.257.vecs) | copy-start | bytes 73732
Sparse Core Ops, SparseCore 0:
  11.1 69.5 all-gather.5
  84.3 69.5 all-gather.3
  157.0 61.7 all-gather.7
  224.6 171.9 reduce-scatter.1

commit v3 on v2

--- a/solution.py
+++ b/solution.py
@@ -89,8 +89,8 @@
 
 
 def entry_kernel(
-    seqs, blks, parts, x_ref, w_ref, o_ref, wall_ref,
-    own_sem, ssem, rsem, wl, ws, wr, us, ur,
+    seqs, blks, parts, x_ref, w_ref, a0, a1, a2, o_ref, wall_ref, f0, f1, f2,
+    own_sem, ssem, rsem, wl, ws, wr, us, ur, al, zs, zr, ns, nr, ms, mr,
 ):
     half = blks // 2
     s = lax.axis_index("seq")
@@ -118,8 +118,41 @@
     def piece(src, blk, p, to, way):
         return send(src, o_ref.at[blk, p], ssem.at[way, blk, p], rsem.at[blk, p], {"blk": to})
 
+    shards = ((a0, f0), (a1, f1), (a2, f2))
+    x_next = s + 1 - 2 * lax.rem(s, 2)
+    y_next = s + 2 - 4 * (s // 2)
+    across = 3 - s
+    low_part = pl.ds(0, half // 2)
+    high_part = pl.ds(half // 2, half // 2)
+
+    def along(a, d):
+        own_ref, full = shards[a]
+        to = 2 * lax.rem(k + d, half) + c
+        return send(own_ref, full.at[s, k, c], zs.at[a, d], zr.at[a, d], {"blk": to})
+
+    def beside(a, way):
+        full = shards[a][1]
+        whole = full.at[s, :, c]
+        if way == 0:
+            return send(whole, whole, ns.at[a, 0], nr.at[a, 0], {"seq": x_next})
+        if way == 1:
+            return send(whole, whole, ns.at[a, 1], nr.at[a, 1], {"seq": y_next})
+        if way == 2:
+            part = full.at[y_next, low_part, c]
+            return send(part, part, ns.at[a, 2], nr.at[a, 2], {"seq": x_next})
+        part = full.at[x_next, high_part, c]
+        return send(part, part, ns.at[a, 3], nr.at[a, 3], {"seq": y_next})
+
+    def pair(a, i, src):
+        part = shards[a][1].at[src, :, c]
+        return send(part, part, ms.at[a, i], mr.at[a, i], {"blk": mate})
+
     for d in range(1, blks):
         slab(d).start()
+    for a in range(3):
+        for d in range(1, half):
+            along(a, d).start()
+        pltpu.make_async_copy(shards[a][0], shards[a][1].at[s, k, c], al.at[a]).start()
     own_slab = pltpu.make_async_copy(w_ref.at[b], wall_ref.at[s, b], wl)
     own_slab.start()
     for p in range(parts):
@@ -139,6 +172,22 @@
         slab(d).wait_recv()
     for d in range(1, seqs):
         group(d).start()
+    for a in range(3):
+        pltpu.make_async_copy(shards[a][0], shards[a][1].at[s, k, c], al.at[a]).wait()
+        for d in range(1, half):
+            along(a, d).wait_recv()
+        beside(a, 0).start()
+        beside(a, 1).start()
+        pair(a, 0, s).start()
+
+    def second(a):
+        beside(a, 1).wait_recv()
+        beside(a, 2).start()
+        pair(a, 2, y_next).start()
+        beside(a, 0).wait_recv()
+        beside(a, 3).start()
+        pair(a, 1, x_next).start()
+
     for t in range(1, half):
         for p in range(parts):
             @pl.when(k - t >= 0)
@@ -162,6 +211,12 @@
                     piece(o_ref.at[blk, p], blk, p, left, 0).start()
 
                 piece(o_ref.at[blk, p], blk, p, mate, 2).start()
+
+        second(t - 1)
+    for a in range(3):
+        beside(a, 2).wait_recv()
+        beside(a, 3).wait_recv()
+        pair(a, 3, across).start()
     for j in range(half):
         blk = 2 * j + 1 - c
         for p in range(parts):
@@ -183,9 +238,16 @@
         slab(d).wait_send()
     for d in range(1, seqs):
         group(d).wait()
-
-
-def entry(hidden, slabs, seqs, blks, parts):
+    for a in range(3):
+        for i, src in enumerate((s, x_next, y_next, across)):
+            pair(a, i, src).wait()
+        for way in range(4):
+            beside(a, way).wait_send()
+        for d in range(1, half):
+            along(a, d).wait_send()
+
+
+def entry(hidden, slabs, shards, seqs, blks, parts):
     rows, width = hidden.shape
     dma = pltpu.SemaphoreType.DMA
     return pl.pallas_call(
@@ -194,16 +256,19 @@
         out_shape=(
             jax.ShapeDtypeStruct((blks, parts, rows // parts, width), LOW),
             jax.ShapeDtypeStruct((seqs,) + slabs.shape, LOW),
-        ),
-        in_specs=[spec(pltpu.VMEM)] * 2,
-        out_specs=(spec(ANY), spec(ANY)),
+        )
+        + tuple(jax.ShapeDtypeStruct((seqs, blks // 2, 2) + x.shape, LOW) for x in shards),
+        in_specs=[spec(pltpu.VMEM)] * 5,
+        out_specs=(spec(ANY),) * 5,
         scratch_shapes=[
             dma, dma((3, blks, parts)), dma((blks, parts)), dma,
             dma((blks,)), dma((blks,)), dma((seqs,)), dma((seqs,)),
+            dma((3,)), dma((3, blks // 2)), dma((3, blks // 2)),
+            dma((3, 4)), dma((3, 4)), dma((3, 4)), dma((3, 4)),
         ],
         compiler_params=pltpu.CompilerParams(collective_id=0, has_side_effects=True),
         cost_estimate=pl.CostEstimate(flops=0, transcendentals=0, bytes_accessed=200 * 10**6),
-    )(hidden.reshape(parts, rows // parts, width), slabs)
+    )(hidden.reshape(parts, rows // parts, width), slabs, *shards)
 
 
 def return_kernel(blks, nat_ref, pack_ref, even_ref, odd_ref, buf, lsem, ssem, rsem):
@@ -286,10 +351,18 @@
     )(nat, pack)
 
 
-def spread_kernel(blks, even_ref, odd_ref, nat_ref, pack_ref, buf, lsem, ssem, rsem):
+def spread_kernel(
+    blks, even_ref, odd_ref, grad_ref, nat_ref, pack_ref, total,
+    buf, mine, theirs, lsem, ssem, rsem, ml, ms, mr,
+):
     b = lax.axis_index("blk")
     c = lax.rem(b, 2)
+    mate = b + 1 - 2 * c
     greet([{"blk": lax.rem(b + d, blks)} for d in range(1, blks)])
+    swap = send(grad_ref.at[:, 1 - c], theirs, ms, mr, {"blk": mate})
+    swap.start()
+    load = pltpu.make_async_copy(grad_ref.at[:, c], mine, ml)
+    load.start()
 
     def full(d, slot):
         peer = lax.rem(b + d, blks)
@@ -313,6 +386,13 @@
         @pl.when(jnp.logical_not(to_even))
         def _():
             packed(d, b).start()
+
+    load.wait()
+    swap.wait()
+
+    @pl.loop(0, total.shape[0])
+    def _(o):
+        total[o] = (mine[o].astype(F32) + theirs[o].astype(F32)).astype(LOW)
 
     @pl.when(c == 0)
     def _():
@@ -349,8 +429,9 @@
             packed(d, b).wait_send()
 
 
-def spread_rows(even, odd, collective_id):
+def spread_rows(even, odd, grads, collective_id):
     blks = 2 * even.shape[0]
+    half_shape = grads.shape[:1] + grads.shape[2:]
     dma = pltpu.SemaphoreType.DMA
     return pl.pallas_call(
         functools.partial(spread_kernel, blks),
@@ -358,18 +439,27 @@
         out_shape=(
             jax.ShapeDtypeStruct((blks,) + even.shape[1:], LOW),
             jax.ShapeDtypeStruct((blks,) + odd.shape[1:], LOW),
+            jax.ShapeDtypeStruct(half_shape, LOW),
         ),
-        in_specs=[spec(ANY)] * 2,
-        out_specs=(spec(ANY), spec(ANY)),
-        scratch_shapes=[pltpu.VMEM(even.shape[1:], LOW), dma, dma((blks,)), dma((blks,))],
-        compiler_params=pltpu.CompilerParams(collective_id=collective_id, has_side_effects=True),
+        in_specs=[spec(ANY)] * 3,
+        out_specs=(spec(ANY), spec(ANY), spec(pltpu.VMEM)),
+        scratch_shapes=[
+            pltpu.VMEM(even.shape[1:], LOW),
+            pltpu.VMEM(half_shape, LOW),
+            pltpu.VMEM(half_shape, LOW),
+            dma, dma((blks,)), dma((blks,)), dma, dma, dma,
+        ],
+        compiler_params=pltpu.CompilerParams(
+            collective_id=collective_id, has_side_effects=True, vmem_limit_bytes=BIG
+        ),
         cost_estimate=pl.CostEstimate(flops=0, transcendentals=0, bytes_accessed=80 * 10**6),
-    )(even, odd)
+    )(even, odd, grads)
 
 
 def exit_kernel(
-    seqs, blks, nat_ref, pack_ref, grad_ref, even_ref, odd_ref, out_ref,
-    buf, stage, total, lsem, ssem, rsem, us, ur, gl, gs, gr,
+    seqs, blks, nat_ref, pack_ref, grad_ref, big_ref, even_ref, odd_ref, out_ref, big_out,
+    buf, stage, total, big_stage, big_total,
+    lsem, ssem, rsem, us, ur, gl, gs, gr, bl, bu, bv, cl, cs, cr,
 ):
     s = lax.axis_index("seq")
     b = lax.axis_index("blk")
@@ -387,8 +477,31 @@
         peer = lax.rem(b + d, blks)
         return send(total.at[peer], out_ref.at[b], gs.at[d], gr.at[d], {"blk": peer})
 
+    chips = blks // 2
+    pieces = big_ref.shape[2]
+
+    def big_group(p, d):
+        peer = lax.rem(s + d, seqs)
+        return send(
+            big_ref.at[peer, :, p], big_stage.at[p, d], bu.at[p, d], bv.at[p, d], {"seq": peer}
+        )
+
+    def big_slab(p, d):
+        to = lax.rem(k + d, chips)
+        return send(
+            big_total.at[p, to], big_out.at[k, p], cs.at[p, d], cr.at[p, d], {"blk": 2 * to + c}
+        )
+
+    def big_own(p):
+        return pltpu.make_async_copy(big_ref.at[s, :, p], big_stage.at[p, 0], bl.at[p])
+
+    for p in range(pieces):
+        big_own(p).start()
     for d in range(1, seqs):
         group(d).start()
+    for p in range(pieces):
+        for d in range(1, seqs):
+            big_group(p, d).start()
     start_return(blks, b, k, c, nat_ref, pack_ref, even_ref, odd_ref, buf, lsem, ssem, rsem)
     for d in range(1, seqs):
         group(d).wait_recv()
@@ -402,16 +515,39 @@
     own = pltpu.make_async_copy(total.at[b], out_ref.at[b], gl)
     own.start()
     own.wait()
+    for p in range(pieces):
+        big_own(p).wait()
+        for d in range(1, seqs):
+            big_group(p, d).wait_recv()
+
+        @pl.loop(0, chips)
+        def _(o):
+            acc = big_stage[p, 0, o].astype(F32)
+            for d in range(1, seqs):
+                acc = acc + big_stage[p, d, o].astype(F32)
+            big_total[p, o] = acc.astype(LOW)
+
+        for d in range(1, chips):
+            big_slab(p, d).start()
+        keep = pltpu.make_async_copy(big_total.at[p, k], big_out.at[k, p], cl.at[p])
+        keep.start()
+        keep.wait()
     finish_return(blks, b, k, c, nat_ref, pack_ref, even_ref, odd_ref, ssem, rsem)
     for d in range(1, blks):
         slab(d).wait()
     for d in range(1, seqs):
         group(d).wait_send()
-
-
-def leave(nat, pack, grads):
+    for p in range(pieces):
+        for d in range(1, chips):
+            big_slab(p, d).wait()
+        for d in range(1, seqs):
+            big_group(p, d).wait_send()
+
+
+def leave(nat, pack, grads, big):
     blks = nat.shape[0]
     seqs = grads.shape[0]
+    chips, pieces = big.shape[1:3]
     dma = pltpu.SemaphoreType.DMA
     return pl.pallas_call(
         functools.partial(exit_kernel, seqs, blks),
@@ -420,19 +556,34 @@
             jax.ShapeDtypeStruct((blks // 2,) + nat.shape[1:], LOW),
             jax.ShapeDtypeStruct((blks // 2,) + pack.shape[1:], LOW),
             jax.ShapeDtypeStruct(grads.shape[1:], LOW),
+            jax.ShapeDtypeStruct(big.shape[1:], LOW),
         ),
-        in_specs=[spec(ANY), spec(ANY), spec(pltpu.VMEM)],
-        out_specs=(spec(ANY), spec(ANY), spec(ANY)),
+        in_specs=[spec(ANY), spec(ANY), spec(pltpu.VMEM), spec(ANY)],
+        out_specs=(spec(ANY),) * 4,
         scratch_shapes=[
             pltpu.VMEM(nat.shape[1:], LOW),
             pltpu.VMEM(grads.shape, LOW),
             pltpu.VMEM(grads.shape[1:], LOW),
+            pltpu.VMEM((pieces, seqs, chips) + big.shape[3:], LOW),
+            pltpu.VMEM((pieces, chips) + big.shape[3:], LOW),
             dma, dma((blks,)), dma((blks,)), dma((seqs,)), dma((seqs,)),
             dma, dma((blks,)), dma((blks,)),
+            dma((pieces,)), dma((pieces, seqs)), dma((pieces, seqs)),
+            dma((pieces,)), dma((pieces, chips)), dma((pieces, chips)),
         ],
-        compiler_params=pltpu.CompilerParams(collective_id=3, has_side_effects=True),
+        compiler_params=pltpu.CompilerParams(
+            collective_id=3, has_side_effects=True, vmem_limit_bytes=BIG
+        ),
         cost_estimate=pl.CostEstimate(flops=0, transcendentals=0, bytes_accessed=200 * 10**6),
-    )(nat, pack, grads)
+    )(nat, pack, grads, big)
+
+
+def owner_facts(hd, chips):
+    b = lax.axis_index("blk")
+    k = b // 2
+    odd = lax.rem(b, 2)
+    first = jnp.where(odd == 0, 2 * hd * k, (2 * chips + k) * hd)
+    return 2 - odd, first, (2 - odd) * hd
 
 
 def lane_of(rows):
@@ -445,43 +596,83 @@
     return jnp.where(keep, value, 0.0).astype(LOW)
 
 
+def part_of(u, t):
+    return pl.ds(u * 512 + t, 128, stride=4)
+
+
+def row_part(ref, u, t):
+    return ref[part_of(u, t), :]
+
+
+def column_softmax(scores):
+    weights = jnp.exp(scores - jnp.max(scores, axis=0, keepdims=True))
+    return weights * (1.0 / jnp.sum(weights, axis=0, keepdims=True))
+
+
 def attend_kernel(
-    hd, scale, order, count, hid, weight, bias, proj, nat, pack, rows4, take, mix, back
+    hd, scale, order, hid, gathered, proj, nat, pack, vecs, bias_inner,
+    rows4, take, take_b, mix, mix_b, back, wide_weight, weight,
 ):
-    length = hid.shape[0]
-    step = nat.shape[1]
+    length, width = hid.shape
+    blks, step, _ = nat.shape
+    devices = gathered.shape[0]
+    own_rows = width // devices
+    per = bias_inner.shape[1] // devices
+    heads_here, first, _ = owner_facts(hd, blks // 2)
+    for i in range(devices):
+        slab = gathered[i].astype(F32)
+        wide_weight[i * own_rows : (i + 1) * own_rows, :] = slab[:own_rows, :]
+        vecs[:, i * own_rows : (i + 1) * own_rows] = slab[own_rows:, :own_rows]
+        bias_inner[0:1, i * per : (i + 1) * per] = slab[own_rows : own_rows + 1, 128 : 128 + per]
+    weight[...] = wide_weight[...].astype(LOW)
+    tile = vecs[:, pl.ds(pl.multiple_of(first // 128 * 128, 128), 128)]
+    tile = jnp.where(lax.rem(first, 128) == 0, tile, pltpu.roll(tile, 64, 1))
+    bias = jnp.concatenate([tile[0:1], jnp.zeros((1, 128), F32), tile[1:2]], axis=1)
 
     @pl.loop(0, length // step)
     def _(i):
         at = pl.multiple_of(i * step, step)
-        low = (nn_dot(hid[pl.ds(at, step), :], weight[...]) + bias[...]).astype(LOW)
+        low = (nn_dot(hid[pl.ds(at, step), :], weight[...]) + bias).astype(LOW)
         proj[pl.ds(at, step), :] = low
         wide = low.astype(F32)
         for t in range(3):
-            rows4[pl.ds(at, step), t, :] = wide[:, t * 128 : (t + 1) * 128]
+            rows4[pl.ds(4 * at + t, step, stride=4), :] = wide[:, t * 128 : (t + 1) * 128]
 
     span = GROUP * 128
 
-    @pl.loop(0, count[0])
+    def gather(buf, base):
+        for j in range(span):
+            buf[4 * j : 4 * j + 4, :] = rows4[pl.ds(pl.multiple_of(4 * order[base + j], 4), 4), :]
+
+    def attend_group(slot, buf, out):
+        for u in range(GROUP):
+            own = pl.ds(u * 128, 128)
+            query = low_lanes(row_part(buf, u, 0) * scale, slot, hd)
+            probs = column_softmax(nt_dot(row_part(buf, u, 1).astype(LOW), query))
+            out[own, :] = tn_dot(probs.astype(LOW), row_part(buf, u, 2).astype(LOW))
+
+    def scatter(slot, out, base):
+        for j in range(span):
+            back[pl.ds(slot * length + order[base + j], 1), :] = out[pl.ds(j, 1), :]
+
+    @pl.loop(0, heads_here)
     def _(slot):
-        @pl.loop(0, length // span)
+        begin = slot * length
+        gather(take, begin)
+
+        @pl.loop(0, length // (2 * span))
         def _(i):
-            base = slot * length + i * span
-            for j in range(span):
-                take[j] = rows4[order[base + j]]
-            for u in range(GROUP):
-                own = pl.ds(u * 128, 128)
-                query = low_lanes(take[own, 0, :], slot, hd)
-                scores = nt_dot(query, take[own, 1, :].astype(LOW)) * scale
-                weights = jnp.exp(scores - jnp.max(scores, axis=-1, keepdims=True))
-                probs = weights / jnp.sum(weights, axis=-1, keepdims=True)
-                mix[own, :] = nn_dot(probs.astype(LOW), take[own, 2, :].astype(LOW))
-            for j in range(span):
-                back[pl.ds(slot * length + order[base + j], 1), :] = mix[pl.ds(j, 1), :]
+            base = begin + 2 * i * span
+            gather(take_b, base + span)
+            attend_group(slot, take, mix)
+            scatter(slot, mix, base)
+            gather(take, jnp.minimum(base + 2 * span, begin + length - span))
+            attend_group(slot, take_b, mix_b)
+            scatter(slot, mix_b, base + span)
 
     lane = lane_of(step)
 
-    @pl.when(count[0] == 2)
+    @pl.when(heads_here == 2)
     def _():
         @pl.loop(0, length // step)
         def _(i):
@@ -492,7 +683,7 @@
 
     half = step // 2
 
-    @pl.when(count[0] == 1)
+    @pl.when(heads_here == 1)
     def _():
         @pl.loop(0, length // step)
         def _(i):
@@ -501,8 +692,8 @@
             pack[i] = jnp.where(lane[:half] < hd, back[pl.ds(at, half), :], upper).astype(LOW)
 
 
-def attend(order, count, hid, weight, bias, blks, hd, scale):
-    length = hid.shape[0]
+def attend(order, hid, gathered, blks, ff, hd, scale):
+    length, width = hid.shape
     step = length // blks
     return pl.pallas_call(
         functools.partial(attend_kernel, hd, scale),
@@ -511,29 +702,36 @@
             jax.ShapeDtypeStruct((length, 384), LOW),
             jax.ShapeDtypeStruct((blks, step, 128), LOW),
             jax.ShapeDtypeStruct((blks, step // 2, 128), LOW),
+            jax.ShapeDtypeStruct((8, width), F32),
+            jax.ShapeDtypeStruct((8, ff), F32),
         ),
-        in_specs=[spec(pltpu.SMEM), spec(pltpu.SMEM)] + [spec(pltpu.VMEM)] * 3,
-        out_specs=(spec(pltpu.VMEM),) * 3,
+        in_specs=[spec(pltpu.SMEM)] + [spec(pltpu.VMEM)] * 2,
+        out_specs=(spec(pltpu.VMEM),) * 5,
         scratch_shapes=[
-            pltpu.VMEM((length, 4, 128), F32),
-            pltpu.VMEM((GROUP * 128, 4, 128), F32),
+            pltpu.VMEM((4 * length, 128), F32),
+            pltpu.VMEM((GROUP * 512, 128), F32),
+            pltpu.VMEM((GROUP * 512, 128), F32),
+            pltpu.VMEM((GROUP * 128, 128), F32),
             pltpu.VMEM((GROUP * 128, 128), F32),
             pltpu.VMEM((2 * length, 128), F32),
+            pltpu.VMEM((width, 384), F32),
+            pltpu.VMEM((width, 384), LOW),
         ],
         compiler_params=pltpu.CompilerParams(vmem_limit_bytes=BIG),
         cost_estimate=pl.CostEstimate(
             flops=5 * 10**9, transcendentals=0, bytes_accessed=100 * 10**6
         ),
-    )(order, count, hid, weight, bias)
+    )(order, hid, gathered)
 
 
 def attend_back_kernel(
-    hd, scale, order, count, hidden_hbm, proj, gnat, gpack, extra, znat, zpack, slabs,
-    rows4, take, out4, back4, hid, wide_grad, sem,
+    hd, scale, order, hidden_hbm, proj, gnat, gpack, extra, znat, zpack, slabs,
+    rows4, take, take_b, out4, out4_b, back4, hid, wide_grad, sem,
 ):
     length = proj.shape[0]
     step = gnat.shape[1]
     half = step // 2
+    heads_here, first_col, limit = owner_facts(hd, gnat.shape[0] // 2)
     fetch = pltpu.make_async_copy(hidden_hbm, hid, sem)
     fetch.start()
 
@@ -542,43 +740,57 @@
         at = pl.multiple_of(i * step, step)
         wide = proj[pl.ds(at, step), :].astype(F32)
         for t in range(3):
-            rows4[pl.ds(at, step), t, :] = wide[:, t * 128 : (t + 1) * 128]
-
-        @pl.when(count[0] == 2)
+            rows4[pl.ds(4 * at + t, step, stride=4), :] = wide[:, t * 128 : (t + 1) * 128]
+
+        @pl.when(heads_here == 2)
         def _():
-            rows4[pl.ds(at, step), 3, :] = gnat[i].astype(F32)
-
-        @pl.when(count[0] == 1)
+            rows4[pl.ds(4 * at + 3, step, stride=4), :] = gnat[i].astype(F32)
+
+        @pl.when(heads_here == 1)
         def _():
             pair = gpack[i].astype(F32)
-            rows4[pl.ds(at, half), 3, :] = pair
-            rows4[pl.ds(at + half, half), 3, :] = pltpu.roll(pair, hd, 1)
+            rows4[pl.ds(4 * at + 3, half, stride=4), :] = pair
+            rows4[pl.ds(4 * (at + half) + 3, half, stride=4), :] = pltpu.roll(pair, hd, 1)
 
     span = GROUP * 128
 
-    @pl.loop(0, count[0])
+    def gather(buf, base):
+        for j in range(span):
+            buf[4 * j : 4 * j + 4, :] = rows4[pl.ds(pl.multiple_of(4 * order[base + j], 4), 4), :]
+
+    def attend_group(slot, buf, out):
+        for u in range(GROUP):
+            own = pl.ds(u * 128, 128)
+            query = low_lanes(row_part(buf, u, 0) * scale, slot, hd)
+            grad = low_lanes(row_part(buf, u, 3), slot, hd)
+            keys = row_part(buf, u, 1).astype(LOW)
+            probs = column_softmax(nt_dot(keys, query))
+            prob_grad = nt_dot(row_part(buf, u, 2).astype(LOW), grad)
+            shift = jnp.sum(probs * prob_grad, axis=0, keepdims=True)
+            score_low = (probs * (prob_grad - shift)).astype(LOW)
+            out[part_of(u, 0), :] = tn_dot(score_low, keys) * scale
+            out[part_of(u, 1), :] = nn_dot(score_low, query)
+            out[part_of(u, 2), :] = nn_dot(probs.astype(LOW), grad)
+
+    def scatter(slot, out, base):
+        for j in range(span):
+            at = pl.multiple_of(4 * (slot * length + order[base + j]), 4)
+            back4[pl.ds(at, 4), :] = out[4 * j : 4 * j + 4, :]
+
+    @pl.loop(0, heads_here)
     def _(slot):
-        @pl.loop(0, length // span)
+        begin = slot * length
+        gather(take, begin)
+
+        @pl.loop(0, length // (2 * span))
         def _(i):
-            base = slot * length + i * span
-            for j in range(span):
-                take[j] = rows4[order[base + j]]
-            for u in range(GROUP):
-                own = pl.ds(u * 128, 128)
-                query = low_lanes(take[own, 0, :], slot, hd)
-                grad = low_lanes(take[own, 3, :], slot, hd)
-                keys = take[own, 1, :].astype(LOW)
-                scores = nt_dot(query, keys) * scale
-                weights = jnp.exp(scores - jnp.max(scores, axis=-1, keepdims=True))
-                probs = weights / jnp.sum(weights, axis=-1, keepdims=True)
-                prob_grad = nt_dot(grad, take[own, 2, :].astype(LOW))
-                shift = jnp.sum(probs * prob_grad, axis=-1, keepdims=True)
-                score_low = (probs * (prob_grad - shift)).astype(LOW)
-                out4[own, 0, :] = nn_dot(score_low, keys) * scale
-                out4[own, 1, :] = tn_dot(score_low, query) * scale
-                out4[own, 2, :] = tn_dot(probs.astype(LOW), grad)
-            for j in range(span):
-                back4[slot * length + order[base + j]] = out4[j]
+            base = begin + 2 * i * span
+            gather(take_b, base + span)
+            attend_group(slot, take, out4)
+            scatter(slot, out4, base)
+            gather(take, jnp.minimum(base + 2 * span, begin + length - span))
+            attend_group(slot, take_b, out4_b)
+            scatter(slot, out4_b, base + span)
 
     lane = lane_of(step)
     fetch.wait()
@@ -590,9 +802,9 @@
         parts = []
         for t in range(3):
             cols = pl.ds(t * 128, 128)
-            first = back4[pl.ds(at, step), t, :]
-            second = back4[pl.ds(length + at, step), t, :]
-            second = jnp.where(count[0] == 2, second, jnp.zeros_like(second))
+            first = back4[pl.ds(4 * at + t, step, stride=4), :]
+            second = back4[pl.ds(4 * (length + at) + t, step, stride=4), :]
+            second = jnp.where(heads_here == 2, second, jnp.zeros_like(second))
             low = jnp.where(lane < hd, first, second).astype(LOW)
             znat[i, :, cols] = low
             wide = low.astype(F32)
@@ -606,8 +818,6 @@
     own = hid.shape[1] // devices
     lane8 = lane_of(8)
     row8 = lax.broadcasted_iota(jnp.int32, (8, 128), 0)
-    first_col = count[1]
-    limit = count[2]
     q_row = jnp.broadcast_to(sums[:, :128], (8, 128))
     v_row = jnp.broadcast_to(sums[:, 256:], (8, 128))
     for i in range(devices):
@@ -628,7 +838,7 @@
         ).astype(LOW)
 
 
-def attend_back(order, count, hidden_all, proj, gnat, gpack, extra, hd, scale):
+def attend_back(order, hidden_all, proj, gnat, gpack, extra, hd, scale):
     length = proj.shape[0]
     blks, step, _ = gnat.shape
     devices = extra.shape[0]
@@ -641,13 +851,15 @@
             jax.ShapeDtypeStruct((blks, step // 2, 384), LOW),
             jax.ShapeDtypeStruct((devices, width // devices + 8, 384), LOW),
         ),
-        in_specs=[spec(pltpu.SMEM), spec(pltpu.SMEM), spec(ANY)] + [spec(pltpu.VMEM)] * 4,
+        in_specs=[spec(pltpu.SMEM), spec(ANY)] + [spec(pltpu.VMEM)] * 4,
         out_specs=(spec(pltpu.VMEM),) * 3,
         scratch_shapes=[
-            pltpu.VMEM((length, 4, 128), F32),
-            pltpu.VMEM((GROUP * 128, 4, 128), F32),
-            pltpu.VMEM((GROUP * 128, 4, 128), F32),
-            pltpu.VMEM((2 * length, 4, 128), F32),
+            pltpu.VMEM((4 * length, 128), F32),
+            pltpu.VMEM((GROUP * 512, 128), F32),
+            pltpu.VMEM((GROUP * 512, 128), F32),
+            pltpu.VMEM((GROUP * 512, 128), F32),
+            pltpu.VMEM((GROUP * 512, 128), F32),
+            pltpu.VMEM((8 * length, 128), F32),
             pltpu.VMEM(hidden_all.shape, LOW),
             pltpu.VMEM((width, 384), F32),
             pltpu.SemaphoreType.DMA,
@@ -656,7 +868,7 @@
         cost_estimate=pl.CostEstimate(
             flops=8 * 10**9, transcendentals=0, bytes_accessed=120 * 10**6
         ),
-    )(order, count, hidden_all, proj, gnat, gpack, extra)
+    )(order, hidden_all, proj, gnat, gpack, extra)
 
 
 def middle_kernel(
@@ -886,7 +1098,7 @@
 
 
 def final_kernel(
-    hd, zeven, zodd, proj_hbm, resid, proj_grads, share,
+    hd, zeven, zodd, proj_hbm, resid, proj_grads, shares,
     out, gq, gk, gv, go, gi, gu, g0, g1, g2, g3, g4, g5, g6, g7, g8, wp, triple, sem,
 ):
     rows, width = resid.shape
@@ -924,15 +1136,23 @@
     ff = gi.shape[1]
     outer_rows = gu.shape[0]
     folds = ff // width
-    gu[...] = share[:outer_rows, :].astype(F32)
+
+    def share(at, size):
+        total = shares[0, at : at + size, :].astype(F32)
+        for z in range(1, chips):
+            total = total + shares[z, at : at + size, :].astype(F32)
+        return total
+
+    for r in range(0, outer_rows, 16):
+        gu[r : r + 16, :] = share(r, 16)
     for h in range(0, folds, 2):
         at = outer_rows + h * own
         for r in range(0, own, 8):
-            pair = share[at + 2 * r : at + 2 * r + 16, :].astype(F32)
+            pair = share(at + 2 * r, 16)
             gi[r : r + 8, h * width : (h + 1) * width] = pair[:8]
             gi[r : r + 8, (h + 1) * width : (h + 2) * width] = pair[8:]
     at = outer_rows + folds * own
-    go[...] = share[at : at + own + 8, :].astype(F32)[:own]
+    go[...] = share(at, own + 8)[:own]
     total = proj_grads[0, :, :128].astype(F32)[own:]
     for d in range(1, 2 * chips):
         total = total + proj_grads[d, :, :128].astype(F32)[own:]
@@ -953,7 +1173,7 @@
         out[:, cols] = nt_dot(triple[...], wp[pl.ds(at, wide), :]) + resid[:, cols]
 
 
-def final(zeven, zodd, projections, resid, proj_grads, share, own, ff, hd):
+def final(zeven, zodd, projections, resid, proj_grads, shares, own, ff, hd):
     rows, width = resid.shape
     mats = [(rows, width)] + [(own, width)] * 4 + [(own, ff), (ff * own // width, width)]
     vectors = [(own,)] * 5 + [(ff * own // width,)] + [(own,)] * 3
@@ -972,16 +1192,59 @@
         cost_estimate=pl.CostEstimate(
             flops=2 * 10**9, transcendentals=0, bytes_accessed=12 * 10**6
         ),
-    )(zeven, zodd, projections, resid, proj_grads, share)
-
-
-def by_device(value, chips, hd):
-    rows = value.shape[0]
-    wide = chips * 2 * hd
-    even = value[:, :wide].reshape(rows, chips, 2 * hd).transpose(1, 0, 2)
-    odd = value[:, wide:].reshape(rows, chips, hd).transpose(1, 0, 2)
-    odd = jnp.pad(odd, ((0, 0), (0, 0), (0, hd)))
-    return jnp.stack([even, odd], axis=1).reshape(2 * chips, rows, 2 * hd)
+    )(zeven, zodd, projections, resid, proj_grads, shares)
+
+
+def prelude_kernel(
+    hd, q, k, v, o, inner, outer, b0, b1, b2, b3, b4, b5, b6, b7, b8,
+    slabs, first_half, outer_low, projections, tile,
+):
+    own, width = q.shape
+    chips = slabs.shape[0] // 2
+    first_half[:, :width] = o[...].astype(LOW)
+    first_half[:, width:] = inner[...].astype(LOW)
+    outer_low[...] = outer[...].astype(LOW)
+    for t, ref in enumerate((q, k, v)):
+        projections[:, t * width : (t + 1) * width] = ref[...].astype(LOW)
+    tile[...] = jnp.zeros_like(tile)
+    for i, ref in enumerate((b0, b1, b2, b3, b4, b5, b6, b7)):
+        tile[i : i + 1, :own] = ref[...].reshape(1, own)
+    tile[0:1, 128 : 128 + b8.shape[0]] = b8[...].reshape(1, b8.shape[0])
+    keep = lane_of(own) < hd
+    for t, ref in enumerate((q, k, v)):
+        cols = slice(t * 128, (t + 1) * 128)
+        below = tile[:, cols]
+        for d in range(2 * chips):
+            z = d // 2
+            if d % 2 == 0:
+                part = ref[:, z * 128 : (z + 1) * 128]
+            else:
+                at = chips * 128 + z // 2 * 128
+                part = ref[:, at : at + 128]
+                if z % 2:
+                    part = pltpu.roll(part, hd, 1)
+                part = jnp.where(keep, part, 0.0)
+            slabs[d, :16, cols] = part[:16].astype(LOW)
+            slabs[d, 16:, cols] = jnp.concatenate([part[16:], below], axis=0).astype(LOW)
+
+
+def prelude(weights, vectors, blks, hd):
+    own, width = weights[0].shape
+    ff = weights[4].shape[1]
+    return pl.pallas_call(
+        functools.partial(prelude_kernel, hd),
+        name="prelude",
+        out_shape=(
+            jax.ShapeDtypeStruct((blks, own + 8, 384), LOW),
+            jax.ShapeDtypeStruct((own, width + ff), LOW),
+            jax.ShapeDtypeStruct(weights[5].shape, LOW),
+            jax.ShapeDtypeStruct((own, 3 * width), LOW),
+        ),
+        in_specs=[spec(pltpu.VMEM)] * 15,
+        out_specs=(spec(pltpu.VMEM),) * 4,
+        scratch_shapes=[pltpu.VMEM((8, 384), F32)],
+        cost_estimate=pl.CostEstimate(flops=10**6, transcendentals=0, bytes_accessed=3 * 10**6),
+    )(*weights, *vectors)
 
 
 def fast_body(seqs, blks, heads):
@@ -1001,49 +1264,23 @@
         b = lax.axis_index("blk")
         k = b // 2
         even_core = lax.rem(b, 2) == 0
-        query_low, key_low, value_low, output_low, inner_low_w, outer_low_w = [
-            w.astype(LOW)
-            for w in (
-                query_weight, key_weight, value_weight, output_weight, inner_weight, outer_weight,
-            )
-        ]
-        small = jnp.concatenate(
-            [
+        slabs, half_own, outer_own, proj_own = prelude(
+            (query_weight, key_weight, value_weight, output_weight, inner_weight, outer_weight),
+            (
                 query_bias, value_bias, output_bias, attention_gain, attention_shift,
                 outer_bias, final_gain, final_shift, inner_bias,
-            ]
-        ).astype(LOW)
-        slabs = jnp.concatenate(
-            [by_device(w, chips, hd) for w in (query_low, key_low, value_low)], axis=2
-        )
-        extra = jnp.pad(small[None, :], ((0, 7), (0, 384 - small.shape[0])))
-        slabs = jnp.concatenate(
-            [slabs, jnp.broadcast_to(extra[None], (blks,) + extra.shape)], axis=1
-        )
-        axes = ("seq", "blk")
-        first_half = lax.all_gather(
-            jnp.concatenate([output_low, inner_low_w], axis=1), axes, axis=0, tiled=True
-        )
-        outer_full = lax.all_gather(outer_low_w, axes, axis=0, tiled=True)
-        projections = lax.all_gather(
-            jnp.concatenate([query_low, key_low, value_low], axis=1), axes, axis=0, tiled=True
-        )
-        hidden_all, gathered = entry(hidden_in, slabs, seqs, blks, 2)
+            ),
+            blks,
+            hd,
+        )
+        hidden_all, gathered, first_half, outer_full, projections = entry(
+            hidden_in, slabs, (half_own, outer_own, proj_own), seqs, blks, 2
+        )
+        first_half = first_half.reshape(width, width + hidden_units)
+        outer_full = outer_full.reshape(hidden_units, width)
+        projections = projections.reshape(width, 3 * width)
         hidden_all = hidden_all.reshape(length, width)
-        gathered = gathered.reshape(devices, own + 8, 384)
-        weight_own = gathered[:, :own].reshape(width, 384)
-        vec = gathered[:, own, : small.shape[0]]
-        vecs = (
-            vec[:, : 8 * own].reshape(devices, 8, own).transpose(1, 0, 2).reshape(8, width)
-        ).astype(F32)
-        bias_inner = vec[:, 8 * own :].reshape(1, hidden_units).astype(F32)
-        bias_query, bias_value = [
-            by_device(vecs[i : i + 1], chips, hd) for i in (0, 1)
-        ]
-        bias_own = lax.dynamic_index_in_dim(
-            jnp.concatenate([bias_query, jnp.zeros_like(bias_query), bias_value], axis=2),
-            b, 0, keepdims=False,
-        )
+        gathered = gathered.reshape((devices,) + slabs.shape[1:])
         order = cluster_order[0]
         head_first = jnp.where(even_core, 2 * k, 2 * chips + k)
         order_own = jnp.concatenate(
@@ -1052,34 +1289,30 @@
                 lax.dynamic_index_in_dim(order, 2 * k + 1, 0, keepdims=False),
             ]
         )
-        count = jnp.stack(
-            [
-                jnp.where(even_core, 2, 1),
-                jnp.where(even_core, 2 * hd * k, (2 * chips + k) * hd),
-                jnp.where(even_core, 2 * hd, hd),
-            ]
-        ).astype(jnp.int32)
-        proj, cnat, cpack = attend(
-            order_own, count, hidden_all, weight_own, bias_own, blks, hd, scale
+        proj, cnat, cpack, vecs, bias_inner = attend(
+            order_own, hidden_all, gathered, blks, hidden_units, hd, scale
         )
         ceven, codd = return_rows(cnat, cpack, 1)
         hidden_out, residual_grad, geven, godd, merged, extra = middle(
             ceven, codd, hidden_in, first_half, outer_full, vecs, bias_inner, cotangent,
             grad_mask, devices, hd,
         )
-        share = lax.psum_scatter(
-            merged.reshape(-1, width), axes, scatter_dimension=0, tiled=True
-        )
-        gnat, gpack = spread_rows(geven, godd, 2)
+        slab = merged.shape[1:]
+        gnat, gpack, summed = spread_rows(
+            geven, godd, merged.reshape((seqs * chips, 2) + slab), 2
+        )
         znat, zpack, grads = attend_back(
-            order_own, count, hidden_all, proj, gnat, gpack, extra, hd, scale
-        )
-        zeven, zodd, proj_grads = leave(
-            znat, zpack, grads.reshape((seqs, blks) + grads.shape[1:])
+            order_own, hidden_all, proj, gnat, gpack, extra, hd, scale
+        )
+        pieces = 2
+        zeven, zodd, proj_grads, big_grads = leave(
+            znat, zpack, grads.reshape((seqs, blks) + grads.shape[1:]),
+            summed.reshape(seqs, chips, pieces, slab[0] // pieces, width),
         )
         return (hidden_out,) + tuple(
             final(
-                zeven, zodd, projections, residual_grad, proj_grads, share, own, hidden_units, hd
+                zeven, zodd, projections, residual_grad, proj_grads,
+                big_grads.reshape((chips,) + slab), own, hidden_units, hd,
             )
         )
 
@@ -1320,7 +1553,7 @@
     )
     seqs, blks = mesh.shape["seq"], mesh.shape["blk"]
     heads = 12
-    fast = blks % 2 == 0 and 3 * blks == 2 * heads
+    fast = seqs == 4 and blks == 8
     return jax.shard_map(
         fast_body(seqs, blks, heads) if fast else body,
         mesh=mesh,

time: 416 us -> 364 us (0.88); the launches traced: 411 us -> 364 us
  Pallas kernels: 376 us -> 361 us
  between operations: 14.3 us -> 0.89 us
  other arithmetic: 10.2 us -> 0.62 us
  waiting for transfers between devices: 5.58 us -> 0 us
  local copies, waits for them, and re-layouts: 5.35 us -> 0.74 us
    pallas_call x1, Pallas kernels: 47.6 us -> 25.1 us  [attend_back(): pl.pallas_call(functools.partial(attend_back_kernel, hd, scale), name='at...]
    pallas_call x1, Pallas kernels: 82.2 us -> 99.6 us  [entry(): pl.pallas_call(functools.partial(entry_kernel, seqs, blks, parts), name='...]
    pallas_call x1, Pallas kernels: 43.4 us -> 35.1 us  [return_rows(): pl.pallas_call(functools.partial(return_kernel, blks), name='return_rows'...]
    pallas_call x1, Pallas kernels: 30.7 us -> 23.5 us  [attend(): pl.pallas_call(functools.partial(attend_kernel, hd, scale), name='attend'...]
    convert_element_type x8 -> x0, other arithmetic: 6.26 us -> none  [the longest x6 6.18 us: run(): w.astype(LOW)]
    reduce_scatter x1 -> x0, waiting for transfers between devices: 5.46 us -> none  [run(): lax.psum_scatter(merged.reshape(-1, width), axes, scatter_dimension=0, ti...]
  transfers between devices with their start and end apart: 4 -> 0, of which waited for: 1 -> 0; matrix products, arithmetic and copies ran while one was open for 3% -> 0% of each run, Pallas kernels for 89% -> 0%
where the time goes in v3:
time: 364 us
  Pallas kernels  361 us (99%)
    pallas_call x1, Pallas kernels, leave(): pl.pallas_call(functools.partial(exit_kernel, seqs, blks), name='leave',...  102 us
    pallas_call x1, Pallas kernels, entry(): pl.pallas_call(functools.partial(entry_kernel, seqs, blks, parts), name='...  99.6 us
    pallas_call x1, Pallas kernels, middle(): pl.pallas_call(functools.partial(middle_kernel, hd), name='middle', out_s...  42 us
    pallas_call x1, Pallas kernels, return_rows(): pl.pallas_call(functools.partial(return_kernel, blks), name='return_rows'...  35.1 us
    pallas_call x1, Pallas kernels, attend_back(): pl.pallas_call(functools.partial(attend_back_kernel, hd, scale), name='at...  25.1 us
    pallas_call x1, Pallas kernels, attend(): pl.pallas_call(functools.partial(attend_kernel, hd, scale), name='attend'...  23.5 us
    pallas_call x1, Pallas kernels, spread_rows(): pl.pallas_call(functools.partial(spread_kernel, blks), name='spread_rows'...  23 us
    pallas_call x1, Pallas kernels, final(): pl.pallas_call(functools.partial(final_kernel, hd), name='final', out_sha...  8.58 us

profile of v3, /device:TPU:9, one launch (start us, length us, event | category | flops | bytes accessed | tf_op | source)
XLA Modules:
  0.0 363.7 jit_solution(18306208304000128709)
XLA Ops:
  0.7 0.7 constant_dynamic-slice_fusion.1
  1.4 0.6 pad_add_fusion.order
  2.0 2.1 prelude.1
  4.1 99.6 %entry.1 = (bf16[8,2,256,768]{3,2,1,0:T(8,128)(2,1)}, bf16[4,8,32,384]{3,2,1,0:T(8,128)(2,1)}, bf16[4,4,2,24,3840]{4,3,2,1,0:T(8,128)(2,1)}, bf16[4,4,2,96,768]{...) custom-call(bf16[2,256,768]{2,1,0:T(8,128)(2,1)} %bitcast.16, bf16[8,32,384]{2,1,0:T(8,128)(2,1)} %get-tuple-element.65.w_ref, ...), custom_call_target="tpu_custom_call" | custom-call | bytes 200000000 | tf_op jit(solution)/shard_map/entry/pallas_call | solution.py:253
  103.7 23.5 %attend.1 = (bf16[4096,384]{1,0:T(8,128)(2,1)}, bf16[8,512,128]{2,1,0:T(8,128)(2,1)}, bf16[8,256,128]{2,1,0:T(8,128)(2,1)}, f32[8,768]{1,0:T(8,128)}, f32[8,3072]{1,0:T(8,128)}) custom-call(s32[8192]{0:T(1024)} %pad_add_fusion.order, bf16[4096,768]{1,0:T(8,128)(2,1)} %bitcast.20, bf16[32,32,384]{2,1,0:T(8,128)(2,1)} %bitcast.24), custom_call_target="tpu_custom_call" | custom-call | flops 5000000000 | bytes 100000000 | tf_op jit(solution)/shard_map/attend/pallas_call | solution.py:698
  127.2 35.1 %return_rows.1 = (bf16[4,512,128]{2,1,0:T(8,128)(2,1)}, bf16[4,256,128]{2,1,0:T(8,128)(2,1)}) custom-call(bf16[8,512,128]{2,1,0:T(8,128)(2,1)} %get-tuple-element.71.nat_ref, bf16[8,256,128]{2,1,0:T(8,128)(2,1)} %get-tuple-element.72.pack_ref), custom_call_target="tpu_custom_call" | custom-call | bytes 80000000 | tf_op jit(solution)/shard_map/return_rows/pallas_call | solution.py:339
  162.4 42.0 %middle.1 = (bf16[512,768]{1,0:T(8,128)(2,1)}, f32[512,768]{1,0:T(8,128)}, bf16[4,512,128]{2,1,0:T(8,128)(2,1)}, bf16[4,256,128]{2,1,0:T(8,128)(2,1)}, bf16[32,2...) custom-call(bf16[4,512,128]{2,1,0:T(8,128)(2,1)} %get-tuple-element.73.ceven, bf16[4,256,128]{2,1,0:T(8,128)(2,1)} %get-tuple-element.74.codd, ...), custom_call_target="tpu_custom_call" | custom-call | flops 16999999488 | bytes 40000000 | tf_op jit(solution)/shard_map/middle/pallas_call | solution.py:1068
  204.4 23.0 %spread_rows.1 = (bf16[8,512,128]{2,1,0:T(8,128)(2,1)}, bf16[8,256,128]{2,1,0:T(8,128)(2,1)}, bf16[16,224,768]{2,1,0:T(8,128)(2,1)}) custom-call(bf16[4,512,128]{2,1,0:T(8,128)(2,1)} %get-tuple-element.81.even_ref, bf16[4,256,128]{2,1,0:T(8,128)(2,1)} %get-tuple-element.82.odd_ref, bf16[16,2,224,768]{3,2,1,0:T(8,128)(2,1)} %bitcast.12), custom_call_target="tpu_custom_call" | custom-call | bytes 80000000 | tf_op jit(solution)/shard_map/spread_rows/pallas_call | solution.py:436
  227.4 25.1 %attend_back.1 = (bf16[8,512,384]{2,1,0:T(8,128)(2,1)}, bf16[8,256,384]{2,1,0:T(8,128)(2,1)}, bf16[32,32,384]{2,1,0:T(8,128)(2,1)}) custom-call(s32[8192]{0:T(1024)} %pad_add_fusion.order, bf16[4096,768]{1,0:T(8,128)(2,1)} %bitcast.21, bf16[4096,384]{1,0:T(8,128)(2,1)} %get-tuple-element.80.proj, bf16[8,512,128]{2,1,0:T(8,128)(2,1)} %get-tuple-element.84.gnat, ...), custom_call_target="tpu_custom_call" | custom-call | flops 8000000000 | bytes 120000000 | tf_op jit(solution)/shard_map/attend_back/pallas_call | solution.py:846
  252.5 102.4 %leave.1 = (bf16[4,512,384]{2,1,0:T(8,128)(2,1)}, bf16[4,256,384]{2,1,0:T(8,128)(2,1)}, bf16[8,32,384]{2,1,0:T(8,128)(2,1)}, bf16[4,2,112,768]{3,2,1,0:T(8,128)(2,1)}) custom-call(bf16[8,512,384]{2,1,0:T(8,128)(2,1)} %get-tuple-element.87.nat_ref, bf16[8,256,384]{2,1,0:T(8,128)(2,1)} %get-tuple-element.88.pack_ref, bf16[4,8,32,384]{3,2,1,0:T(8,128)(2,1)} %bitcast.17, ...), custom_call_target="tpu_custom_call" | custom-call | bytes 200000000 | tf_op jit(solution)/shard_map/leave/pallas_call | solution.py:552
  354.9 8.6 %final.1 = (f32[512,768]{1,0:T(8,128)}, f32[24,768]{1,0:T(8,128)}, f32[24,768]{1,0:T(8,128)}, f32[24,768]{1,0:T(8,128)}, f32[24,768]{1,0:T(8,128)}, /*index=5*/f...) custom-call(bf16[4,512,384]{2,1,0:T(8,128)(2,1)} %get-tuple-element., ...), custom_call_target="tpu_custom_call" | custom-call | flops 2000000000 | bytes 12000000 | tf_op jit(solution)/shard_map/final/pallas_call | solution.py:1180

commit v4 on v3

--- a/solution.py
+++ b/solution.py
@@ -352,8 +352,8 @@
 
 
 def spread_kernel(
-    blks, even_ref, odd_ref, grad_ref, nat_ref, pack_ref, total,
-    buf, mine, theirs, lsem, ssem, rsem, ml, ms, mr,
+    blks, even_ref, odd_ref, grad_ref, nat_ref, pack_ref, total_hbm,
+    buf, mine, theirs, total, lsem, ssem, rsem, ml, ms, mr, tl,
 ):
     b = lax.axis_index("blk")
     c = lax.rem(b, 2)
@@ -393,6 +393,9 @@
     @pl.loop(0, total.shape[0])
     def _(o):
         total[o] = (mine[o].astype(F32) + theirs[o].astype(F32)).astype(LOW)
+
+    store = pltpu.make_async_copy(total, total_hbm, tl)
+    store.start()
 
     @pl.when(c == 0)
     def _():
@@ -427,6 +430,8 @@
         @pl.when(jnp.logical_not(to_even))
         def _():
             packed(d, b).wait_send()
+
+    store.wait()
 
 
 def spread_rows(even, odd, grads, collective_id):
@@ -442,12 +447,13 @@
             jax.ShapeDtypeStruct(half_shape, LOW),
         ),
         in_specs=[spec(ANY)] * 3,
-        out_specs=(spec(ANY), spec(ANY), spec(pltpu.VMEM)),
+        out_specs=(spec(ANY),) * 3,
         scratch_shapes=[
             pltpu.VMEM(even.shape[1:], LOW),
             pltpu.VMEM(half_shape, LOW),
             pltpu.VMEM(half_shape, LOW),
-            dma, dma((blks,)), dma((blks,)), dma, dma, dma,
+            pltpu.VMEM(half_shape, LOW),
+            dma, dma((blks,)), dma((blks,)), dma, dma, dma, dma,
         ],
         compiler_params=pltpu.CompilerParams(
             collective_id=collective_id, has_side_effects=True, vmem_limit_bytes=BIG
@@ -610,8 +616,8 @@
 
 
 def attend_kernel(
-    hd, scale, order, hid, gathered, proj, nat, pack, vecs, bias_inner,
-    rows4, take, take_b, mix, mix_b, back, wide_weight, weight,
+    hd, scale, order, hid_hbm, gathered, proj_hbm, nat, pack, vecs, bias_inner,
+    rows4, take, take_b, mix, mix_b, back, wide_weight, weight, hid, proj, in_sems, out_sem,
 ):
     length, width = hid.shape
     blks, step, _ = nat.shape
@@ -619,6 +625,13 @@
     own_rows = width // devices
     per = bias_inner.shape[1] // devices
     heads_here, first, _ = owner_facts(hd, blks // 2)
+
+    def fetch(i):
+        part = pl.ds(pl.multiple_of(i * step, step), step)
+        return pltpu.make_async_copy(hid_hbm.at[part], hid.at[part], in_sems.at[i])
+
+    for i in range(length // step):
+        fetch(i).start()
     for i in range(devices):
         slab = gathered[i].astype(F32)
         wide_weight[i * own_rows : (i + 1) * own_rows, :] = slab[:own_rows, :]
@@ -632,12 +645,15 @@
     @pl.loop(0, length // step)
     def _(i):
         at = pl.multiple_of(i * step, step)
+        fetch(i).wait()
         low = (nn_dot(hid[pl.ds(at, step), :], weight[...]) + bias).astype(LOW)
         proj[pl.ds(at, step), :] = low
         wide = low.astype(F32)
         for t in range(3):
             rows4[pl.ds(4 * at + t, step, stride=4), :] = wide[:, t * 128 : (t + 1) * 128]
 
+    store = pltpu.make_async_copy(proj, proj_hbm, out_sem)
+    store.start()
     span = GROUP * 128
 
     def gather(buf, base):
@@ -690,6 +706,8 @@
             at = pl.multiple_of(i * step, step)
             upper = pltpu.roll(back[pl.ds(at + half, half), :], hd, 1)
             pack[i] = jnp.where(lane[:half] < hd, back[pl.ds(at, half), :], upper).astype(LOW)
+
+    store.wait()
 
 
 def attend(order, hid, gathered, blks, ff, hd, scale):
@@ -705,8 +723,8 @@
             jax.ShapeDtypeStruct((8, width), F32),
             jax.ShapeDtypeStruct((8, ff), F32),
         ),
-        in_specs=[spec(pltpu.SMEM)] + [spec(pltpu.VMEM)] * 2,
-        out_specs=(spec(pltpu.VMEM),) * 5,
+        in_specs=[spec(pltpu.SMEM), spec(ANY), spec(pltpu.VMEM)],
+        out_specs=(spec(ANY),) + (spec(pltpu.VMEM),) * 4,
         scratch_shapes=[
             pltpu.VMEM((4 * length, 128), F32),
             pltpu.VMEM((GROUP * 512, 128), F32),
@@ -716,6 +734,10 @@
             pltpu.VMEM((2 * length, 128), F32),
             pltpu.VMEM((width, 384), F32),
             pltpu.VMEM((width, 384), LOW),
+            pltpu.VMEM((length, width), LOW),
+            pltpu.VMEM((length, 384), LOW),
+            pltpu.SemaphoreType.DMA((blks,)),
+            pltpu.SemaphoreType.DMA,
         ],
         compiler_params=pltpu.CompilerParams(vmem_limit_bytes=BIG),
         cost_estimate=pl.CostEstimate(
@@ -725,8 +747,9 @@
 
 
 def attend_back_kernel(
-    hd, scale, order, hidden_hbm, proj, gnat, gpack, extra, znat, zpack, slabs,
-    rows4, take, take_b, out4, out4_b, back4, hid, wide_grad, sem,
+    hd, scale, order, hidden_hbm, proj, gnat, gpack, extra, znat_hbm, zpack_hbm, slabs,
+    rows4, take, take_b, out4, out4_b, back4, hid, wide_grad,
+    znat, zpack, sem, nat_sems, pack_sems,
 ):
     length = proj.shape[0]
     step = gnat.shape[1]
@@ -756,7 +779,7 @@
 
     def gather(buf, base):
         for j in range(span):
-            buf[4 * j : 4 * j + 4, :] = rows4[pl.ds(pl.multiple_of(4 * order[base + j], 4), 4), :]
+            buf[4 * j : 4 * j + 4, :] = rows4[pl.ds(pl.multiple_of(order[base + j], 4), 4), :]
 
     def attend_group(slot, buf, out):
         for u in range(GROUP):
@@ -773,9 +796,10 @@
             out[part_of(u, 2), :] = nn_dot(probs.astype(LOW), grad)
 
     def scatter(slot, out, base):
+        back_slot = back4.at[pl.ds(pl.multiple_of(4 * slot * length, 4 * length), 4 * length), :]
         for j in range(span):
-            at = pl.multiple_of(4 * (slot * length + order[base + j]), 4)
-            back4[pl.ds(at, 4), :] = out[4 * j : 4 * j + 4, :]
+            at = pl.multiple_of(order[base + j], 4)
+            back_slot[pl.ds(at, 4), :] = out[4 * j : 4 * j + 4, :]
 
     @pl.loop(0, heads_here)
     def _(slot):
@@ -796,6 +820,12 @@
     fetch.wait()
     wide_grad[...] = jnp.zeros_like(wide_grad)
     zero = jnp.zeros((1, 384), F32)
+
+    def put_nat(i):
+        return pltpu.make_async_copy(znat.at[i], znat_hbm.at[i], nat_sems.at[i])
+
+    def put_pack(i):
+        return pltpu.make_async_copy(zpack.at[i], zpack_hbm.at[i], pack_sems.at[i])
 
     def settle(i, sums):
         at = pl.multiple_of(i * step, step)
@@ -810,6 +840,8 @@
             wide = low.astype(F32)
             parts.append(jnp.sum(wide, axis=0, keepdims=True))
             zpack[i, :, cols] = (wide[:half] + pltpu.roll(wide[half:], hd, 1)).astype(LOW)
+        put_nat(i).start()
+        put_pack(i).start()
         wide_grad[...] += tn_dot(hid[pl.ds(at, step), :], znat[i])
         return sums + jnp.concatenate(parts, axis=1)
 
@@ -836,9 +868,13 @@
         slabs[i, own - 8 :, :] = jnp.concatenate(
             [wide_grad[at + own - 8 : at + own, :], tail], axis=0
         ).astype(LOW)
+    for i in range(length // step):
+        put_nat(i).wait()
+        put_pack(i).wait()
 
 
 def attend_back(order, hidden_all, proj, gnat, gpack, extra, hd, scale):
+    order = 4 * order
     length = proj.shape[0]
     blks, step, _ = gnat.shape
     devices = extra.shape[0]
@@ -852,7 +888,7 @@
             jax.ShapeDtypeStruct((devices, width // devices + 8, 384), LOW),
         ),
         in_specs=[spec(pltpu.SMEM), spec(ANY)] + [spec(pltpu.VMEM)] * 4,
-        out_specs=(spec(pltpu.VMEM),) * 3,
+        out_specs=(spec(ANY), spec(ANY), spec(pltpu.VMEM)),
         scratch_shapes=[
             pltpu.VMEM((4 * length, 128), F32),
             pltpu.VMEM((GROUP * 512, 128), F32),
@@ -862,7 +898,11 @@
             pltpu.VMEM((8 * length, 128), F32),
             pltpu.VMEM(hidden_all.shape, LOW),
             pltpu.VMEM((width, 384), F32),
+            pltpu.VMEM((blks, step, 384), LOW),
+            pltpu.VMEM((blks, step // 2, 384), LOW),
             pltpu.SemaphoreType.DMA,
+            pltpu.SemaphoreType.DMA((blks,)),
+            pltpu.SemaphoreType.DMA((blks,)),
         ],
         compiler_params=pltpu.CompilerParams(vmem_limit_bytes=BIG),
         cost_estimate=pl.CostEstimate(
@@ -873,8 +913,8 @@
 
 def middle_kernel(
     hd, ceven, codd, hidden, first_hbm, outer_hbm, vecs, bias_inner, cot, mask,
-    hout, resid, geven, godd, merged, extra,
-    wa, wb, ctx, act, slope, ilow, first, flow, olow, unit, acc, hid_low, sums, inner_sums, sems,
+    hout, resid, geven, godd, merged_hbm, extra,
+    wa, wb, ctx, act, slope, ilow, first, flow, olow, unit, acc, hid_low, sums, inner_sums, merged, sems,
 ):
     rows, width = hidden.shape
     ff = outer_hbm.shape[0]
@@ -1027,10 +1067,18 @@
 
     folds = ff // width
     many = block // own_rows
-
-    @pl.loop(0, width // block)
-    def _(m):
-        cols = pl.ds(pl.multiple_of(m * block, block), block)
+    size = merged.shape[1]
+    put_outer = pltpu.make_async_copy(
+        merged.at[:, pl.ds(0, outer_rows)], merged_hbm.at[:, pl.ds(0, outer_rows)], sems.at[3]
+    )
+    put_outer.start()
+
+    def put_rest(m):
+        part = (pl.ds(m * many, many), pl.ds(outer_rows, size - outer_rows))
+        return pltpu.make_async_copy(merged.at[part], merged_hbm.at[part], sems.at[4 + m])
+
+    for m in range(width // block):
+        cols = slice(m * block, (m + 1) * block)
         for h in range(0, folds, 2):
             left = tn_dot(flow[:, cols], ilow[:, h * width : (h + 1) * width])
             right = tn_dot(flow[:, cols], ilow[:, (h + 1) * width : (h + 2) * width])
@@ -1049,6 +1097,7 @@
             merged[m * many + i, at + 16 : at + 32, :] = jnp.concatenate(
                 [part[base + 16 : base + 24, :], jnp.zeros((8, width), F32)], axis=0
             ).astype(LOW)
+        put_rest(m).start()
 
     row8 = lax.broadcasted_iota(jnp.int32, (8, 128), 0)
     for i in range(devices):
@@ -1057,6 +1106,9 @@
         inner = inner_sums[0:1, i * outer_rows : (i + 1) * outer_rows]
         inner = jnp.concatenate([inner, jnp.zeros((1, 128 - outer_rows), F32)], axis=1)
         extra[i] = jnp.where(row8 == 7, jnp.broadcast_to(inner, (8, 128)), piece)
+    put_outer.wait()
+    for m in range(width // block):
+        put_rest(m).wait()
 
 
 def middle(ceven, codd, hidden, first_half, outer_full, vecs, bias_inner, cot, mask, devices, hd):
@@ -1077,7 +1129,7 @@
             jax.ShapeDtypeStruct((devices, 8, 128), F32),
         ),
         in_specs=[spec(pltpu.VMEM)] * 3 + [spec(ANY)] * 2 + [spec(pltpu.VMEM)] * 4,
-        out_specs=(spec(pltpu.VMEM),) * 6,
+        out_specs=(spec(pltpu.VMEM),) * 4 + (spec(ANY), spec(pltpu.VMEM)),
         scratch_shapes=[
             pltpu.VMEM(first_half.shape, LOW),
             pltpu.VMEM(outer_full.shape, LOW),
@@ -1088,7 +1140,8 @@
             wide_f32, wide_low, wide_low, wide_f32, wide_f32, wide_low,
             pltpu.VMEM((8, width), F32),
             pltpu.VMEM((8, ff), F32),
-            pltpu.SemaphoreType.DMA((3,)),
+            pltpu.VMEM((devices, slab, width), LOW),
+            pltpu.SemaphoreType.DMA((4 + width // 384,)),
         ],
         compiler_params=pltpu.CompilerParams(vmem_limit_bytes=BIG),
         cost_estimate=pl.CostEstimate(

time: 364 us -> 354 us (0.973)
  Pallas kernels: 361 us -> 351 us
where the time goes in v4:
time: 354 us
  Pallas kernels  351 us (99%)
    pallas_call x1, Pallas kernels, leave(): pl.pallas_call(functools.partial(exit_kernel, seqs, blks), name='leave',...  101 us
    pallas_call x1, Pallas kernels, entry(): pl.pallas_call(functools.partial(entry_kernel, seqs, blks, parts), name='...  99.6 us
    pallas_call x1, Pallas kernels, middle(): pl.pallas_call(functools.partial(middle_kernel, hd), name='middle', out_s...  40 us
    pallas_call x1, Pallas kernels, return_rows(): pl.pallas_call(functools.partial(return_kernel, blks), name='return_rows'...  35.2 us
    pallas_call x1, Pallas kernels, attend_back(): pl.pallas_call(functools.partial(attend_back_kernel, hd, scale), name='at...  22.7 us
    pallas_call x1, Pallas kernels, attend(): pl.pallas_call(functools.partial(attend_kernel, hd, scale), name='attend'...  21.8 us
    pallas_call x1, Pallas kernels, spread_rows(): pl.pallas_call(functools.partial(spread_kernel, blks), name='spread_rows'...  20.6 us
    pallas_call x1, Pallas kernels, final(): pl.pallas_call(functools.partial(final_kernel, hd), name='final', out_sha...  8.58 us

profile of v4, /device:TPU:9, one launch (start us, length us, event | category | flops | bytes accessed | tf_op | source)
XLA Modules:
  0.0 353.7 jit_solution(12890231902652643885)
XLA Ops:
  0.7 0.7 constant_dynamic-slice_fusion.1
  1.4 0.6 broadcast_multiply_fusion
  2.1 2.1 prelude.1
  4.2 99.6 %entry.1 = (bf16[8,2,256,768]{3,2,1,0:T(8,128)(2,1)}, bf16[4,8,32,384]{3,2,1,0:T(8,128)(2,1)}, bf16[4,4,2,24,3840]{4,3,2,1,0:T(8,128)(2,1)}, bf16[4,4,2,96,768]{...) custom-call(bf16[2,256,768]{2,1,0:T(8,128)(2,1)} %bitcast.16, bf16[8,32,384]{2,1,0:T(8,128)(2,1)} %get-tuple-element.65.w_ref, ...), custom_call_target="tpu_custom_call" | custom-call | bytes 200000000 | tf_op jit(solution)/shard_map/entry/pallas_call | solution.py:253
  103.7 21.8 %attend.1 = (bf16[4096,384]{1,0:T(8,128)(2,1)}, bf16[8,512,128]{2,1,0:T(8,128)(2,1)}, bf16[8,256,128]{2,1,0:T(8,128)(2,1)}, f32[8,768]{1,0:T(8,128)}, f32[8,3072]{1,0:T(8,128)}) custom-call(s32[8192]{0:T(1024)} %get-tuple-element.116.order, bf16[4096,768]{1,0:T(8,128)(2,1)} %bitcast.20, bf16[32,32,384]{2,1,0:T(8,128)(2,1)} %bitcast.24), custom_call_target="tpu_custom_call" | custom-call | flops 5000000000 | bytes 100000000 | tf_op jit(solution)/shard_map/attend/pallas_call | solution.py:716
  125.5 35.2 %return_rows.1 = (bf16[4,512,128]{2,1,0:T(8,128)(2,1)}, bf16[4,256,128]{2,1,0:T(8,128)(2,1)}) custom-call(bf16[8,512,128]{2,1,0:T(8,128)(2,1)} %get-tuple-element.71.nat_ref, bf16[8,256,128]{2,1,0:T(8,128)(2,1)} %get-tuple-element.72.pack_ref), custom_call_target="tpu_custom_call" | custom-call | bytes 80000000 | tf_op jit(solution)/shard_map/return_rows/pallas_call | solution.py:339
  160.7 40.0 %middle.1 = (bf16[512,768]{1,0:T(8,128)(2,1)}, f32[512,768]{1,0:T(8,128)}, bf16[4,512,128]{2,1,0:T(8,128)(2,1)}, bf16[4,256,128]{2,1,0:T(8,128)(2,1)}, bf16[32,2...) custom-call(bf16[4,512,128]{2,1,0:T(8,128)(2,1)} %get-tuple-element.73.ceven, bf16[4,256,128]{2,1,0:T(8,128)(2,1)} %get-tuple-element.74.codd, ...), custom_call_target="tpu_custom_call" | custom-call | flops 16999999488 | bytes 40000000 | tf_op jit(solution)/shard_map/middle/pallas_call | solution.py:1120
  200.7 20.6 %spread_rows.1 = (bf16[8,512,128]{2,1,0:T(8,128)(2,1)}, bf16[8,256,128]{2,1,0:T(8,128)(2,1)}, bf16[16,224,768]{2,1,0:T(8,128)(2,1)}) custom-call(bf16[4,512,128]{2,1,0:T(8,128)(2,1)} %get-tuple-element.81.even_ref, bf16[4,256,128]{2,1,0:T(8,128)(2,1)} %get-tuple-element.82.odd_ref, bf16[16,2,224,768]{3,2,1,0:T(8,128)(2,1)} %bitcast.12), custom_call_target="tpu_custom_call" | custom-call | bytes 80000000 | tf_op jit(solution)/shard_map/spread_rows/pallas_call | solution.py:441
  221.3 22.7 %attend_back.1 = (bf16[8,512,384]{2,1,0:T(8,128)(2,1)}, bf16[8,256,384]{2,1,0:T(8,128)(2,1)}, bf16[32,32,384]{2,1,0:T(8,128)(2,1)}) custom-call(s32[8192]{0:T(1024)} %get-tuple-element.115.order, bf16[4096,768]{1,0:T(8,128)(2,1)} %bitcast.21, bf16[4096,384]{1,0:T(8,128)(2,1)} %get-tuple-element.80.proj, bf16[8,512,128]{2,1,0:T(8,128)(2,1)} %get-tuple-element.84.gnat, ...), custom_call_target="tpu_custom_call" | custom-call | flops 8000000000 | bytes 120000000 | tf_op jit(solution)/shard_map/attend_back/pallas_call | solution.py:882
  244.0 100.9 %leave.1 = (bf16[4,512,384]{2,1,0:T(8,128)(2,1)}, bf16[4,256,384]{2,1,0:T(8,128)(2,1)}, bf16[8,32,384]{2,1,0:T(8,128)(2,1)}, bf16[4,2,112,768]{3,2,1,0:T(8,128)(2,1)}) custom-call(bf16[8,512,384]{2,1,0:T(8,128)(2,1)} %get-tuple-element.87.nat_ref, bf16[8,256,384]{2,1,0:T(8,128)(2,1)} %get-tuple-element.88.pack_ref, bf16[4,8,32,384]{3,2,1,0:T(8,128)(2,1)} %bitcast.17, ...), custom_call_target="tpu_custom_call" | custom-call | bytes 200000000 | tf_op jit(solution)/shard_map/leave/pallas_call | solution.py:558
  345.0 8.6 %final.1 = (f32[512,768]{1,0:T(8,128)}, f32[24,768]{1,0:T(8,128)}, f32[24,768]{1,0:T(8,128)}, f32[24,768]{1,0:T(8,128)}, f32[24,768]{1,0:T(8,128)}, /*index=5*/f...) custom-call(bf16[4,512,384]{2,1,0:T(8,128)(2,1)} %get-tuple-element., ...), custom_call_target="tpu_custom_call" | custom-call | flops 2000000000 | bytes 12000000 | tf_op jit(solution)/shard_map/final/pallas_call | solution.py:1233

commit v5 on v4

--- a/solution.py
+++ b/solution.py
@@ -188,6 +188,11 @@
         beside(a, 3).start()
         pair(a, 1, x_next).start()
 
+    def third(a):
+        beside(a, 2).wait_recv()
+        beside(a, 3).wait_recv()
+        pair(a, 3, across).start()
+
     for t in range(1, half):
         for p in range(parts):
             @pl.when(k - t >= 0)
@@ -212,11 +217,14 @@
 
                 piece(o_ref.at[blk, p], blk, p, mate, 2).start()
 
-        second(t - 1)
-    for a in range(3):
-        beside(a, 2).wait_recv()
-        beside(a, 3).wait_recv()
-        pair(a, 3, across).start()
+        if t == 1:
+            second(0)
+            second(1)
+        if t == 2:
+            second(2)
+            third(0)
+            third(1)
+    third(2)
     for j in range(half):
         blk = 2 * j + 1 - c
         for p in range(parts):

time: 354 us -> 351 us (level)
  no operation moved by 1% of the time
where the time goes in v5:
time: 351 us; the launch traced here: 350 us
  Pallas kernels  348 us (99%)
    pallas_call x1, Pallas kernels, leave(): pl.pallas_call(functools.partial(exit_kernel, seqs, blks), name='leave',...  101 us
    pallas_call x1, Pallas kernels, entry(): pl.pallas_call(functools.partial(entry_kernel, seqs, blks, parts), name='...  99.6 us
    pallas_call x1, Pallas kernels, middle(): pl.pallas_call(functools.partial(middle_kernel, hd), name='middle', out_s...  40 us
    pallas_call x1, Pallas kernels, return_rows(): pl.pallas_call(functools.partial(return_kernel, blks), name='return_rows'...  32.2 us
    pallas_call x1, Pallas kernels, attend_back(): pl.pallas_call(functools.partial(attend_back_kernel, hd, scale), name='at...  22.7 us
    pallas_call x1, Pallas kernels, attend(): pl.pallas_call(functools.partial(attend_kernel, hd, scale), name='attend'...  21.8 us
    pallas_call x1, Pallas kernels, spread_rows(): pl.pallas_call(functools.partial(spread_kernel, blks), name='spread_rows'...  19.9 us
    pallas_call x1, Pallas kernels, final(): pl.pallas_call(functools.partial(final_kernel, hd), name='final', out_sha...  8.58 us

profile of v5, /device:TPU:9, one launch (start us, length us, event | category | flops | bytes accessed | tf_op | source)
XLA Modules:
  0.0 350.2 jit_solution(1194317888699460502)
XLA Ops:
  0.7 0.7 constant_dynamic-slice_fusion.1
  1.4 0.6 broadcast_multiply_fusion
  2.1 2.1 prelude.1
  4.2 99.6 %entry.1 = (bf16[8,2,256,768]{3,2,1,0:T(8,128)(2,1)}, bf16[4,8,32,384]{3,2,1,0:T(8,128)(2,1)}, bf16[4,4,2,24,3840]{4,3,2,1,0:T(8,128)(2,1)}, bf16[4,4,2,96,768]{...) custom-call(bf16[2,256,768]{2,1,0:T(8,128)(2,1)} %bitcast.16, bf16[8,32,384]{2,1,0:T(8,128)(2,1)} %get-tuple-element.65.w_ref, ...), custom_call_target="tpu_custom_call" | custom-call | bytes 200000000 | tf_op jit(solution)/shard_map/entry/pallas_call | solution.py:261
  103.7 21.8 %attend.1 = (bf16[4096,384]{1,0:T(8,128)(2,1)}, bf16[8,512,128]{2,1,0:T(8,128)(2,1)}, bf16[8,256,128]{2,1,0:T(8,128)(2,1)}, f32[8,768]{1,0:T(8,128)}, f32[8,3072]{1,0:T(8,128)}) custom-call(s32[8192]{0:T(1024)} %get-tuple-element.116.order, bf16[4096,768]{1,0:T(8,128)(2,1)} %bitcast.20, bf16[32,32,384]{2,1,0:T(8,128)(2,1)} %bitcast.24), custom_call_target="tpu_custom_call" | custom-call | flops 5000000000 | bytes 100000000 | tf_op jit(solution)/shard_map/attend/pallas_call | solution.py:724
  125.5 32.2 %return_rows.1 = (bf16[4,512,128]{2,1,0:T(8,128)(2,1)}, bf16[4,256,128]{2,1,0:T(8,128)(2,1)}) custom-call(bf16[8,512,128]{2,1,0:T(8,128)(2,1)} %get-tuple-element.71.nat_ref, bf16[8,256,128]{2,1,0:T(8,128)(2,1)} %get-tuple-element.72.pack_ref), custom_call_target="tpu_custom_call" | custom-call | bytes 80000000 | tf_op jit(solution)/shard_map/return_rows/pallas_call | solution.py:347
  157.7 40.0 %middle.1 = (bf16[512,768]{1,0:T(8,128)(2,1)}, f32[512,768]{1,0:T(8,128)}, bf16[4,512,128]{2,1,0:T(8,128)(2,1)}, bf16[4,256,128]{2,1,0:T(8,128)(2,1)}, bf16[32,2...) custom-call(bf16[4,512,128]{2,1,0:T(8,128)(2,1)} %get-tuple-element.73.ceven, bf16[4,256,128]{2,1,0:T(8,128)(2,1)} %get-tuple-element.74.codd, ...), custom_call_target="tpu_custom_call" | custom-call | flops 16999999488 | bytes 40000000 | tf_op jit(solution)/shard_map/middle/pallas_call | solution.py:1128
  197.7 19.9 %spread_rows.1 = (bf16[8,512,128]{2,1,0:T(8,128)(2,1)}, bf16[8,256,128]{2,1,0:T(8,128)(2,1)}, bf16[16,224,768]{2,1,0:T(8,128)(2,1)}) custom-call(bf16[4,512,128]{2,1,0:T(8,128)(2,1)} %get-tuple-element.81.even_ref, bf16[4,256,128]{2,1,0:T(8,128)(2,1)} %get-tuple-element.82.odd_ref, bf16[16,2,224,768]{3,2,1,0:T(8,128)(2,1)} %bitcast.12), custom_call_target="tpu_custom_call" | custom-call | bytes 80000000 | tf_op jit(solution)/shard_map/spread_rows/pallas_call | solution.py:449
  217.6 22.7 %attend_back.1 = (bf16[8,512,384]{2,1,0:T(8,128)(2,1)}, bf16[8,256,384]{2,1,0:T(8,128)(2,1)}, bf16[32,32,384]{2,1,0:T(8,128)(2,1)}) custom-call(s32[8192]{0:T(1024)} %get-tuple-element.115.order, bf16[4096,768]{1,0:T(8,128)(2,1)} %bitcast.21, bf16[4096,384]{1,0:T(8,128)(2,1)} %get-tuple-element.80.proj, bf16[8,512,128]{2,1,0:T(8,128)(2,1)} %get-tuple-element.84.gnat, ...), custom_call_target="tpu_custom_call" | custom-call | flops 8000000000 | bytes 120000000 | tf_op jit(solution)/shard_map/attend_back/pallas_call | solution.py:890
  240.3 101.1 %leave.1 = (bf16[4,512,384]{2,1,0:T(8,128)(2,1)}, bf16[4,256,384]{2,1,0:T(8,128)(2,1)}, bf16[8,32,384]{2,1,0:T(8,128)(2,1)}, bf16[4,2,112,768]{3,2,1,0:T(8,128)(2,1)}) custom-call(bf16[8,512,384]{2,1,0:T(8,128)(2,1)} %get-tuple-element.87.nat_ref, bf16[8,256,384]{2,1,0:T(8,128)(2,1)} %get-tuple-element.88.pack_ref, bf16[4,8,32,384]{3,2,1,0:T(8,128)(2,1)} %bitcast.17, ...), custom_call_target="tpu_custom_call" | custom-call | bytes 200000000 | tf_op jit(solution)/shard_map/leave/pallas_call | solution.py:566
  341.4 8.6 %final.1 = (f32[512,768]{1,0:T(8,128)}, f32[24,768]{1,0:T(8,128)}, f32[24,768]{1,0:T(8,128)}, f32[24,768]{1,0:T(8,128)}, f32[24,768]{1,0:T(8,128)}, /*index=5*/f...) custom-call(bf16[4,512,384]{2,1,0:T(8,128)(2,1)} %get-tuple-element., ...), custom_call_target="tpu_custom_call" | custom-call | flops 2000000000 | bytes 12000000 | tf_op jit(solution)/shard_map/final/pallas_call | solution.py:1241

commit v6 on v5

--- a/solution.py
+++ b/solution.py
@@ -949,8 +949,8 @@
         ctx[:half, at : at + 128] = jnp.where(low_half, here, pltpu.roll(there, hd, 1)).astype(LOW)
         ctx[half:, at : at + 128] = jnp.where(low_half, pltpu.roll(here, hd, 1), there).astype(LOW)
     sums[...] = jnp.zeros_like(sums)
-    wide = 256
-    tile = 64
+    wide = 768
+    tile = 128
 
     def add_rows(row, value):
         sums[row : row + 1, :] += jnp.sum(value, axis=0, keepdims=True)

time: 351 us -> 346 us (0.986)
  Pallas kernels: 348 us -> 343 us
    pallas_call x1, Pallas kernels: 40 us -> 34.6 us  [middle(): pl.pallas_call(functools.partial(middle_kernel, hd), name='middle', out_s...]
where the time goes in v6:
time: 346 us; the launch traced here: 345 us
  Pallas kernels  343 us (99%)
    pallas_call x1, Pallas kernels, leave(): pl.pallas_call(functools.partial(exit_kernel, seqs, blks), name='leave',...  101 us
    pallas_call x1, Pallas kernels, entry(): pl.pallas_call(functools.partial(entry_kernel, seqs, blks, parts), name='...  99.6 us
    pallas_call x1, Pallas kernels, middle(): pl.pallas_call(functools.partial(middle_kernel, hd), name='middle', out_s...  34.6 us
    pallas_call x1, Pallas kernels, return_rows(): pl.pallas_call(functools.partial(return_kernel, blks), name='return_rows'...  32.2 us
    pallas_call x1, Pallas kernels, attend_back(): pl.pallas_call(functools.partial(attend_back_kernel, hd, scale), name='at...  22.9 us
    pallas_call x1, Pallas kernels, attend(): pl.pallas_call(functools.partial(attend_kernel, hd, scale), name='attend'...  21.8 us
    pallas_call x1, Pallas kernels, spread_rows(): pl.pallas_call(functools.partial(spread_kernel, blks), name='spread_rows'...  19.9 us
    pallas_call x1, Pallas kernels, final(): pl.pallas_call(functools.partial(final_kernel, hd), name='final', out_sha...  8.58 us

profile of v6, /device:TPU:9, one launch (start us, length us, event | category | flops | bytes accessed | tf_op | source)
XLA Modules:
  0.0 345.1 jit_solution(16240167603827058402)
XLA Ops:
  0.7 0.7 constant_dynamic-slice_fusion.1
  1.4 0.6 broadcast_multiply_fusion
  2.1 2.1 prelude.1
  4.2 99.6 %entry.1 = (bf16[8,2,256,768]{3,2,1,0:T(8,128)(2,1)}, bf16[4,8,32,384]{3,2,1,0:T(8,128)(2,1)}, bf16[4,4,2,24,3840]{4,3,2,1,0:T(8,128)(2,1)}, bf16[4,4,2,96,768]{...) custom-call(bf16[2,256,768]{2,1,0:T(8,128)(2,1)} %bitcast.16, bf16[8,32,384]{2,1,0:T(8,128)(2,1)} %get-tuple-element.65.w_ref, ...), custom_call_target="tpu_custom_call" | custom-call | bytes 200000000 | tf_op jit(solution)/shard_map/entry/pallas_call | solution.py:261
  103.7 21.8 %attend.1 = (bf16[4096,384]{1,0:T(8,128)(2,1)}, bf16[8,512,128]{2,1,0:T(8,128)(2,1)}, bf16[8,256,128]{2,1,0:T(8,128)(2,1)}, f32[8,768]{1,0:T(8,128)}, f32[8,3072]{1,0:T(8,128)}) custom-call(s32[8192]{0:T(1024)} %get-tuple-element.116.order, bf16[4096,768]{1,0:T(8,128)(2,1)} %bitcast.20, bf16[32,32,384]{2,1,0:T(8,128)(2,1)} %bitcast.24), custom_call_target="tpu_custom_call" | custom-call | flops 5000000000 | bytes 100000000 | tf_op jit(solution)/shard_map/attend/pallas_call | solution.py:724
  125.5 32.2 %return_rows.1 = (bf16[4,512,128]{2,1,0:T(8,128)(2,1)}, bf16[4,256,128]{2,1,0:T(8,128)(2,1)}) custom-call(bf16[8,512,128]{2,1,0:T(8,128)(2,1)} %get-tuple-element.71.nat_ref, bf16[8,256,128]{2,1,0:T(8,128)(2,1)} %get-tuple-element.72.pack_ref), custom_call_target="tpu_custom_call" | custom-call | bytes 80000000 | tf_op jit(solution)/shard_map/return_rows/pallas_call | solution.py:347
  157.7 34.6 %middle.1 = (bf16[512,768]{1,0:T(8,128)(2,1)}, f32[512,768]{1,0:T(8,128)}, bf16[4,512,128]{2,1,0:T(8,128)(2,1)}, bf16[4,256,128]{2,1,0:T(8,128)(2,1)}, bf16[32,2...) custom-call(bf16[4,512,128]{2,1,0:T(8,128)(2,1)} %get-tuple-element.73.ceven, bf16[4,256,128]{2,1,0:T(8,128)(2,1)} %get-tuple-element.74.codd, ...), custom_call_target="tpu_custom_call" | custom-call | flops 16999999488 | bytes 40000000 | tf_op jit(solution)/shard_map/middle/pallas_call | solution.py:1128
  192.4 19.9 %spread_rows.1 = (bf16[8,512,128]{2,1,0:T(8,128)(2,1)}, bf16[8,256,128]{2,1,0:T(8,128)(2,1)}, bf16[16,224,768]{2,1,0:T(8,128)(2,1)}) custom-call(bf16[4,512,128]{2,1,0:T(8,128)(2,1)} %get-tuple-element.81.even_ref, bf16[4,256,128]{2,1,0:T(8,128)(2,1)} %get-tuple-element.82.odd_ref, bf16[16,2,224,768]{3,2,1,0:T(8,128)(2,1)} %bitcast.12), custom_call_target="tpu_custom_call" | custom-call | bytes 80000000 | tf_op jit(solution)/shard_map/spread_rows/pallas_call | solution.py:449
  212.3 22.9 %attend_back.1 = (bf16[8,512,384]{2,1,0:T(8,128)(2,1)}, bf16[8,256,384]{2,1,0:T(8,128)(2,1)}, bf16[32,32,384]{2,1,0:T(8,128)(2,1)}) custom-call(s32[8192]{0:T(1024)} %get-tuple-element.115.order, bf16[4096,768]{1,0:T(8,128)(2,1)} %bitcast.21, bf16[4096,384]{1,0:T(8,128)(2,1)} %get-tuple-element.80.proj, bf16[8,512,128]{2,1,0:T(8,128)(2,1)} %get-tuple-element.84.gnat, ...), custom_call_target="tpu_custom_call" | custom-call | flops 8000000000 | bytes 120000000 | tf_op jit(solution)/shard_map/attend_back/pallas_call | solution.py:890
  235.2 101.1 %leave.1 = (bf16[4,512,384]{2,1,0:T(8,128)(2,1)}, bf16[4,256,384]{2,1,0:T(8,128)(2,1)}, bf16[8,32,384]{2,1,0:T(8,128)(2,1)}, bf16[4,2,112,768]{3,2,1,0:T(8,128)(2,1)}) custom-call(bf16[8,512,384]{2,1,0:T(8,128)(2,1)} %get-tuple-element.87.nat_ref, bf16[8,256,384]{2,1,0:T(8,128)(2,1)} %get-tuple-element.88.pack_ref, bf16[4,8,32,384]{3,2,1,0:T(8,128)(2,1)} %bitcast.17, ...), custom_call_target="tpu_custom_call" | custom-call | bytes 200000000 | tf_op jit(solution)/shard_map/leave/pallas_call | solution.py:566
  336.3 8.6 %final.1 = (f32[512,768]{1,0:T(8,128)}, f32[24,768]{1,0:T(8,128)}, f32[24,768]{1,0:T(8,128)}, f32[24,768]{1,0:T(8,128)}, f32[24,768]{1,0:T(8,128)}, /*index=5*/f...) custom-call(bf16[4,512,384]{2,1,0:T(8,128)(2,1)} %get-tuple-element., ...), custom_call_target="tpu_custom_call" | custom-call | flops 2000000000 | bytes 12000000 | tf_op jit(solution)/shard_map/final/pallas_call | solution.py:1241
